TPU v7x, 32 devices: a whole 2x2x4 slice. The times are simulated.
32 devices in a mesh: seqs: 2 (over x), ctx: 16 (over z, y, core).
Axes of the slice: x: 2, y: 2, z: 4, core: 2. Of those that a mesh axis runs over, the one named last changes fastest.
Arguments:
- queries: bfloat16 [16384, 2048], P(('seqs', 'ctx')), parts along dimension 0, may hold values from -5 to 5
- keys: bfloat16 [16384, 2048], P(('seqs', 'ctx')), parts along dimension 0, may hold values from -5 to 5
- values: bfloat16 [16384, 2048], P(('seqs', 'ctx')), parts along dimension 0, may hold values from -6 to 6
- x_in: bfloat16 [16384, 2048], P(('seqs', 'ctx')), parts along dimension 0, may hold values from -6 to 6
- log_decay: float32 [16384, 32], P(('seqs', 'ctx')), parts along dimension 0, may hold values from -0.7 to 0, as said below
- b_in: bfloat16 [16384, 64], P(('seqs', 'ctx')), parts along dimension 0, may hold values from -0.75 to 0.75
- c_in: bfloat16 [16384, 64], P(('seqs', 'ctx')), parts along dimension 0, may hold values from -0.125 to 0.125
- skip_d: float32 [32], replicated, may hold values from 0.5 to 2
Outputs:
- attended: bfloat16 [16384, 2048], P(('seqs', 'ctx')), parts along dimension 0
- scan_out: bfloat16 [16384, 2048], P(('seqs', 'ctx')), parts along dimension 0
There are 2 independent parts, one for each index of `seqs`. A program takes and returns all parts, laid end to end along the dimension named above; an argument that names none is the same for every part. Nothing has to cross between parts.
Inputs may be any that keep to these rules, and one draw needn't show every extreme that they name: log_decay is negative in every entry.
All inputs are finite; a program needn't handle non-finite values.
Results may differ from a plain program's by a relative error of at most 0.0043.
Values may be sent and summed in bfloat16 or wider, within the bound.
No kernel may reach another device: no remote copies, remote signals or barrier semaphores. Data moves between devices by JAX's collectives and lax.ppermute only.
A program may use at most 384 MiB of HBM per device.

v0:
```python
import jax
import jax.numpy as jnp
from jax import lax
from jax.sharding import PartitionSpec as P

TOK_DEV = 512
WINDOW = 2048
AH = 16
HD = 128
SCAN_HEADS = 32
P_SIZE = 64
N = 64


def passed_along(array, axis, by):
    count = lax.axis_size(axis)
    pairs = [(i, i + by) for i in range(count) if 0 <= i + by < count]
    return lax.ppermute(array, axis, pairs)


def carried_in(array, axis, combine, identity):
    count, index = (lax.axis_size(axis), lax.axis_index(axis))
    everything = jax.tree.map(lambda part: lax.all_gather(part, axis), array)
    start = jax.tree.map(
        lambda part, zero: jnp.broadcast_to(jnp.asarray(zero, part.dtype), part.shape),
        array,
        identity,
    )

    def turn(k, before):
        reached = k < index
        new = combine(before, jax.tree.map(lambda part: part[k], everything))
        return jax.tree.map(lambda a, b: jnp.where(reached, a, b), new, before)

    return lax.fori_loop(0, count, turn, start)


def attend_group(queries, key_rows, value_rows, allowed, heads):
    rows = queries.shape[0]
    query_heads = queries.reshape(rows, heads, HD)
    key_heads = key_rows.reshape(key_rows.shape[0], heads, HD)
    value_heads = value_rows.reshape(value_rows.shape[0], heads, HD)
    scores = jnp.einsum(
        "ihd,jhd->hij", query_heads, key_heads, preferred_element_type=jnp.float32
    ) * HD ** (-0.5)
    scores = jnp.where(allowed[None], scores, -1e30)
    row_max = jnp.max(scores, axis=2, keepdims=True)
    probs = jnp.where(allowed[None], jnp.exp(scores - row_max), 0.0)
    totals = jnp.sum(probs, axis=2)
    weights = probs.astype(jnp.bfloat16)
    summed = jnp.einsum("hij,jhd->ihd", weights, value_heads, preferred_element_type=jnp.float32)
    result = summed / jnp.transpose(totals)[:, :, None]
    return result.astype(jnp.bfloat16).reshape(rows, heads * HD)


def attend_local(queries, key_rows, value_rows, allowed):
    width = 2 * HD
    outputs = []
    for group in range(AH // 2):
        low = group * width
        outputs.append(
            attend_group(
                queries[:, low : low + width],
                key_rows[:, low : low + width],
                value_rows[:, low : low + width],
                allowed,
                2,
            )
        )
    return jnp.concatenate(outputs, axis=1)


def combine_blocks(earlier, following):
    joined_total = earlier[0] + following[0]
    joined_state = jnp.exp(following[0])[:, None, None] * earlier[1] + following[1]
    return (joined_total, joined_state)


def shards(queries, keys, values, x_in, log_decay, b_in, c_in, skip_d):
    device = lax.axis_index("ctx")
    reach_devs = (WINDOW + TOK_DEV - 1) // TOK_DEV
    key_parts = []
    value_parts = []
    current = (keys, values)
    for offset in range(reach_devs):
        current = passed_along((current[0], current[1]), "ctx", 1)
        key_parts.insert(0, current[0])
        value_parts.insert(0, current[1])
    key_rows = jnp.concatenate(key_parts + [keys], axis=0)
    value_rows = jnp.concatenate(value_parts + [values], axis=0)
    query_pos = device * TOK_DEV + jnp.arange(TOK_DEV, dtype=jnp.int32)
    key_pos = (device - reach_devs) * TOK_DEV + jnp.arange(
        (reach_devs + 1) * TOK_DEV, dtype=jnp.int32
    )
    allowed = (
        (key_pos[None, :] <= query_pos[:, None])
        & (key_pos[None, :] > query_pos[:, None] - WINDOW)
        & (key_pos[None, :] >= 0)
    )
    attended = attend_local(queries, key_rows, value_rows, allowed)
    states_in = x_in.reshape(TOK_DEV, SCAN_HEADS, P_SIZE)
    cumulative = jnp.cumsum(log_decay, axis=0)
    block_total = cumulative[-1]
    order_mask = jnp.arange(TOK_DEV)[:, None] >= jnp.arange(TOK_DEV)[None, :]
    gaps = jnp.transpose(cumulative)[:, :, None] - jnp.transpose(cumulative)[:, None, :]
    decay_mat = jnp.where(order_mask[None], jnp.exp(jnp.where(order_mask[None], gaps, 0.0)), 0.0)
    intersections = jnp.dot(c_in, jnp.transpose(b_in), preferred_element_type=jnp.float32)
    mixing = (decay_mat * intersections[None]).astype(jnp.bfloat16)
    within = jnp.einsum("htu,uhp->thp", mixing, states_in, preferred_element_type=jnp.float32)
    states_float = states_in.astype(jnp.float32)
    weighted = (states_float * jnp.exp(block_total[None, :] - cumulative)[:, :, None]).astype(
        jnp.bfloat16
    )
    own_state = jnp.einsum("thp,tn->hpn", weighted, b_in, preferred_element_type=jnp.float32)
    identity = (
        jnp.zeros((SCAN_HEADS,), jnp.float32),
        jnp.zeros((SCAN_HEADS, P_SIZE, N), jnp.float32),
    )
    earlier_total, carried = carried_in((block_total, own_state), "ctx", combine_blocks, identity)
    inter = jnp.exp(cumulative)[:, :, None] * jnp.einsum(
        "tn,hpn->thp", c_in.astype(jnp.float32), carried, precision=lax.Precision.HIGHEST
    )
    result = within + inter + skip_d[None, :, None] * states_float
    scan_out = result.astype(jnp.bfloat16).reshape(TOK_DEV, SCAN_HEADS * P_SIZE)
    return (attended, scan_out)


def solution(mesh):
    in_specs = (
        P(("seqs", "ctx"), None),
        P(("seqs", "ctx"), None),
        P(("seqs", "ctx"), None),
        P(("seqs", "ctx"), None),
        P(("seqs", "ctx"), None),
        P(("seqs", "ctx"), None),
        P(("seqs", "ctx"), None),
        P(),
    )
    out_specs = (P(("seqs", "ctx"), None), P(("seqs", "ctx"), None))
    return jax.shard_map(shards, mesh=mesh, in_specs=in_specs, out_specs=out_specs, check_vma=False)
```

profile of v0, /device:TPU:13, one launch (start us, length us, event | category | flops | bytes accessed | tf_op | source)
XLA Modules:
  0.0 514.5 jit_solution(10265082132633499686)
XLA Ops:
  7.2 3.7 collective-permute-start
  11.0 2.9 copy.150
  13.9 2.1 collective-permute-start.4
  15.9 18.3 %collective-permute-done = bf16[512,2048]{1,0:T(8,128)(2,1)} collective-permute-done((bf16[512,2048]{1,0:T(8,128)(2,1)}, bf16[512,2048]{1,0:T(8,128)(2,1)}, u32[]{:S(2)}, u32[]{:S(2)}) %collective-permute-start) | collective-permute-done | bytes 2097184 | tf_op jit(solution)/shard_map/ppermute | solution.py:18
  34.2 5.3 %collective-permute-start.1 = (bf16[512,2048]{1,0:T(8,128)(2,1)}, bf16[512,2048]{1,0:T(8,128)(2,1)}, u32[]{:S(2)}, u32[]{:S(2)}) collective-permute-start(bf16[512,2048]{1,0:T(8,128)(2,1)} %collective-permute-done), channel_id=1, source_target_pairs={{0,1},{1,2},{2,3},{3,4},{4,5},{5,6},{6,7},{7,8},{8,9},{9,10},{10,1... | collective-permute-start | bytes 6291464 | tf_op jit(solution)/shard_map/ppermute | solution.py:18
  39.5 17.1 %collective-permute-done.4 = bf16[512,2048]{0,1:T(8,128)(2,1)} collective-permute-done((bf16[512,2048]{0,1:T(8,128)(2,1)S(1)}, bf16[512,2048]{0,1:T(8,128)(2,1)}, u32[]{:S(2)}, u32[]{:S(2)}) %collective-permute-start.4) | collective-permute-done | bytes 2097184 | tf_op jit(solution)/shard_map/ppermute | solution.py:18
  56.6 5.4 %collective-permute-start.5 = (bf16[512,2048]{0,1:T(8,128)(2,1)}, bf16[512,2048]{0,1:T(8,128)(2,1)}, u32[]{:S(2)}, u32[]{:S(2)}) collective-permute-start(bf16[512,2048]{0,1:T(8,128)(2,1)} %collective-permute-done.4), channel_id=1, source_target_pairs={{0,1},{1,2},{2,3},{3,4},{4,5},{5,6},{6,7},{7,8},{8,9},{9,10},{10,1... | collective-permute-start | bytes 6291464 | tf_op jit(solution)/shard_map/ppermute | solution.py:18
  62.0 17.2 %collective-permute-done.1 = bf16[512,2048]{1,0:T(8,128)(2,1)} collective-permute-done((bf16[512,2048]{1,0:T(8,128)(2,1)}, bf16[512,2048]{1,0:T(8,128)(2,1)}, u32[]{:S(2)}, u32[]{:S(2)}) %collective-permute-start.1) | collective-permute-done | bytes 2097184 | tf_op jit(solution)/shard_map/ppermute | solution.py:18
  79.2 5.3 %collective-permute-start.2 = (bf16[512,2048]{1,0:T(8,128)(2,1)}, bf16[512,2048]{1,0:T(8,128)(2,1)}, u32[]{:S(2)}, u32[]{:S(2)}) collective-permute-start(bf16[512,2048]{1,0:T(8,128)(2,1)} %collective-permute-done.1), channel_id=1, source_target_pairs={{0,1},{1,2},{2,3},{3,4},{4,5},{5,6},{6,7},{7,8},{8,9},{9,10},{10,1... | collective-permute-start | bytes 6291464 | tf_op jit(solution)/shard_map/ppermute | solution.py:18
  86.8 14.9 %collective-permute-done.5 = bf16[512,2048]{0,1:T(8,128)(2,1)} collective-permute-done((bf16[512,2048]{0,1:T(8,128)(2,1)}, bf16[512,2048]{0,1:T(8,128)(2,1)}, u32[]{:S(2)}, u32[]{:S(2)}) %collective-permute-start.5) | collective-permute-done | bytes 2097184 | tf_op jit(solution)/shard_map/ppermute | solution.py:18
  101.6 5.3 %collective-permute-start.6 = (bf16[512,2048]{0,1:T(8,128)(2,1)}, bf16[512,2048]{0,1:T(8,128)(2,1)}, u32[]{:S(2)}, u32[]{:S(2)}) collective-permute-start(bf16[512,2048]{0,1:T(8,128)(2,1)} %collective-permute-done.5), channel_id=1, source_target_pairs={{0,1},{1,2},{2,3},{3,4},{4,5},{5,6},{6,7},{7,8},{8,9},{9,10},{10,1... | collective-permute-start | bytes 6291464 | tf_op jit(solution)/shard_map/ppermute | solution.py:18
  106.9 17.2 %collective-permute-done.2 = bf16[512,2048]{1,0:T(8,128)(2,1)} collective-permute-done((bf16[512,2048]{1,0:T(8,128)(2,1)}, bf16[512,2048]{1,0:T(8,128)(2,1)}, u32[]{:S(2)}, u32[]{:S(2)}) %collective-permute-start.2) | collective-permute-done | bytes 2097184 | tf_op jit(solution)/shard_map/ppermute | solution.py:18
  124.1 5.3 %collective-permute-start.3 = (bf16[512,2048]{1,0:T(8,128)(2,1)}, bf16[512,2048]{1,0:T(8,128)(2,1)}, u32[]{:S(2)}, u32[]{:S(2)}) collective-permute-start(bf16[512,2048]{1,0:T(8,128)(2,1)} %collective-permute-done.2), channel_id=1, source_target_pairs={{0,1},{1,2},{2,3},{3,4},{4,5},{5,6},{6,7},{7,8},{8,9},{9,10},{10,1... | collective-permute-start | bytes 6291464 | tf_op jit(solution)/shard_map/ppermute | solution.py:18
  130.1 2.9 copy.201
  134.7 2.8 fusion.177
  137.5 1.8 copy.227
  139.3 1.8 copy.228
  141.1 1.8 copy.229
  142.9 1.8 copy.230
  144.7 1.8 copy.231
  146.5 1.8 copy.232
  151.0 72.0 %all-gather.1 = f32[16,1,32]{2,1,0:T(1,128)S(1)} all-gather(f32[1,1,32]{2,1,0:T(1,128)S(1)} %bitcast.268), channel_id=1, replica_groups=mesh['seqs'=2,'ctx'=16] {'ctx'}, dimensions={0}, use_global_device_ids=true | all-gather | bytes 2176 | tf_op jit(solution)/shard_map/all_gather | solution.py:23
  225.1 2.9 and_and_fusion
  228.0 5.7 %collective-permute-start.7 = (bf16[512,2048]{0,1:T(8,128)(2,1)}, bf16[512,2048]{0,1:T(8,128)(2,1)}, u32[]{:S(2)}, u32[]{:S(2)}) collective-permute-start(bf16[512,2048]{0,1:T(8,128)(2,1)} %collective-permute-done.6), channel_id=1, source_target_pairs={{0,1},{1,2},{2,3},{3,4},{4,5},{5,6},{6,7},{7,8},{8,9},{9,10},{10,1... | collective-permute-start | bytes 6291464 | tf_op jit(solution)/shard_map/ppermute | solution.py:18
  237.2 1.9 constant_dynamic-update-slice_fusion.2
  239.1 1.9 constant_dynamic-update-slice_fusion.1
  241.5 4.1 fusion.176
  245.6 2.4 copy.149
  248.0 44.8 %collective-permute-done.7 = bf16[512,2048]{0,1:T(8,128)(2,1)} collective-permute-done((bf16[512,2048]{0,1:T(8,128)(2,1)}, bf16[512,2048]{0,1:T(8,128)(2,1)}, u32[]{:S(2)}, u32[]{:S(2)}) %collective-permute-start.7) | collective-permute-done | bytes 2097184 | tf_op jit(solution)/shard_map/ppermute | solution.py:18
  298.0 1.9 constant_dynamic-update-slice_fusion.6
  300.4 4.0 fusion.175
  304.4 10.3 %fusion.178 = (f32[2,512]{1,0:T(2,128)S(1)}, bf16[2,512,2560]{1,2,0:T(8,128)(2,1)}) fusion(pred[512,2560]{0,1:T(8,128)(4,1)} %and_and_fusion, bf16[2560,2,128]{0,2,1:T(8,128)(2,1)} %bitcast.242, bf16[512,2,128]{0,2,1:T(8,128)(2,1)S(1)} %bitcast.258), kind=kOutput, calls=%fused_computation.174 | convolution fusion | flops 686819840 | bytes 8130560 | tf_op jit(solution)/shard_map/sub | solution.py:48
  314.7 4.5 fusion.130
  320.2 2.6 copy.156
  322.9 10.4 %fusion.179 = (f32[2,512]{1,0:T(2,128)S(1)}, bf16[2,512,2560]{1,2,0:T(8,128)(2,1)}) fusion(pred[512,2560]{0,1:T(8,128)(4,1)} %and_and_fusion, bf16[2560,2,128]{0,2,1:T(8,128)(2,1)} %bitcast.241, bf16[512,2,128]{0,2,1:T(8,128)(2,1)} %bitcast.257), kind=kOutput, calls=%fused_computation.175 | convolution fusion | flops 686819840 | bytes 8130560 | tf_op jit(solution)/shard_map/sub | solution.py:48
  333.3 4.5 fusion.133
  337.8 1.8 copy.192
  339.6 2.7 copy.161
  342.3 10.4 %fusion.180 = (f32[2,512]{1,0:T(2,128)S(1)}, bf16[2,512,2560]{1,2,0:T(8,128)(2,1)}) fusion(pred[512,2560]{0,1:T(8,128)(4,1)} %and_and_fusion, bf16[2560,2,128]{0,2,1:T(8,128)(2,1)} %bitcast.240, bf16[512,2,128]{0,2,1:T(8,128)(2,1)} %bitcast.256), kind=kOutput, calls=%fused_computation.176 | convolution fusion | flops 686819840 | bytes 8130560 | tf_op jit(solution)/shard_map/sub | solution.py:48
  352.7 4.5 fusion.136
  357.1 1.8 copy.193
  358.9 2.9 copy.166
  361.9 10.4 %fusion.181 = (f32[2,512]{1,0:T(2,128)S(1)}, bf16[2,512,2560]{1,2,0:T(8,128)(2,1)}) fusion(pred[512,2560]{0,1:T(8,128)(4,1)} %and_and_fusion, bf16[2560,2,128]{0,2,1:T(8,128)(2,1)} %bitcast.239, bf16[512,2,128]{0,2,1:T(8,128)(2,1)} %bitcast.255), kind=kOutput, calls=%fused_computation.177 | convolution fusion | flops 686819840 | bytes 8130560 | tf_op jit(solution)/shard_map/sub | solution.py:48
  372.3 4.5 fusion.139
  378.5 2.6 copy.171
  381.1 10.4 %fusion.182 = (f32[2,512]{1,0:T(2,128)S(1)}, bf16[2,512,2560]{1,2,0:T(8,128)(2,1)}) fusion(pred[512,2560]{0,1:T(8,128)(4,1)} %and_and_fusion, bf16[2560,2,128]{0,2,1:T(8,128)(2,1)} %bitcast.238, bf16[512,2,128]{0,2,1:T(8,128)(2,1)} %bitcast.254), kind=kOutput, calls=%fused_computation.178 | convolution fusion | flops 686819840 | bytes 8130560 | tf_op jit(solution)/shard_map/sub | solution.py:48
  391.5 4.4 fusion.142
  396.0 1.8 copy.195
  397.8 2.6 copy.176
  400.4 10.4 %fusion.183 = (f32[2,512]{1,0:T(2,128)S(1)}, bf16[2,512,2560]{1,2,0:T(8,128)(2,1)}) fusion(pred[512,2560]{0,1:T(8,128)(4,1)} %and_and_fusion, bf16[2560,2,128]{0,2,1:T(8,128)(2,1)} %bitcast.237, bf16[512,2,128]{0,2,1:T(8,128)(2,1)} %bitcast.253), kind=kOutput, calls=%fused_computation.179 | convolution fusion | flops 686819840 | bytes 8130560 | tf_op jit(solution)/shard_map/sub | solution.py:48
  410.8 4.4 fusion.145
  415.2 1.8 copy.196
  417.0 2.7 copy.181
  419.7 10.4 %fusion.184 = (f32[2,512]{1,0:T(2,128)S(1)}, bf16[2,512,2560]{1,2,0:T(8,128)(2,1)}) fusion(pred[512,2560]{0,1:T(8,128)(4,1)} %and_and_fusion, bf16[2560,2,128]{0,2,1:T(8,128)(2,1)} %bitcast.236, bf16[512,2,128]{0,2,1:T(8,128)(2,1)} %bitcast.252), kind=kOutput, calls=%fused_computation.180 | convolution fusion | flops 686819840 | bytes 8130560 | tf_op jit(solution)/shard_map/sub | solution.py:48
  430.1 4.5 fusion.148
  434.6 1.8 copy.197
  436.4 2.7 copy.186
  439.1 10.4 %fusion.185 = (f32[2,512]{1,0:T(2,128)S(1)}, bf16[2,512,2560]{1,2,0:T(8,128)(2,1)}) fusion(pred[512,2560]{0,1:T(8,128)(4,1)} %and_and_fusion, bf16[2560,2,128]{0,2,1:T(8,128)(2,1)} %bitcast.235, bf16[512,2,128]{0,2,1:T(8,128)(2,1)} %bitcast.251), kind=kOutput, calls=%fused_computation.181 | convolution fusion | flops 686819840 | bytes 8130560 | tf_op jit(solution)/shard_map/sub | solution.py:48
  449.5 4.4 fusion.151
  454.0 1.8 copy.198
  465.3 24.1 %while.14 = (s32[]{:T(128)}, f32[32,64,64]{2,1,0:T(8,128)S(1)}, s32[]{:T(128)}, f32[16,32]{1,0:T(8,128)S(1)}, f32[16,32,64,64]{3,2,1,0:T(8,128)}, /*index=5*/s32[]{:T(128)}, s32[]{:T(128)}) while((s32[]{:T(128)}, f32[32,64,64]{2,1,0:T(8,128)S(1)}, s32[]{:T(128)}, f32[16,32]{1,0:T(8,128)S(1)}, f32[16,32,64,64]{3,2,1,0:T(8,128)}, ...), condition=%wide.region_19.20_spmd.clone, body=%wide.region_18.19_spmd.clone.sunk | while | flops 524292 | bytes 1573361 | solution.py:35
  489.5 1.9 fusion.154
  491.4 11.9 %fusion.61 = bf16[512,32,64]{0,2,1:T(8,128)(2,1)} fusion(bf16[512,32,64]{0,2,1:T(8,128)(2,1)S(1)} %bitcast.232, f32[32,64,512]{2,1,0:T(8,128)S(1)} %fusion.154, f32[512,512]{1,0:T(8,128)S(1)} %copy-done.4, f32[32,512]{1,0:T(8,128)S(1)} %copy-done.11, pred[512,512]{1,0:T(8,128)(4,1)S(1)} %copy-done.9, f32[32]{0:T(128)S(1)} %copy-done.14, ...), kind=kOutput, calls=%fused_computation.83 | convolution fusion | flops 1121976320 | bytes 9830528 | tf_op jit(solution)/shard_map/htu,uhp->thp/dot_general | solution.py:109
  503.3 3.9 copy.202
  (101 shorter events, 55.2 us)
Async XLA Ops:
  7.2 216.6 %copy-start = (bf16[512,64]{0,1:T(8,128)(2,1)S(1)}, bf16[512,64]{0,1:T(8,128)(2,1)}, u32[]{:S(2)}) copy-start(bf16[512,64]{0,1:T(8,128)(2,1)} %param.16) | copy-start | bytes 196612
  7.2 77.3 %copy-start.13 = (f32[512,32]{0,1:T(8,128)S(1)}, f32[512,32]{0,1:T(8,128)}, u32[]{:S(2)}) copy-start(f32[512,32]{0,1:T(8,128)} %param.14) | copy-start | bytes 196612
  7.2 458.1 %all-gather.4.cloned.1.call-start = ((), (), s32[]{:S(2)}) async-start(), calls=%async_computation | async-start | bytes 17825792 | tf_op jit(solution)/shard_map/all_gather | solution.py:23
  7.2 27.0 %collective-permute-start = (bf16[512,2048]{1,0:T(8,128)(2,1)}, bf16[512,2048]{1,0:T(8,128)(2,1)}, u32[]{:S(2)}, u32[]{:S(2)}) collective-permute-start(bf16[512,2048]{1,0:T(8,128)(2,1)} %param.12), channel_id=1, source_target_pairs={{0,1},{1,2},{2,3},{3,4},{4,5},{5,6},{6,7},{7,8},{8,9},{9,10},{10,1... | collective-permute-start | bytes 6291464 | tf_op jit(solution)/shard_map/ppermute | solution.py:18
  13.8 115.6 %copy-start.1 = (bf16[512,2048]{0,1:T(8,128)(2,1)}, bf16[512,2048]{0,1:T(8,128)(2,1)S(1)}, u32[]{:S(2)}) copy-start(bf16[512,2048]{0,1:T(8,128)(2,1)S(1)} %copy.150) | copy-start | bytes 6291460
  13.8 119.1 %copy-start.8 = (bf16[512,64]{0,1:T(8,128)(2,1)S(1)}, bf16[512,64]{0,1:T(8,128)(2,1)}, u32[]{:S(2)}) copy-start(bf16[512,64]{0,1:T(8,128)(2,1)} %param.15) | copy-start | bytes 196612
  13.9 42.7 %collective-permute-start.4 = (bf16[512,2048]{0,1:T(8,128)(2,1)S(1)}, bf16[512,2048]{0,1:T(8,128)(2,1)}, u32[]{:S(2)}, u32[]{:S(2)}) collective-permute-start(bf16[512,2048]{0,1:T(8,128)(2,1)S(1)} %copy.150), channel_id=1, source_target_pairs={{0,1},{1,2},{2,3},{3,4},{4,5},{5,6},{6,7},{7,8},{8,9},{9,10},{10,1... | collective-permute-start | bytes 6291464 | tf_op jit(solution)/shard_map/ppermute | solution.py:18
  34.2 44.9 %collective-permute-start.1 = (bf16[512,2048]{1,0:T(8,128)(2,1)}, bf16[512,2048]{1,0:T(8,128)(2,1)}, u32[]{:S(2)}, u32[]{:S(2)}) collective-permute-start(bf16[512,2048]{1,0:T(8,128)(2,1)} %collective-permute-done), channel_id=1, source_target_pairs={{0,1},{1,2},{2,3},{3,4},{4,5},{5,6},{6,7},{7,8},{8,9},{9,10},{10,1... | collective-permute-start | bytes 6291464 | tf_op jit(solution)/shard_map/ppermute | solution.py:18
  56.6 45.0 %collective-permute-start.5 = (bf16[512,2048]{0,1:T(8,128)(2,1)}, bf16[512,2048]{0,1:T(8,128)(2,1)}, u32[]{:S(2)}, u32[]{:S(2)}) collective-permute-start(bf16[512,2048]{0,1:T(8,128)(2,1)} %collective-permute-done.4), channel_id=1, source_target_pairs={{0,1},{1,2},{2,3},{3,4},{4,5},{5,6},{6,7},{7,8},{8,9},{9,10},{10,1... | collective-permute-start | bytes 6291464 | tf_op jit(solution)/shard_map/ppermute | solution.py:18
  79.2 44.9 %collective-permute-start.2 = (bf16[512,2048]{1,0:T(8,128)(2,1)}, bf16[512,2048]{1,0:T(8,128)(2,1)}, u32[]{:S(2)}, u32[]{:S(2)}) collective-permute-start(bf16[512,2048]{1,0:T(8,128)(2,1)} %collective-permute-done.1), channel_id=1, source_target_pairs={{0,1},{1,2},{2,3},{3,4},{4,5},{5,6},{6,7},{7,8},{8,9},{9,10},{10,1... | collective-permute-start | bytes 6291464 | tf_op jit(solution)/shard_map/ppermute | solution.py:18
  101.6 126.3 %collective-permute-start.6 = (bf16[512,2048]{0,1:T(8,128)(2,1)}, bf16[512,2048]{0,1:T(8,128)(2,1)}, u32[]{:S(2)}, u32[]{:S(2)}) collective-permute-start(bf16[512,2048]{0,1:T(8,128)(2,1)} %collective-permute-done.5), channel_id=1, source_target_pairs={{0,1},{1,2},{2,3},{3,4},{4,5},{5,6},{6,7},{7,8},{8,9},{9,10},{10,1... | collective-permute-start | bytes 6291464 | tf_op jit(solution)/shard_map/ppermute | solution.py:18
  124.1 109.6 %collective-permute-start.3 = (bf16[512,2048]{1,0:T(8,128)(2,1)}, bf16[512,2048]{1,0:T(8,128)(2,1)}, u32[]{:S(2)}, u32[]{:S(2)}) collective-permute-start(bf16[512,2048]{1,0:T(8,128)(2,1)} %collective-permute-done.2), channel_id=1, source_target_pairs={{0,1},{1,2},{2,3},{3,4},{4,5},{5,6},{6,7},{7,8},{8,9},{9,10},{10,1... | collective-permute-start | bytes 6291464 | tf_op jit(solution)/shard_map/ppermute | solution.py:18
  228.0 64.8 %collective-permute-start.7 = (bf16[512,2048]{0,1:T(8,128)(2,1)}, bf16[512,2048]{0,1:T(8,128)(2,1)}, u32[]{:S(2)}, u32[]{:S(2)}) collective-permute-start(bf16[512,2048]{0,1:T(8,128)(2,1)} %collective-permute-done.6), channel_id=1, source_target_pairs={{0,1},{1,2},{2,3},{3,4},{4,5},{5,6},{6,7},{7,8},{8,9},{9,10},{10,1... | collective-permute-start | bytes 6291464 | tf_op jit(solution)/shard_map/ppermute | solution.py:18
  239.1 2.2 copy-start.3
  298.0 2.2 copy-start.2
  300.4 4.0 copy-start.10
  455.7 7.4 %copy-start.5 = (bf16[512,256]{1,0:T(8,128)(2,1)S(1)}, bf16[512,256]{1,0:T(8,128)(2,1)}, u32[]{:S(2)}) copy-start(bf16[512,256]{1,0:T(8,128)(2,1)} %copy.196) | copy-start | bytes 786436
  455.7 8.1 %copy-start.6 = (bf16[512,256]{1,0:T(8,128)(2,1)S(1)}, bf16[512,256]{1,0:T(8,128)(2,1)}, u32[]{:S(2)}) copy-start(bf16[512,256]{1,0:T(8,128)(2,1)} %copy.197) | copy-start | bytes 786436
  455.7 8.8 %copy-start.7 = (bf16[512,256]{1,0:T(8,128)(2,1)S(1)}, bf16[512,256]{1,0:T(8,128)(2,1)}, u32[]{:S(2)}) copy-start(bf16[512,256]{1,0:T(8,128)(2,1)} %copy.198) | copy-start | bytes 786436
  489.4 1.9 copy-start.4
  489.4 1.9 copy-start.9
  489.4 1.9 copy-start.11
  489.4 1.9 copy-start.12
  489.5 1.9 copy-start.14
Sparse Core Ops, SparseCore 0:
  134.8 158.7 all-gather.3
where the time goes:
time: 522 us; the launch traced here: 515 us
  matrix products  135 us (26%)
  waiting for transfers between devices  130 us (25%)
  local copies, waits for them, and re-layouts  94.3 us (18%)
  blocking collectives  72 us (14%)
  starting transfers between devices  38 us (7%)
  other arithmetic  29.7 us (6%)
  between operations  15 us (3%)
    ppermute x8, waiting for transfers between devices, passed_along(): return lax.ppermute(array, axis, pairs)  129 us
    sub x8, matrix products, attend_group(): probs = jnp.where(allowed[None], jnp.exp(scores - row_max), 0.0)  83.1 us
    all_gather x1, blocking collectives, carried_in(): everything = jax.tree.map(lambda part: lax.all_gather(part, axis), array)  72 us
    unnamed x56, local copies, waits for them, and re-layouts  46.9 us
    ppermute x8, starting transfers between devices, passed_along(): return lax.ppermute(array, axis, pairs)  38 us
    dot_general x8, matrix products, attend_group(): jnp.einsum('hij,jhd->ihd', weights, value_heads, preferred_element_type=j...  35.6 us
    slice x9, local copies, waits for them, and re-layouts, attend_local(): value_rows[:, low:low + width]  25.4 us
    select_n x16, other arithmetic, turn(): return jax.tree.map(lambda a, b: jnp.where(reached, a, b), new, before)  23.4 us
  transfers between devices with their start and end apart: 9, of which 6 were waited for; matrix products, arithmetic and copies ran while one was open for 42% of the time, Pallas kernels for 0%

commit v1 on v0

v1 whole, which is shorter than its diff:
```python
import functools

import jax
import jax.numpy as jnp
from jax import lax
from jax.experimental import pallas as pl
from jax.experimental.pallas import tpu as pltpu
from jax.sharding import PartitionSpec as P

TOK_DEV = 512
WINDOW = 2048
AH = 16
HD = 128
SCAN_HEADS = 32
P_SIZE = 64
N = 64
GROUP = WINDOW // TOK_DEV
SUB = 128
CHUNKS = (2, 2, 2, 2, 2, 2, 2, 2)
NEG = -1e30
EXP_SCALE = HD ** (-0.5) * 1.4426950408889634
F32 = jnp.float32
BF16 = jnp.bfloat16


def cyclic(array, by):
    count = lax.axis_size("ctx")
    return lax.ppermute(array, "ctx", [(i, (i + by) % count) for i in range(count)])


def swapped(array, bit):
    count = lax.axis_size("ctx")
    return lax.ppermute(array, "ctx", [(i, i ^ bit) for i in range(count)])


def dot_t(a, b):
    return lax.dot_general(a, b, (((1,), (1,)), ((), ())), preferred_element_type=F32)


def dot_f32(a, b):
    return jnp.dot(a, b, preferred_element_type=F32)


def attend_kernel(flags, q, k, v, z, d, e, g, xk, xv, out, keys, vals):
    odd = flags[0]
    later = flags[1]
    full = flags[2]

    @pl.when(pl.program_id(0) == 0)
    def _():
        vals[:, :, HD:] = jnp.ones((5, TOK_DEV, HD), BF16)

    keys[0] = k[...]
    vals[0, :, :HD] = v[...]
    keys[1] = z[0]
    vals[1, :, :HD] = z[1]
    keys[2] = d[0]
    vals[2, :, :HD] = d[1]

    @pl.when(odd == 1)
    def _():
        keys[3] = xk[...]
        vals[3, :, :HD] = xv[...]

    @pl.when(odd == 0)
    def _():
        keys[3] = e[0]
        vals[3, :, :HD] = e[1]

    keys[4] = g[0]
    vals[4, :, :HD] = g[1]

    def tile(first, rows, masked):
        qt = q[first : first + rows, :]
        row = lax.broadcasted_iota(jnp.int32, (rows, TOK_DEV), 0) + first
        col = lax.broadcasted_iota(jnp.int32, (rows, TOK_DEV), 1)
        causal = col <= row
        own = dot_t(qt, keys[0])
        prev = dot_t(qt, keys[1])
        s2 = dot_t(qt, keys[2])
        s3 = dot_t(qt, keys[3])
        s4 = dot_t(qt, keys[4])
        if masked:
            prev = jnp.full_like(prev, NEG)
            bias_d = jnp.where(later == 1, 0.0, NEG)
            bias_e = jnp.where(odd == 1, 0.0, NEG)
            s2 = s2 + bias_d
            s3 = s3 + bias_e
            s4 = s4 + bias_d
        s0 = jnp.where(causal, own, prev)
        top = jnp.maximum(jnp.maximum(s0, s2), jnp.maximum(s3, s4))
        top = jnp.max(top, axis=1, keepdims=True) * EXP_SCALE
        p0 = jnp.exp2(s0 * EXP_SCALE - top)
        p2 = jnp.exp2(s2 * EXP_SCALE - top).astype(BF16)
        p3 = jnp.exp2(s3 * EXP_SCALE - top).astype(BF16)
        p4 = jnp.exp2(s4 * EXP_SCALE - top).astype(BF16)
        po = jnp.where(causal, p0, 0.0).astype(BF16)
        pp = jnp.where(causal, 0.0, p0).astype(BF16)
        acc = dot_f32(po, vals[0]) + dot_f32(pp, vals[1])
        acc = acc + dot_f32(p2, vals[2]) + dot_f32(p3, vals[3]) + dot_f32(p4, vals[4])
        out[first : first + rows, :] = (acc[:, :HD] / acc[:, HD:]).astype(BF16)

    @pl.when(full == 1)
    def _():
        for first in range(0, TOK_DEV, 128):
            tile(first, 128, False)

    @pl.when(full == 0)
    def _():
        for first in range(0, TOK_DEV, 128):
            tile(first, 128, True)


def attend(flags, low, heads, queries, keys, values, z, d, e, g, xk, xv):
    wide = pl.BlockSpec((TOK_DEV, HD), lambda j, f: (0, low + j))
    pair = pl.BlockSpec((2, TOK_DEV, HD), lambda j, f: (0, 0, j))
    return pl.pallas_call(
        attend_kernel,
        name="attend",
        out_shape=jax.ShapeDtypeStruct((TOK_DEV, heads * HD), BF16),
        grid_spec=pltpu.PrefetchScalarGridSpec(
            num_scalar_prefetch=1,
            grid=(heads,),
            in_specs=[wide, wide, wide, pair, pair, pair, pair, wide, wide],
            out_specs=pl.BlockSpec((TOK_DEV, HD), lambda j, f: (0, j)),
            scratch_shapes=[
                pltpu.VMEM((5, TOK_DEV, HD), BF16),
                pltpu.VMEM((5, TOK_DEV, 2 * HD), BF16),
            ],
        ),
        compiler_params=pltpu.CompilerParams(vmem_limit_bytes=32 << 20),
    )(flags, queries, keys, values, z, d, e, g, xk, xv)


def split3(a):
    hi = a.astype(BF16)
    rest = a - hi.astype(F32)
    mid = rest.astype(BF16)
    low = (rest - mid.astype(F32)).astype(BF16)
    return hi, mid, low


def split2(a):
    hi = a.astype(BF16)
    return hi, (a - hi.astype(F32)).astype(BF16)


def pick(head, width):
    row = lax.broadcasted_iota(jnp.int32, (3 * SCAN_HEADS, width), 0) % SCAN_HEADS
    return (row == head).astype(BF16)


def local_kernel(x, decay, decay_t, b, c, skip, part, state, cum_out, cums, cum_t, cross):
    step = pl.program_id(0)

    @pl.when(step == 0)
    def _():
        t = lax.broadcasted_iota(jnp.int32, (TOK_DEV, TOK_DEV), 0)
        u = lax.broadcasted_iota(jnp.int32, (TOK_DEV, TOK_DEV), 1)
        lower = (t >= u).astype(BF16)
        upper = (t <= u).astype(BF16)
        hi, mid, low = split3(decay[...])
        total = dot_f32(lower, hi) + dot_f32(lower, mid) + dot_f32(lower, low)
        cum_out[...] = total
        hi, mid, low = split3(total)
        cums[:, 0:32] = hi
        cums[:, 32:64] = mid
        cums[:, 64:96] = low
        hi, mid, low = split3(decay_t[...])
        cum_t[...] = dot_f32(hi, upper) + dot_f32(mid, upper) + dot_f32(low, upper)
        for s in range(TOK_DEV // SUB):
            at = pl.ds(s * SUB, SUB)
            cross[at, :] = dot_t(c[at, :], b[at, :])

    t = lax.broadcasted_iota(jnp.int32, (SUB, SUB), 0)
    u = lax.broadcasted_iota(jnp.int32, (SUB, SUB), 1)
    lower = t >= u
    left = u < P_SIZE
    first = 2 * step
    cum_a = dot_f32(cums[...], pick(first, SUB))
    cum_b = dot_f32(cums[...], pick(first + 1, SUB))
    row_a = cum_t[pl.ds(first, 1), :]
    row_b = cum_t[pl.ds(first + 1, 1), :]
    carry = jnp.zeros((N, SUB), F32)
    before = jnp.zeros((1, SUB), F32)
    for s in range(TOK_DEV // SUB):
        at = pl.ds(s * SUB, SUB)
        a = cum_a[s * SUB : (s + 1) * SUB, :]
        bb = cum_b[s * SUB : (s + 1) * SUB, :]
        both = jnp.where(left, a, bb)
        xs = x[at, :]
        xf = xs.astype(F32)
        inner = cross[at, :]
        gap_a = jnp.where(lower, a - row_a[:, s * SUB : (s + 1) * SUB], NEG)
        gap_b = jnp.where(lower, bb - row_b[:, s * SUB : (s + 1) * SUB], NEG)
        mix_a = (jnp.exp(gap_a) * inner).astype(BF16)
        mix_b = (jnp.exp(gap_b) * inner).astype(BF16)
        x_a = jnp.where(left, xf, 0.0).astype(BF16)
        x_b = jnp.where(left, 0.0, xf).astype(BF16)
        y = dot_f32(
            jnp.concatenate([mix_a, mix_b], axis=1), jnp.concatenate([x_a, x_b], axis=0)
        )
        if s > 0:
            hi, low = split2(carry)
            cs = c[at, :]
            reach = dot_f32(
                jnp.concatenate([cs, cs], axis=1), jnp.concatenate([hi, low], axis=0)
            )
            y = y + jnp.exp(both - before) * reach
        part[at, :] = y + skip[...] * xf
        end = both[SUB - 1 : SUB, :]
        weighted = (xf * jnp.exp(end - both)).astype(BF16)
        added = lax.dot_general(
            b[at, :], weighted, (((0,), (0,)), ((), ())), preferred_element_type=F32
        )
        carry = jnp.exp(end - before) * carry + added
        before = end
    state[0:N, :] = carry
    state[N : N + 8, :] = jnp.broadcast_to(before, (8, SUB))


def scan_local(x_in, log_decay, b_in, c_in, skip_wide):
    whole = lambda shape: pl.BlockSpec(shape, lambda j: (0, 0))
    return pl.pallas_call(
        local_kernel,
        name="scan_local",
        out_shape=(
            jax.ShapeDtypeStruct((TOK_DEV, SCAN_HEADS * P_SIZE), F32),
            jax.ShapeDtypeStruct((N + 8, SCAN_HEADS * P_SIZE), F32),
            jax.ShapeDtypeStruct((TOK_DEV, SCAN_HEADS), F32),
        ),
        grid=(SCAN_HEADS // 2,),
        in_specs=[
            pl.BlockSpec((TOK_DEV, SUB), lambda j: (0, j)),
            whole((TOK_DEV, SCAN_HEADS)),
            whole((SCAN_HEADS, TOK_DEV)),
            whole((TOK_DEV, N)),
            whole((TOK_DEV, N)),
            pl.BlockSpec((1, SUB), lambda j: (0, j)),
        ],
        out_specs=(
            pl.BlockSpec((TOK_DEV, SUB), lambda j: (0, j)),
            pl.BlockSpec((N + 8, SUB), lambda j: (0, j)),
            whole((TOK_DEV, SCAN_HEADS)),
        ),
        scratch_shapes=[
            pltpu.VMEM((TOK_DEV, 3 * SCAN_HEADS), BF16),
            pltpu.VMEM((SCAN_HEADS, TOK_DEV), F32),
            pltpu.VMEM((TOK_DEV, SUB), F32),
        ],
        compiler_params=pltpu.CompilerParams(vmem_limit_bytes=32 << 20),
    )(x_in, log_decay, jnp.transpose(log_decay), b_in, c_in, skip_wide)


def finish_kernel(part, cum, c, carried, out):
    step = pl.program_id(0)
    width = out.shape[1]
    hi, mid, low = split3(cum[...])
    row = lax.broadcasted_iota(jnp.int32, (3 * SCAN_HEADS, width), 0) % SCAN_HEADS
    lane = lax.broadcasted_iota(jnp.int32, (3 * SCAN_HEADS, width), 1) // P_SIZE
    chosen = (row == lane + step * (width // P_SIZE)).astype(BF16)
    wide = dot_f32(jnp.concatenate([hi, mid, low], axis=1), chosen)
    hi, low = split2(carried[...])
    cs = c[...]
    reach = dot_f32(jnp.concatenate([cs, cs], axis=1), jnp.concatenate([hi, low], axis=0))
    out[...] = (part[...] + jnp.exp(wide) * reach).astype(BF16)


def scan_finish(part, cum, c_in, carried):
    width = 512
    whole = lambda shape: pl.BlockSpec(shape, lambda j: (0, 0))
    column = lambda rows: pl.BlockSpec((rows, width), lambda j: (0, j))
    return pl.pallas_call(
        finish_kernel,
        name="scan_finish",
        out_shape=jax.ShapeDtypeStruct((TOK_DEV, SCAN_HEADS * P_SIZE), BF16),
        grid=(SCAN_HEADS * P_SIZE // width,),
        in_specs=[
            column(TOK_DEV),
            whole((TOK_DEV, SCAN_HEADS)),
            whole((TOK_DEV, N)),
            column(N),
        ],
        out_specs=column(TOK_DEV),
        compiler_params=pltpu.CompilerParams(vmem_limit_bytes=32 << 20),
    )(part, cum, c_in, carried)


def joined(earlier, following):
    total = earlier[N:] + following[N:]
    state = jnp.exp(following[N : N + 1]) * earlier[:N] + following[:N]
    return jnp.concatenate([state, total], axis=0)


def carried_in(own, core, side, plane):
    width = own.shape[1]
    half, quarter = width // 2, width // 4
    mine = jnp.where(core == 0, own[:, :half], own[:, half:])
    other = swapped(jnp.where(core == 0, own[:, half:], own[:, :half]), 1)
    first = jnp.where(core == 0, mine, other)
    second = jnp.where(core == 0, other, mine)
    chip = joined(first, second)
    mine = jnp.where(side == 0, chip[:, :quarter], chip[:, quarter:])
    other = swapped(jnp.where(side == 0, chip[:, quarter:], chip[:, :quarter]), 2)
    lower = jnp.where(side == 0, mine, other)
    upper = jnp.where(side == 0, other, mine)
    total = joined(lower, upper)
    planes = lax.axis_size("ctx") // GROUP
    carry = jnp.zeros_like(total)
    if planes <= 4:
        for back in range(planes - 1, 0, -1):
            came = cyclic(total, GROUP * back)
            carry = jnp.where(plane >= back, joined(carry, came), carry)
    else:
        carry = jnp.where(plane >= 1, cyclic(total, GROUP), carry)
        reach = 1
        while reach < planes:
            came = cyclic(carry, GROUP * reach)
            carry = jnp.where(plane >= reach, joined(came, carry), carry)
            reach *= 2
    after = joined(carry, lower)
    keep = jnp.where(side == 0, carry, after)
    came = swapped(jnp.where(side == 0, after, carry)[:N], 2)
    keep = keep[:N]
    chip_in = jnp.concatenate(
        [jnp.where(side == 0, keep, came), jnp.where(side == 0, came, keep)], axis=1
    )
    next_in = jnp.exp(first[N : N + 1]) * chip_in + first[:N]
    keep = jnp.where(core == 0, chip_in, next_in)
    came = swapped(jnp.where(core == 0, next_in, chip_in), 1)
    return jnp.concatenate(
        [jnp.where(core == 0, keep, came), jnp.where(core == 0, came, keep)], axis=1
    )


def shards(queries, keys, values, x_in, log_decay, b_in, c_in, skip_d):
    device = lax.axis_index("ctx")
    core = device % 2
    side = (device // 2) % 2
    plane = device // GROUP
    flags = jnp.stack(
        [core, side, jnp.where(plane > 0, 1, 0)], axis=0
    ).astype(jnp.int32)
    owns = []
    low = 0
    for heads in CHUNKS:
        cols = slice(low * HD, (low + heads) * HD)
        owns.append(jnp.stack([keys[:, cols], values[:, cols]]))
        low += heads
    befores = [cyclic(own, GROUP) for own in owns]
    near_k, near_v = swapped(keys, 1), swapped(values, 1)
    skip_wide = jnp.repeat(skip_d, P_SIZE)[None, :]
    part, own_state, cum = scan_local(x_in, log_decay, b_in, c_in, skip_wide)
    carried = carried_in(own_state, core, side, plane)
    outs = []
    low = 0
    for heads, own, before in zip(CHUNKS, owns, befores):
        d = swapped(jnp.where(side == 0, own, before), 2)
        e = swapped(before, 1)
        g = swapped(d, 1)
        outs.append(
            attend(flags, low, heads, queries, keys, values, before, d, e, g, near_k, near_v)
        )
        low += heads
    scan_out = scan_finish(part, cum, c_in, carried)
    return (jnp.concatenate(outs, axis=1), scan_out)


def solution(mesh):
    row = P(("seqs", "ctx"), None)
    in_specs = (row,) * 7 + (P(),)
    return jax.shard_map(
        shards, mesh=mesh, in_specs=in_specs, out_specs=(row, row), check_vma=False
    )
```

time: 522 us -> 263 us (0.50)
  matrix products: 135 us -> 0 us
  local copies, waits for them, and re-layouts: 94.3 us -> 16 us
  Pallas kernels: 0 us -> 72.9 us
  blocking collectives: 72 us -> 0 us
  waiting for transfers between devices: 130 us -> 115 us
  other arithmetic: 29.7 us -> 15.4 us
  between operations: 15 us -> 2 us
    sub x8 -> x0, matrix products: 83.1 us -> none  [attend_group(): probs = jnp.where(allowed[None], jnp.exp(scores - row_max), 0.0)]
    pallas_call x0 -> x10, Pallas kernels: none -> 72.9 us  [the longest x8 54.5 us: attend(): pl.pallas_call(attend_kernel, name='attend', out_shape=jax.ShapeDtypeStru...]
    all_gather x1 -> x0, blocking collectives: 72 us -> none  [carried_in(): everything = jax.tree.map(lambda part: lax.all_gather(part, axis), array)]
    dot_general x12 -> x0, matrix products: 52.3 us -> none  [the longest x8 35.6 us: attend_group(): jnp.einsum('hij,jhd->ihd', weights, value_heads, preferred_element_type=j...]
    unnamed x56 -> x152, local copies, waits for them, and re-layouts: 46.9 us -> 11.8 us
    slice x13 -> x1, local copies, waits for them, and re-layouts: 32.5 us -> 0.01 us  [joined(): total = earlier[N:] + following[N:]]
    select_n x16 -> x19, other arithmetic: 23.4 us -> 6.86 us  [the longest x8 3.68 us: shards(): d = swapped(jnp.where(side == 0, own, before), 2)]
    ppermute x8 -> x41, waiting for transfers between devices: 129 us -> 115 us  [the longest x30 66.3 us: swapped(): return lax.ppermute(array, 'ctx', [(i, i ^ bit) for i in range(count)])]
  transfers between devices with their start and end apart: 9 -> 41, of which waited for: 6 -> 16; matrix products, arithmetic and copies ran while one was open for 42% -> 6% of each run, Pallas kernels for 0% -> 26%
where the time goes in v1:
time: 263 us; the launch traced here: 259 us
  waiting for transfers between devices  115 us (44%)
  Pallas kernels  72.9 us (28%)
  starting transfers between devices  37.6 us (14%)
  local copies, waits for them, and re-layouts  16 us (6%)
  other arithmetic  15.4 us (6%)
    ppermute x30, waiting for transfers between devices, swapped(): return lax.ppermute(array, 'ctx', [(i, i ^ bit) for i in range(count)])  66.3 us
    pallas_call x8, Pallas kernels, attend(): pl.pallas_call(attend_kernel, name='attend', out_shape=jax.ShapeDtypeStru...  54.5 us
    ppermute x11, waiting for transfers between devices, cyclic(): lax.ppermute(array, 'ctx', [(i, (i + by) % count) for i in range(count)])  48.5 us
    ppermute x30, starting transfers between devices, swapped(): return lax.ppermute(array, 'ctx', [(i, i ^ bit) for i in range(count)])  24.6 us
    pallas_call x1, Pallas kernels, scan_local(): pl.pallas_call(local_kernel, name='scan_local', out_shape=(jax.ShapeDtype...  15.1 us
    ppermute x11, starting transfers between devices, cyclic(): lax.ppermute(array, 'ctx', [(i, (i + by) % count) for i in range(count)])  13 us
    unnamed x152, local copies, waits for them, and re-layouts  11.8 us
    another operation x8, other arithmetic, shards(): owns.append(jnp.stack([keys[:, cols], values[:, cols]]))  8.25 us
  transfers between devices with their start and end apart: 41, of which 16 were waited for; matrix products, arithmetic and copies ran while one was open for 6% of the time, Pallas kernels for 26%

profile of v1, /device:TPU:13, one launch (start us, length us, event | category | flops | bytes accessed | tf_op | source)
XLA Modules:
  0.0 258.7 jit_solution(5495985556037169882)
XLA Ops:
  0.6 2.7 %slice_bitcast_fusion = (bf16[1,512,256]{2,1,0:T(8,128)(2,1)}, bf16[1,512,256]{2,1,0:T(8,128)(2,1)}, bf16[1,512,256]{2,1,0:T(8,128)(2,1)}, bf16[1,512,256]{2,1,0...) fusion(bf16[512,2048]{1,0:T(8,128)(2,1)} %v.15), kind=kLoop, calls=%fused_computation.26 | loop fusion | bytes 4194304 | tf_op jit(solution)/shard_map/stack | solution.py:348
  3.4 1.3 slice_bitcast_fusion.1
  4.7 0.8 pad_maximum_fusion
  5.6 1.3 collective-permute-start
  6.9 0.8 pad_maximum_fusion.1
  7.7 1.3 collective-permute-start.6
  9.0 0.9 pad_maximum_fusion.2
  9.9 0.8 pad_maximum_fusion.3
  10.7 1.3 collective-permute-start.14
  12.0 0.8 copy.10.decay
  13.3 1.6 copy-done.10
  14.9 0.9 copy-done.11
  15.8 15.1 %scan_local.1 = (f32[512,2048]{1,0:T(8,128)S(1)}, f32[72,2048]{1,0:T(8,128)S(1)}, f32[512,32]{1,0:T(8,128)S(1)}) custom-call(bf16[512,2048]{1,0:T(8,128)(2,1)S(1)} %copy-done.10, f32[512,32]{1,0:T(8,128)S(1)} %copy-done.11, f32[32,512]{1,0:T(8,128)S(1)} %bitcast.43, bf16[512,64]{1,0:T(8,128)(2,1)S(1)} %copy.11.b, bf16[512,64]{1,0:T(8,128)(2,1)S(1)} %copy.12.c, ...), custom_call_target="tpu_custom_call" | custom-call | tf_op jit(solution)/shard_map/scan_local/pallas_call | solution.py:224
  30.9 2.0 copy-done.2
  33.6 0.8 slice_select_fusion.1
  34.4 1.8 collective-permute-start.34
  36.2 1.9 pad_maximum_fusion.4
  38.1 0.8 pad_maximum_fusion.5
  39.0 1.1 pad_maximum_fusion.6
  40.0 1.1 pad_maximum_fusion.7
  41.1 1.0 broadcast_select_fusion.9
  42.6 5.2 %collective-permute-done.35 = f32[72,512]{1,0:T(8,128)S(1)} collective-permute-done((f32[72,512]{1,0:T(8,128)S(1)}, f32[72,512]{1,0:T(8,128)S(1)}, u32[]{:S(2)}, u32[]{:S(2)}) %collective-permute-start.35) | collective-permute-done | bytes 147488 | tf_op jit(solution)/shard_map/ppermute | solution.py:33
  48.2 9.1 %collective-permute-done.38 = f32[72,512]{1,0:T(8,128)S(1)} collective-permute-done((f32[72,512]{1,0:T(8,128)S(1)}, f32[72,512]{1,0:T(8,128)S(1)}, u32[]{:S(2)}, u32[]{:S(2)}) %collective-permute-start.38) | collective-permute-done | bytes 147488 | tf_op jit(solution)/shard_map/ppermute | solution.py:28
  58.1 6.5 %collective-permute-done.37 = f32[72,512]{1,0:T(8,128)S(1)} collective-permute-done((f32[72,512]{1,0:T(8,128)S(1)}, f32[72,512]{1,0:T(8,128)S(1)}, u32[]{:S(2)}, u32[]{:S(2)}) %collective-permute-start.37) | collective-permute-done | bytes 147488 | tf_op jit(solution)/shard_map/ppermute | solution.py:28
  64.6 1.8 collective-permute-start.36
  66.5 5.6 %collective-permute-done.36 = f32[72,512]{1,0:T(8,128)S(1)} collective-permute-done((f32[72,512]{1,0:T(8,128)S(1)}, f32[72,512]{1,0:T(8,128)S(1)}, u32[]{:S(2)}, u32[]{:S(2)}) %collective-permute-start.36) | collective-permute-done | bytes 147488 | tf_op jit(solution)/shard_map/ppermute | solution.py:28
  72.3 1.3 collective-permute-start.22
  73.9 1.1 broadcast_select_fusion.7
  75.0 2.5 collective-permute-done.39
  77.5 4.3 %collective-permute-start.26 = (bf16[2,512,256]{2,1,0:T(8,128)(2,1)S(1)}, bf16[2,512,256]{2,1,0:T(8,128)(2,1)S(1)}, u32[]{:S(2)}, u32[]{:S(2)}) collective-permute-start(bf16[2,512,256]{2,1,0:T(8,128)(2,1)S(1)} %pad_maximum_fusion.6), channel_id=1, source_target_pairs={{0,4},{1,5},{2,6},{3,7},{4,8},{5,9},{6,10},{7,11},{8,12},{9,13},{1... | collective-permute-start | bytes 1572872 | tf_op jit(solution)/shard_map/ppermute | solution.py:28
  82.9 3.1 %collective-permute-done.18.z = bf16[2,512,256]{2,1,0:T(8,128)(2,1)S(1)} collective-permute-done((bf16[2,512,256]{2,1,0:T(8,128)(2,1)S(1)}, bf16[2,512,256]{2,1,0:T(8,128)(2,1)S(1)}, u32[]{:S(2)}, u32[]{:S(2)}) %collective-permute-start.18) | collective-permute-done | bytes 524320 | tf_op jit(solution)/shard_map/ppermute | solution.py:28
  86.0 3.5 %collective-permute-start.2 = (bf16[2,512,256]{2,1,0:T(8,128)(2,1)}, bf16[2,512,256]{2,1,0:T(8,128)(2,1)S(1)}, u32[]{:S(2)}, u32[]{:S(2)}) collective-permute-start(bf16[2,512,256]{2,1,0:T(8,128)(2,1)} %collective-permute-done.z), channel_id=1, source_target_pairs={{0,1},{1,0},{2,3},{3,2},{4,5},{5,4},{6,7},{7,6},{8,9},{9,8},{10,11... | collective-permute-start | bytes 1572872 | tf_op jit(solution)/shard_map/ppermute | solution.py:33
  89.5 7.7 %collective-permute-done.22.z = bf16[2,512,256]{2,1,0:T(8,128)(2,1)S(1)} collective-permute-done((bf16[2,512,256]{2,1,0:T(8,128)(2,1)S(1)}, bf16[2,512,256]{2,1,0:T(8,128)(2,1)S(1)}, u32[]{:S(2)}, u32[]{:S(2)}) %collective-permute-start.22) | collective-permute-done | bytes 524320 | tf_op jit(solution)/shard_map/ppermute | solution.py:28
  97.2 3.5 %collective-permute-start.40 = (f32[64,1024]{1,0:T(8,128)S(1)}, f32[64,1024]{1,0:T(8,128)S(1)}, u32[]{:S(2)}, u32[]{:S(2)}) collective-permute-start(f32[64,1024]{1,0:T(8,128)S(1)} %fusion), channel_id=1, source_target_pairs={{0,1},{1,0},{2,3},{3,2},{4,5},{5,4},{6,7},{7,6},{8,9},{9,8},{10,11... | collective-permute-start | bytes 786440 | tf_op jit(solution)/shard_map/ppermute | solution.py:33
  100.8 1.1 broadcast_select_fusion.6
  101.9 6.5 %collective-permute-done.26.z = bf16[2,512,256]{2,1,0:T(8,128)(2,1)S(1)} collective-permute-done((bf16[2,512,256]{2,1,0:T(8,128)(2,1)S(1)}, bf16[2,512,256]{2,1,0:T(8,128)(2,1)S(1)}, u32[]{:S(2)}, u32[]{:S(2)}) %collective-permute-start.26) | collective-permute-done | bytes 524320 | tf_op jit(solution)/shard_map/ppermute | solution.py:28
  108.7 1.1 broadcast_select_fusion.5
  109.8 10.0 %collective-permute-done.30.z = bf16[2,512,256]{2,1,0:T(8,128)(2,1)S(1)} collective-permute-done((bf16[2,512,256]{2,1,0:T(8,128)(2,1)S(1)}, bf16[2,512,256]{2,1,0:T(8,128)(2,1)S(1)}, u32[]{:S(2)}, u32[]{:S(2)}) %collective-permute-start.30) | collective-permute-done | bytes 524320 | tf_op jit(solution)/shard_map/ppermute | solution.py:28
  119.8 1.9 collective-permute-start.8
  123.1 1.2 collective-permute-start.15
  124.9 11.1 %collective-permute-done.11.d = bf16[2,512,256]{2,1,0:T(8,128)(2,1)} collective-permute-done((bf16[2,512,256]{2,1,0:T(8,128)(2,1)S(1)}, bf16[2,512,256]{2,1,0:T(8,128)(2,1)}, u32[]{:S(2)}, u32[]{:S(2)}) %collective-permute-start.11) | collective-permute-done | bytes 524320 | tf_op jit(solution)/shard_map/ppermute | solution.py:33
  136.0 1.3 collective-permute-start.5
  137.6 9.5 %collective-permute-done.15.d = bf16[2,512,256]{2,1,0:T(8,128)(2,1)S(1)} collective-permute-done((bf16[2,512,256]{2,1,0:T(8,128)(2,1)S(1)}, bf16[2,512,256]{2,1,0:T(8,128)(2,1)S(1)}, u32[]{:S(2)}, u32[]{:S(2)}) %collective-permute-start.15) | collective-permute-done | bytes 524320 | tf_op jit(solution)/shard_map/ppermute | solution.py:33
  147.1 1.3 collective-permute-start.20
  148.9 9.5 %collective-permute-done.19.d = bf16[2,512,256]{2,1,0:T(8,128)(2,1)S(1)} collective-permute-done((bf16[2,512,256]{2,1,0:T(8,128)(2,1)S(1)}, bf16[2,512,256]{2,1,0:T(8,128)(2,1)S(1)}, u32[]{:S(2)}, u32[]{:S(2)}) %collective-permute-start.19) | collective-permute-done | bytes 524320 | tf_op jit(solution)/shard_map/ppermute | solution.py:33
  158.3 1.3 collective-permute-start.24
  160.0 9.6 %collective-permute-done.23.d = bf16[2,512,256]{2,1,0:T(8,128)(2,1)S(1)} collective-permute-done((bf16[2,512,256]{2,1,0:T(8,128)(2,1)S(1)}, bf16[2,512,256]{2,1,0:T(8,128)(2,1)S(1)}, u32[]{:S(2)}, u32[]{:S(2)}) %collective-permute-start.23) | collective-permute-done | bytes 524320 | tf_op jit(solution)/shard_map/ppermute | solution.py:33
  170.6 1.5 collective-permute-start.3
  172.1 8.7 %collective-permute-done.27.d = bf16[2,512,256]{2,1,0:T(8,128)(2,1)S(1)} collective-permute-done((bf16[2,512,256]{2,1,0:T(8,128)(2,1)S(1)}, bf16[2,512,256]{2,1,0:T(8,128)(2,1)S(1)}, u32[]{:S(2)}, u32[]{:S(2)}) %collective-permute-start.27) | collective-permute-done | bytes 524320 | tf_op jit(solution)/shard_map/ppermute | solution.py:33
  180.8 1.3 collective-permute-start.9
  182.1 10.1 %collective-permute-done.31.d = bf16[2,512,256]{2,1,0:T(8,128)(2,1)} collective-permute-done((bf16[2,512,256]{2,1,0:T(8,128)(2,1)S(1)}, bf16[2,512,256]{2,1,0:T(8,128)(2,1)}, u32[]{:S(2)}, u32[]{:S(2)}) %collective-permute-start.31) | collective-permute-done | bytes 524320 | tf_op jit(solution)/shard_map/ppermute | solution.py:33
  192.2 0.8 collective-permute-start.13
  193.6 1.2 broadcast_select_fusion.11
  195.8 2.2 copy-done.3
  198.0 3.3 %scan_finish.1 = bf16[512,2048]{1,0:T(8,128)(2,1)} custom-call(f32[512,2048]{1,0:T(8,128)S(1)} %copy-done.3, f32[512,32]{1,0:T(8,128)S(1)} %copy-done.33, bf16[512,64]{1,0:T(8,128)(2,1)S(1)} %copy.12.c, f32[64,2048]{1,0:T(8,128)S(1)} %pad_maximum_fusion.8.carried), custom_call_target="tpu_custom_call" | custom-call | tf_op jit(solution)/shard_map/scan_finish/pallas_call | solution.py:273
  201.3 6.8 %attend.8 = bf16[512,256]{1,0:T(8,128)(2,1)S(1)} custom-call(s32[3]{0:T(128)S(1)} %pad_add_fusion.flags, bf16[512,2048]{1,0:T(8,128)(2,1)S(1)} %copy-done.1, bf16[512,2048]{1,0:T(8,128)(2,1)S(1)} %copy-done, bf16[512,2048]{1,0:T(8,128)(2,1)} %v.15, bf16[2,512,256]{2,1,0:T(8,128)(2,1)} %collective-permute-done.z, ...), custom_call_target="tpu_custom_call" | custom-call | tf_op jit(solution)/shard_map/attend/pallas_call | solution.py:117
  208.1 6.8 %attend.9 = bf16[512,256]{1,0:T(8,128)(2,1)S(1)} custom-call(s32[3]{0:T(128)S(1)} %pad_add_fusion.flags, bf16[512,2048]{1,0:T(8,128)(2,1)S(1)} %copy-done.1, bf16[512,2048]{1,0:T(8,128)(2,1)S(1)} %copy-done, bf16[512,2048]{1,0:T(8,128)(2,1)} %v.15, bf16[2,512,256]{2,1,0:T(8,128)(2,1)} %collective-permute-done.6.z, ...), custom_call_target="tpu_custom_call" | custom-call | tf_op jit(solution)/shard_map/attend/pallas_call | solution.py:117
  215.0 7.0 %attend.10 = bf16[512,256]{1,0:T(8,128)(2,1)S(1)} custom-call(s32[3]{0:T(128)S(1)} %pad_add_fusion.flags, bf16[512,2048]{1,0:T(8,128)(2,1)S(1)} %copy-done.1, bf16[512,2048]{1,0:T(8,128)(2,1)S(1)} %copy-done, bf16[512,2048]{1,0:T(8,128)(2,1)} %v.15, bf16[2,512,256]{2,1,0:T(8,128)(2,1)} %collective-permute-done.10.z, ...), custom_call_target="tpu_custom_call" | custom-call | tf_op jit(solution)/shard_map/attend/pallas_call | solution.py:117
  222.6 6.7 %attend.11 = bf16[512,256]{1,0:T(8,128)(2,1)S(1)} custom-call(s32[3]{0:T(128)S(1)} %pad_add_fusion.flags, bf16[512,2048]{1,0:T(8,128)(2,1)S(1)} %copy-done.1, bf16[512,2048]{1,0:T(8,128)(2,1)S(1)} %copy-done, bf16[512,2048]{1,0:T(8,128)(2,1)} %v.15, bf16[2,512,256]{2,1,0:T(8,128)(2,1)S(1)} %collective-permute-done.14.z, bf16[2,512,256]{2,1,0:T(8,128)(2,1)S(1)} %copy-done.15, ...), custom_call_target="tpu_custom_call" | custom-call | tf_op jit(solution)/shard_map/attend/pallas_call | solution.py:117
  229.4 6.9 %attend.12 = bf16[512,256]{1,0:T(8,128)(2,1)S(1)} custom-call(s32[3]{0:T(128)S(1)} %pad_add_fusion.flags, bf16[512,2048]{1,0:T(8,128)(2,1)S(1)} %copy-done.1, bf16[512,2048]{1,0:T(8,128)(2,1)S(1)} %copy-done, bf16[512,2048]{1,0:T(8,128)(2,1)} %v.15, bf16[2,512,256]{2,1,0:T(8,128)(2,1)S(1)} %collective-permute-done.18.z, bf16[2,512,256]{2,1,0:T(8,128)(2,1)S(1)} %copy-done.23, ...), custom_call_target="tpu_custom_call" | custom-call | tf_op jit(solution)/shard_map/attend/pallas_call | solution.py:117
  236.4 6.7 %attend.13 = bf16[512,256]{1,0:T(8,128)(2,1)S(1)} custom-call(s32[3]{0:T(128)S(1)} %pad_add_fusion.flags, bf16[512,2048]{1,0:T(8,128)(2,1)S(1)} %copy-done.1, bf16[512,2048]{1,0:T(8,128)(2,1)S(1)} %copy-done, bf16[512,2048]{1,0:T(8,128)(2,1)} %v.15, bf16[2,512,256]{2,1,0:T(8,128)(2,1)S(1)} %copy-done.5, bf16[2,512,256]{2,1,0:T(8,128)(2,1)S(1)} %copy-done.27, ...), custom_call_target="tpu_custom_call" | custom-call | tf_op jit(solution)/shard_map/attend/pallas_call | solution.py:117
  243.2 7.0 %attend.14 = bf16[512,256]{1,0:T(8,128)(2,1)S(1)} custom-call(s32[3]{0:T(128)S(1)} %pad_add_fusion.flags, bf16[512,2048]{1,0:T(8,128)(2,1)S(1)} %copy-done.1, bf16[512,2048]{1,0:T(8,128)(2,1)S(1)} %copy-done, bf16[512,2048]{1,0:T(8,128)(2,1)} %v.15, bf16[2,512,256]{2,1,0:T(8,128)(2,1)S(1)} %copy-done.9, bf16[2,512,256]{2,1,0:T(8,128)(2,1)S(1)} %copy-done.29, ...), custom_call_target="tpu_custom_call" | custom-call | tf_op jit(solution)/shard_map/attend/pallas_call | solution.py:117
  250.3 6.7 %attend.15 = bf16[512,256]{1,0:T(8,128)(2,1)S(1)} custom-call(s32[3]{0:T(128)S(1)} %pad_add_fusion.flags, bf16[512,2048]{1,0:T(8,128)(2,1)S(1)} %copy-done.1, bf16[512,2048]{1,0:T(8,128)(2,1)S(1)} %copy-done, bf16[512,2048]{1,0:T(8,128)(2,1)} %v.15, bf16[2,512,256]{2,1,0:T(8,128)(2,1)S(1)} %copy-done.7, bf16[2,512,256]{2,1,0:T(8,128)(2,1)} %collective-permute-done.31.d, ...), custom_call_target="tpu_custom_call" | custom-call | tf_op jit(solution)/shard_map/attend/pallas_call | solution.py:117
  257.1 1.3 copy-done.69
  (234 shorter events, 11.0 us)
Async XLA Ops:
  5.6 66.8 %collective-permute-start = (bf16[2,512,256]{2,1,0:T(8,128)(2,1)}, bf16[2,512,256]{2,1,0:T(8,128)(2,1)}, u32[]{:S(2)}, u32[]{:S(2)}) collective-permute-start(bf16[2,512,256]{2,1,0:T(8,128)(2,1)} %pad_maximum_fusion), channel_id=1, source_target_pairs={{0,4},{1,5},{2,6},{3,7},{4,8},{5,9},{6,10},{7,11},{8,12},{9,13},{1... | collective-permute-start | bytes 1572872 | tf_op jit(solution)/shard_map/ppermute | solution.py:28
  7.7 66.0 %collective-permute-start.6 = (bf16[2,512,256]{2,1,0:T(8,128)(2,1)}, bf16[2,512,256]{2,1,0:T(8,128)(2,1)}, u32[]{:S(2)}, u32[]{:S(2)}) collective-permute-start(bf16[2,512,256]{2,1,0:T(8,128)(2,1)} %pad_maximum_fusion.1), channel_id=1, source_target_pairs={{0,4},{1,5},{2,6},{3,7},{4,8},{5,9},{6,10},{7,11},{8,12},{9,13},{1... | collective-permute-start | bytes 1572872 | tf_op jit(solution)/shard_map/ppermute | solution.py:28
  9.8 72.0 %collective-permute-start.10 = (bf16[2,512,256]{2,1,0:T(8,128)(2,1)}, bf16[2,512,256]{2,1,0:T(8,128)(2,1)}, u32[]{:S(2)}, u32[]{:S(2)}) collective-permute-start(bf16[2,512,256]{2,1,0:T(8,128)(2,1)} %pad_maximum_fusion.2), channel_id=1, source_target_pairs={{0,4},{1,5},{2,6},{3,7},{4,8},{5,9},{6,10},{7,11},{8,12},{9,13},{1... | collective-permute-start | bytes 1572872 | tf_op jit(solution)/shard_map/ppermute | solution.py:28
  10.7 71.9 %collective-permute-start.14 = (bf16[2,512,256]{2,1,0:T(8,128)(2,1)}, bf16[2,512,256]{2,1,0:T(8,128)(2,1)S(1)}, u32[]{:S(2)}, u32[]{:S(2)}) collective-permute-start(bf16[2,512,256]{2,1,0:T(8,128)(2,1)} %pad_maximum_fusion.3), channel_id=1, source_target_pairs={{0,4},{1,5},{2,6},{3,7},{4,8},{5,9},{6,10},{7,11},{8,12},{9,13},{1... | collective-permute-start | bytes 1572872 | tf_op jit(solution)/shard_map/ppermute | solution.py:28
  34.4 6.7 %collective-permute-start.34 = (f32[72,1024]{1,0:T(8,128)}, f32[72,1024]{1,0:T(8,128)}, u32[]{:S(2)}, u32[]{:S(2)}) collective-permute-start(f32[72,1024]{1,0:T(8,128)} %slice_select_fusion.1), channel_id=1, source_target_pairs={{0,1},{1,0},{2,3},{3,2},{4,5},{5,4},{6,7},{7,6},{8,9},{9,8},{10,11... | collective-permute-start | bytes 884744 | tf_op jit(solution)/shard_map/ppermute | solution.py:33
  42.2 40.4 %copy-start.35 = (f32[72,1024]{1,0:T(8,128)}, f32[72,1024]{1,0:T(8,128)S(1)}, u32[]{:S(2)}) copy-start(f32[72,1024]{1,0:T(8,128)S(1)} %get-tuple-element.25) | copy-start | bytes 884740
  42.2 29.9 %copy-start.65 = (bf16[2,512,256]{2,1,0:T(8,128)(2,1)S(1)}, bf16[2,512,256]{2,1,0:T(8,128)(2,1)}, u32[]{:S(2)}) copy-start(bf16[2,512,256]{2,1,0:T(8,128)(2,1)} %pad_maximum_fusion.4) | copy-start | bytes 1572868
  42.3 5.5 %collective-permute-start.35 = (f32[72,512]{1,0:T(8,128)S(1)}, f32[72,512]{1,0:T(8,128)S(1)}, u32[]{:S(2)}, u32[]{:S(2)}) collective-permute-start(f32[72,512]{1,0:T(8,128)S(1)} %broadcast_select_fusion.15), channel_id=1, source_target_pairs={{0,2},{1,3},{2,0},{3,1},{4,6},{5,7},{6,4},{7,5},{8,10},{9,11},{10,... | collective-permute-start | bytes 442376 | tf_op jit(solution)/shard_map/ppermute | solution.py:33
  47.9 26.0 %copy-start.59 = (bf16[1,512,256]{2,1,0:T(8,128)(2,1)S(1)}, bf16[1,512,256]{2,1,0:T(8,128)(2,1)}, u32[]{:S(2)}) copy-start(bf16[1,512,256]{2,1,0:T(8,128)(2,1)} %copy-done.58) | copy-start | bytes 786436
  48.0 9.3 %collective-permute-start.38 = (f32[72,512]{1,0:T(8,128)S(1)}, f32[72,512]{1,0:T(8,128)S(1)}, u32[]{:S(2)}, u32[]{:S(2)}) collective-permute-start(f32[72,512]{1,0:T(8,128)S(1)} %pad_maximum_fusion.11), channel_id=1, source_target_pairs={{0,12},{1,13},{2,14},{3,15},{4,0},{5,1},{6,2},{7,3},{8,4},{9,5},{1... | collective-permute-start | bytes 442376 | tf_op jit(solution)/shard_map/ppermute | solution.py:28
  57.3 7.3 %collective-permute-start.37 = (f32[72,512]{1,0:T(8,128)S(1)}, f32[72,512]{1,0:T(8,128)S(1)}, u32[]{:S(2)}, u32[]{:S(2)}) collective-permute-start(f32[72,512]{1,0:T(8,128)S(1)} %pad_maximum_fusion.11), channel_id=1, source_target_pairs={{0,8},{1,9},{2,10},{3,11},{4,12},{5,13},{6,14},{7,15},{8,0},{9,1},... | collective-permute-start | bytes 442376 | tf_op jit(solution)/shard_map/ppermute | solution.py:28
  64.6 7.5 %collective-permute-start.36 = (f32[72,512]{1,0:T(8,128)S(1)}, f32[72,512]{1,0:T(8,128)S(1)}, u32[]{:S(2)}, u32[]{:S(2)}) collective-permute-start(f32[72,512]{1,0:T(8,128)S(1)} %pad_maximum_fusion.11), channel_id=1, source_target_pairs={{0,4},{1,5},{2,6},{3,7},{4,8},{5,9},{6,10},{7,11},{8,12},{9,13},{1... | collective-permute-start | bytes 442376 | tf_op jit(solution)/shard_map/ppermute | solution.py:28
  72.1 13.8 %collective-permute-start.18 = (bf16[2,512,256]{2,1,0:T(8,128)(2,1)S(1)}, bf16[2,512,256]{2,1,0:T(8,128)(2,1)S(1)}, u32[]{:S(2)}, u32[]{:S(2)}) collective-permute-start(bf16[2,512,256]{2,1,0:T(8,128)(2,1)S(1)} %copy-done.65), channel_id=1, source_target_pairs={{0,4},{1,5},{2,6},{3,7},{4,8},{5,9},{6,10},{7,11},{8,12},{9,13},{1... | collective-permute-start | bytes 1572872 | tf_op jit(solution)/shard_map/ppermute | solution.py:28
  72.2 28.6 %copy-start.55 = (bf16[1,512,256]{2,1,0:T(8,128)(2,1)S(1)}, bf16[1,512,256]{2,1,0:T(8,128)(2,1)}, u32[]{:S(2)}) copy-start(bf16[1,512,256]{2,1,0:T(8,128)(2,1)} %copy-done.54) | copy-start | bytes 786436
  72.2 28.6 %copy-start.57 = (bf16[1,512,256]{2,1,0:T(8,128)(2,1)S(1)}, bf16[1,512,256]{2,1,0:T(8,128)(2,1)}, u32[]{:S(2)}) copy-start(bf16[1,512,256]{2,1,0:T(8,128)(2,1)} %copy-done.56) | copy-start | bytes 786436
  72.3 36.4 %copy-start.51 = (bf16[1,512,256]{2,1,0:T(8,128)(2,1)S(1)}, bf16[1,512,256]{2,1,0:T(8,128)(2,1)}, u32[]{:S(2)}) copy-start(bf16[1,512,256]{2,1,0:T(8,128)(2,1)} %copy-done.50) | copy-start | bytes 786436
  72.3 36.4 %copy-start.53 = (bf16[1,512,256]{2,1,0:T(8,128)(2,1)S(1)}, bf16[1,512,256]{2,1,0:T(8,128)(2,1)}, u32[]{:S(2)}) copy-start(bf16[1,512,256]{2,1,0:T(8,128)(2,1)} %copy-done.52) | copy-start | bytes 786436
  72.3 24.9 %collective-permute-start.22 = (bf16[2,512,256]{2,1,0:T(8,128)(2,1)S(1)}, bf16[2,512,256]{2,1,0:T(8,128)(2,1)S(1)}, u32[]{:S(2)}, u32[]{:S(2)}) collective-permute-start(bf16[2,512,256]{2,1,0:T(8,128)(2,1)S(1)} %copy-done.64), channel_id=1, source_target_pairs={{0,4},{1,5},{2,6},{3,7},{4,8},{5,9},{6,10},{7,11},{8,12},{9,13},{1... | collective-permute-start | bytes 1572872 | tf_op jit(solution)/shard_map/ppermute | solution.py:28
  73.7 3.8 %collective-permute-start.39 = (f32[64,512]{1,0:T(8,128)S(1)}, f32[64,512]{1,0:T(8,128)S(1)}, u32[]{:S(2)}, u32[]{:S(2)}) collective-permute-start(f32[64,512]{1,0:T(8,128)S(1)} %fusion.5), channel_id=1, source_target_pairs={{0,2},{1,3},{2,0},{3,1},{4,6},{5,7},{6,4},{7,5},{8,10},{9,11},{10,... | collective-permute-start | bytes 393224 | tf_op jit(solution)/shard_map/ppermute | solution.py:33
  77.5 30.9 %collective-permute-start.26 = (bf16[2,512,256]{2,1,0:T(8,128)(2,1)S(1)}, bf16[2,512,256]{2,1,0:T(8,128)(2,1)S(1)}, u32[]{:S(2)}, u32[]{:S(2)}) collective-permute-start(bf16[2,512,256]{2,1,0:T(8,128)(2,1)S(1)} %pad_maximum_fusion.6), channel_id=1, source_target_pairs={{0,4},{1,5},{2,6},{3,7},{4,8},{5,9},{6,10},{7,11},{8,12},{9,13},{1... | collective-permute-start | bytes 1572872 | tf_op jit(solution)/shard_map/ppermute | solution.py:28
  81.8 40.8 %copy-start.62 = (f32[64,512]{1,0:T(8,128)}, f32[64,512]{1,0:T(8,128)S(1)}, u32[]{:S(2)}) copy-start(f32[64,512]{1,0:T(8,128)S(1)} %get-tuple-element.30) | copy-start | bytes 393220
  81.8 40.8 %copy-start.63 = (f32[64,512]{1,0:T(8,128)}, f32[64,512]{1,0:T(8,128)S(1)}, u32[]{:S(2)}) copy-start(f32[64,512]{1,0:T(8,128)S(1)} %get-tuple-element.31) | copy-start | bytes 393220
  81.9 40.7 %copy-start.47 = (bf16[1,512,256]{2,1,0:T(8,128)(2,1)S(1)}, bf16[1,512,256]{2,1,0:T(8,128)(2,1)}, u32[]{:S(2)}) copy-start(bf16[1,512,256]{2,1,0:T(8,128)(2,1)} %copy-done.46) | copy-start | bytes 786436
  81.9 40.7 %copy-start.49 = (bf16[1,512,256]{2,1,0:T(8,128)(2,1)S(1)}, bf16[1,512,256]{2,1,0:T(8,128)(2,1)}, u32[]{:S(2)}) copy-start(bf16[1,512,256]{2,1,0:T(8,128)(2,1)} %copy-done.48) | copy-start | bytes 786436
  81.9 37.9 %collective-permute-start.30 = (bf16[2,512,256]{2,1,0:T(8,128)(2,1)S(1)}, bf16[2,512,256]{2,1,0:T(8,128)(2,1)S(1)}, u32[]{:S(2)}, u32[]{:S(2)}) collective-permute-start(bf16[2,512,256]{2,1,0:T(8,128)(2,1)S(1)} %pad_maximum_fusion.7), channel_id=1, source_target_pairs={{0,4},{1,5},{2,6},{3,7},{4,8},{5,9},{6,10},{7,11},{8,12},{9,13},{1... | collective-permute-start | bytes 1572872 | tf_op jit(solution)/shard_map/ppermute | solution.py:28
  82.6 54.6 %copy-start.44 = (bf16[1,512,256]{2,1,0:T(8,128)(2,1)S(1)}, bf16[1,512,256]{2,1,0:T(8,128)(2,1)}, u32[]{:S(2)}) copy-start(bf16[1,512,256]{2,1,0:T(8,128)(2,1)} %get-tuple-element.19) | copy-start | bytes 786436
  82.6 54.6 %copy-start.45 = (bf16[1,512,256]{2,1,0:T(8,128)(2,1)S(1)}, bf16[1,512,256]{2,1,0:T(8,128)(2,1)}, u32[]{:S(2)}) copy-start(bf16[1,512,256]{2,1,0:T(8,128)(2,1)} %get-tuple-element.11) | copy-start | bytes 786436
  82.6 40.1 %collective-permute-start.1 = (bf16[2,512,256]{2,1,0:T(8,128)(2,1)S(1)}, bf16[2,512,256]{2,1,0:T(8,128)(2,1)}, u32[]{:S(2)}, u32[]{:S(2)}) collective-permute-start(bf16[2,512,256]{2,1,0:T(8,128)(2,1)S(1)} %broadcast_select_fusion.7), channel_id=1, source_target_pairs={{0,2},{1,3},{2,0},{3,1},{4,6},{5,7},{6,4},{7,5},{8,10},{9,11},{10,... | collective-permute-start | bytes 1572872 | tf_op jit(solution)/shard_map/ppermute | solution.py:33
  86.0 37.1 %collective-permute-start.2 = (bf16[2,512,256]{2,1,0:T(8,128)(2,1)}, bf16[2,512,256]{2,1,0:T(8,128)(2,1)S(1)}, u32[]{:S(2)}, u32[]{:S(2)}) collective-permute-start(bf16[2,512,256]{2,1,0:T(8,128)(2,1)} %collective-permute-done.z), channel_id=1, source_target_pairs={{0,1},{1,0},{2,3},{3,2},{4,5},{5,4},{6,7},{7,6},{8,9},{9,8},{10,11... | collective-permute-start | bytes 1572872 | tf_op jit(solution)/shard_map/ppermute | solution.py:33
  97.2 61.1 %copy-start.4 = (bf16[2,512,256]{2,1,0:T(8,128)(2,1)}, bf16[2,512,256]{2,1,0:T(8,128)(2,1)S(1)}, u32[]{:S(2)}) copy-start(bf16[2,512,256]{2,1,0:T(8,128)(2,1)S(1)} %collective-permute-done.22.z) | copy-start | bytes 1572868
  97.2 24.4 %collective-permute-start.40 = (f32[64,1024]{1,0:T(8,128)S(1)}, f32[64,1024]{1,0:T(8,128)S(1)}, u32[]{:S(2)}, u32[]{:S(2)}) collective-permute-start(f32[64,1024]{1,0:T(8,128)S(1)} %fusion), channel_id=1, source_target_pairs={{0,1},{1,0},{2,3},{3,2},{4,5},{5,4},{6,7},{7,6},{8,9},{9,8},{10,11... | collective-permute-start | bytes 786440 | tf_op jit(solution)/shard_map/ppermute | solution.py:33
  101.9 46.5 %copy-start.41 = (bf16[1,512,256]{2,1,0:T(8,128)(2,1)S(1)}, bf16[1,512,256]{2,1,0:T(8,128)(2,1)}, u32[]{:S(2)}) copy-start(bf16[1,512,256]{2,1,0:T(8,128)(2,1)} %get-tuple-element.18) | copy-start | bytes 786436
  101.9 46.5 %copy-start.43 = (bf16[1,512,256]{2,1,0:T(8,128)(2,1)S(1)}, bf16[1,512,256]{2,1,0:T(8,128)(2,1)}, u32[]{:S(2)}) copy-start(bf16[1,512,256]{2,1,0:T(8,128)(2,1)} %get-tuple-element.10) | copy-start | bytes 786436
  108.4 40.3 %copy-start.8 = (bf16[2,512,256]{2,1,0:T(8,128)(2,1)}, bf16[2,512,256]{2,1,0:T(8,128)(2,1)S(1)}, u32[]{:S(2)}) copy-start(bf16[2,512,256]{2,1,0:T(8,128)(2,1)S(1)} %collective-permute-done.26.z) | copy-start | bytes 1572868
  108.4 15.9 %collective-permute-start.7 = (bf16[2,512,256]{2,1,0:T(8,128)(2,1)S(1)}, bf16[2,512,256]{2,1,0:T(8,128)(2,1)}, u32[]{:S(2)}, u32[]{:S(2)}) collective-permute-start(bf16[2,512,256]{2,1,0:T(8,128)(2,1)S(1)} %broadcast_select_fusion.6), channel_id=1, source_target_pairs={{0,2},{1,3},{2,0},{3,1},{4,6},{5,7},{6,4},{7,5},{8,10},{9,11},{10,... | collective-permute-start | bytes 1572872 | tf_op jit(solution)/shard_map/ppermute | solution.py:33
  109.8 39.0 %copy-start.38 = (bf16[1,512,256]{2,1,0:T(8,128)(2,1)S(1)}, bf16[1,512,256]{2,1,0:T(8,128)(2,1)}, u32[]{:S(2)}) copy-start(bf16[1,512,256]{2,1,0:T(8,128)(2,1)} %get-tuple-element.17) | copy-start | bytes 786436
  109.8 39.0 %copy-start.39 = (bf16[1,512,256]{2,1,0:T(8,128)(2,1)S(1)}, bf16[1,512,256]{2,1,0:T(8,128)(2,1)}, u32[]{:S(2)}) copy-start(bf16[1,512,256]{2,1,0:T(8,128)(2,1)} %get-tuple-element.9) | copy-start | bytes 786436
  119.8 40.1 %copy-start.6 = (bf16[2,512,256]{2,1,0:T(8,128)(2,1)}, bf16[2,512,256]{2,1,0:T(8,128)(2,1)S(1)}, u32[]{:S(2)}) copy-start(bf16[2,512,256]{2,1,0:T(8,128)(2,1)S(1)} %collective-permute-done.30.z) | copy-start | bytes 1572868
  119.8 5.0 %collective-permute-start.8 = (bf16[2,512,256]{2,1,0:T(8,128)(2,1)}, bf16[2,512,256]{2,1,0:T(8,128)(2,1)S(1)}, u32[]{:S(2)}, u32[]{:S(2)}) collective-permute-start(bf16[2,512,256]{2,1,0:T(8,128)(2,1)} %collective-permute-done.6.z), channel_id=1, source_target_pairs={{0,1},{1,0},{2,3},{3,2},{4,5},{5,4},{6,7},{7,6},{8,9},{9,8},{10,11... | collective-permute-start | bytes 1572872 | tf_op jit(solution)/shard_map/ppermute | solution.py:33
  122.4 13.6 %collective-permute-start.11 = (bf16[2,512,256]{2,1,0:T(8,128)(2,1)S(1)}, bf16[2,512,256]{2,1,0:T(8,128)(2,1)}, u32[]{:S(2)}, u32[]{:S(2)}) collective-permute-start(bf16[2,512,256]{2,1,0:T(8,128)(2,1)S(1)} %broadcast_select_fusion.5), channel_id=1, source_target_pairs={{0,2},{1,3},{2,0},{3,1},{4,6},{5,7},{6,4},{7,5},{8,10},{9,11},{10,... | collective-permute-start | bytes 1572872 | tf_op jit(solution)/shard_map/ppermute | solution.py:33
  122.7 37.2 %copy-start.36 = (bf16[1,512,256]{2,1,0:T(8,128)(2,1)S(1)}, bf16[1,512,256]{2,1,0:T(8,128)(2,1)}, u32[]{:S(2)}) copy-start(bf16[1,512,256]{2,1,0:T(8,128)(2,1)} %get-tuple-element.16) | copy-start | bytes 786436
  122.7 37.2 %copy-start.37 = (bf16[1,512,256]{2,1,0:T(8,128)(2,1)S(1)}, bf16[1,512,256]{2,1,0:T(8,128)(2,1)}, u32[]{:S(2)}) copy-start(bf16[1,512,256]{2,1,0:T(8,128)(2,1)} %get-tuple-element.8) | copy-start | bytes 786436
  122.7 14.6 %collective-permute-start.12 = (bf16[2,512,256]{2,1,0:T(8,128)(2,1)}, bf16[2,512,256]{2,1,0:T(8,128)(2,1)S(1)}, u32[]{:S(2)}, u32[]{:S(2)}) collective-permute-start(bf16[2,512,256]{2,1,0:T(8,128)(2,1)} %collective-permute-done.10.z), channel_id=1, source_target_pairs={{0,1},{1,0},{2,3},{3,2},{4,5},{5,4},{6,7},{7,6},{8,9},{9,8},{10,11... | collective-permute-start | bytes 1572872 | tf_op jit(solution)/shard_map/ppermute | solution.py:33
  123.1 24.0 %collective-permute-start.15 = (bf16[2,512,256]{2,1,0:T(8,128)(2,1)S(1)}, bf16[2,512,256]{2,1,0:T(8,128)(2,1)S(1)}, u32[]{:S(2)}, u32[]{:S(2)}) collective-permute-start(bf16[2,512,256]{2,1,0:T(8,128)(2,1)S(1)} %broadcast_select_fusion.4), channel_id=1, source_target_pairs={{0,2},{1,3},{2,0},{3,1},{4,6},{5,7},{6,4},{7,5},{8,10},{9,11},{10,... | collective-permute-start | bytes 1572872 | tf_op jit(solution)/shard_map/ppermute | solution.py:33
  124.4 24.1 %collective-permute-start.16 = (bf16[2,512,256]{2,1,0:T(8,128)(2,1)S(1)}, bf16[2,512,256]{2,1,0:T(8,128)(2,1)S(1)}, u32[]{:S(2)}, u32[]{:S(2)}) collective-permute-start(bf16[2,512,256]{2,1,0:T(8,128)(2,1)S(1)} %collective-permute-done.14.z), channel_id=1, source_target_pairs={{0,1},{1,0},{2,3},{3,2},{4,5},{5,4},{6,7},{7,6},{8,9},{9,8},{10,11... | collective-permute-start | bytes 1572872 | tf_op jit(solution)/shard_map/ppermute | solution.py:33
  124.8 70.4 %collective-permute-start.4 = (bf16[512,2048]{1,0:T(8,128)(2,1)S(1)}, bf16[512,2048]{1,0:T(8,128)(2,1)}, u32[]{:S(2)}, u32[]{:S(2)}) collective-permute-start(bf16[512,2048]{1,0:T(8,128)(2,1)S(1)} %copy-done), channel_id=1, source_target_pairs={{0,1},{1,0},{2,3},{3,2},{4,5},{5,4},{6,7},{7,6},{8,9},{9,8},{10,11... | collective-permute-start | bytes 6291464 | tf_op jit(solution)/shard_map/ppermute | solution.py:33
  136.0 59.4 %collective-permute-start.5 = (bf16[512,2048]{1,0:T(8,128)(2,1)}, bf16[512,2048]{1,0:T(8,128)(2,1)}, u32[]{:S(2)}, u32[]{:S(2)}) collective-permute-start(bf16[512,2048]{1,0:T(8,128)(2,1)} %v.15), channel_id=1, source_target_pairs={{0,1},{1,0},{2,3},{3,2},{4,5},{5,4},{6,7},{7,6},{8,9},{9,8},{10,11... | collective-permute-start | bytes 6291464 | tf_op jit(solution)/shard_map/ppermute | solution.py:33
  137.3 21.0 %collective-permute-start.19 = (bf16[2,512,256]{2,1,0:T(8,128)(2,1)S(1)}, bf16[2,512,256]{2,1,0:T(8,128)(2,1)S(1)}, u32[]{:S(2)}, u32[]{:S(2)}) collective-permute-start(bf16[2,512,256]{2,1,0:T(8,128)(2,1)S(1)} %broadcast_select_fusion.3), channel_id=1, source_target_pairs={{0,2},{1,3},{2,0},{3,1},{4,6},{5,7},{6,4},{7,5},{8,10},{9,11},{10,... | collective-permute-start | bytes 1572872 | tf_op jit(solution)/shard_map/ppermute | solution.py:33
  147.1 12.5 %collective-permute-start.20 = (bf16[2,512,256]{2,1,0:T(8,128)(2,1)S(1)}, bf16[2,512,256]{2,1,0:T(8,128)(2,1)S(1)}, u32[]{:S(2)}, u32[]{:S(2)}) collective-permute-start(bf16[2,512,256]{2,1,0:T(8,128)(2,1)S(1)} %collective-permute-done.18.z), channel_id=1, source_target_pairs={{0,1},{1,0},{2,3},{3,2},{4,5},{5,4},{6,7},{7,6},{8,9},{9,8},{10,11... | collective-permute-start | bytes 1572872 | tf_op jit(solution)/shard_map/ppermute | solution.py:33
  148.5 21.1 %collective-permute-start.23 = (bf16[2,512,256]{2,1,0:T(8,128)(2,1)S(1)}, bf16[2,512,256]{2,1,0:T(8,128)(2,1)S(1)}, u32[]{:S(2)}, u32[]{:S(2)}) collective-permute-start(bf16[2,512,256]{2,1,0:T(8,128)(2,1)S(1)} %broadcast_select_fusion.2), channel_id=1, source_target_pairs={{0,2},{1,3},{2,0},{3,1},{4,6},{5,7},{6,4},{7,5},{8,10},{9,11},{10,... | collective-permute-start | bytes 1572872 | tf_op jit(solution)/shard_map/ppermute | solution.py:33
  148.9 46.9 %copy-start.33 = (f32[512,32]{1,0:T(8,128)S(1)}, f32[512,32]{1,0:T(8,128)}, u32[]{:S(2)}) copy-start(f32[512,32]{1,0:T(8,128)} %copy-done.32) | copy-start | bytes 196612
  158.3 11.5 %collective-permute-start.24 = (bf16[2,512,256]{2,1,0:T(8,128)(2,1)S(1)}, bf16[2,512,256]{2,1,0:T(8,128)(2,1)S(1)}, u32[]{:S(2)}, u32[]{:S(2)}) collective-permute-start(bf16[2,512,256]{2,1,0:T(8,128)(2,1)S(1)} %collective-permute-done.22.z), channel_id=1, source_target_pairs={{0,1},{1,0},{2,3},{3,2},{4,5},{5,4},{6,7},{7,6},{8,9},{9,8},{10,11... | collective-permute-start | bytes 1572872 | tf_op jit(solution)/shard_map/ppermute | solution.py:33
  159.6 21.2 %collective-permute-start.27 = (bf16[2,512,256]{2,1,0:T(8,128)(2,1)S(1)}, bf16[2,512,256]{2,1,0:T(8,128)(2,1)S(1)}, u32[]{:S(2)}, u32[]{:S(2)}) collective-permute-start(bf16[2,512,256]{2,1,0:T(8,128)(2,1)S(1)} %broadcast_select_fusion.1), channel_id=1, source_target_pairs={{0,2},{1,3},{2,0},{3,1},{4,6},{5,7},{6,4},{7,5},{8,10},{9,11},{10,... | collective-permute-start | bytes 1572872 | tf_op jit(solution)/shard_map/ppermute | solution.py:33
  169.6 22.6 %collective-permute-start.31 = (bf16[2,512,256]{2,1,0:T(8,128)(2,1)S(1)}, bf16[2,512,256]{2,1,0:T(8,128)(2,1)}, u32[]{:S(2)}, u32[]{:S(2)}) collective-permute-start(bf16[2,512,256]{2,1,0:T(8,128)(2,1)S(1)} %broadcast_select_fusion), channel_id=1, source_target_pairs={{0,2},{1,3},{2,0},{3,1},{4,6},{5,7},{6,4},{7,5},{8,10},{9,11},{10,... | collective-permute-start | bytes 1572872 | tf_op jit(solution)/shard_map/ppermute | solution.py:33
  170.6 22.5 %collective-permute-start.3 = (bf16[2,512,256]{2,1,0:T(8,128)(2,1)}, bf16[2,512,256]{2,1,0:T(8,128)(2,1)}, u32[]{:S(2)}, u32[]{:S(2)}) collective-permute-start(bf16[2,512,256]{2,1,0:T(8,128)(2,1)} %collective-permute-done.1.d), channel_id=1, source_target_pairs={{0,1},{1,0},{2,3},{3,2},{4,5},{5,4},{6,7},{7,6},{8,9},{9,8},{10,11... | collective-permute-start | bytes 1572872 | tf_op jit(solution)/shard_map/ppermute | solution.py:33
  180.8 12.3 %collective-permute-start.9 = (bf16[2,512,256]{2,1,0:T(8,128)(2,1)}, bf16[2,512,256]{2,1,0:T(8,128)(2,1)}, u32[]{:S(2)}, u32[]{:S(2)}) collective-permute-start(bf16[2,512,256]{2,1,0:T(8,128)(2,1)} %collective-permute-done.7.d), channel_id=1, source_target_pairs={{0,1},{1,0},{2,3},{3,2},{4,5},{5,4},{6,7},{7,6},{8,9},{9,8},{10,11... | collective-permute-start | bytes 1572872 | tf_op jit(solution)/shard_map/ppermute | solution.py:33
  192.2 2.7 %collective-permute-start.13 = (bf16[2,512,256]{2,1,0:T(8,128)(2,1)}, bf16[2,512,256]{2,1,0:T(8,128)(2,1)}, u32[]{:S(2)}, u32[]{:S(2)}) collective-permute-start(bf16[2,512,256]{2,1,0:T(8,128)(2,1)} %collective-permute-done.11.d), channel_id=1, source_target_pairs={{0,1},{1,0},{2,3},{3,2},{4,5},{5,4},{6,7},{7,6},{8,9},{9,8},{10,11... | collective-permute-start | bytes 1572872 | tf_op jit(solution)/shard_map/ppermute | solution.py:33
  193.1 28.9 %collective-permute-start.17 = (bf16[2,512,256]{2,1,0:T(8,128)(2,1)}, bf16[2,512,256]{2,1,0:T(8,128)(2,1)S(1)}, u32[]{:S(2)}, u32[]{:S(2)}) collective-permute-start(bf16[2,512,256]{2,1,0:T(8,128)(2,1)} %copy-done.14), channel_id=1, source_target_pairs={{0,1},{1,0},{2,3},{3,2},{4,5},{5,4},{6,7},{7,6},{8,9},{9,8},{10,11... | collective-permute-start | bytes 1572872 | tf_op jit(solution)/shard_map/ppermute | solution.py:33
  193.1 29.1 %collective-permute-start.21 = (bf16[2,512,256]{2,1,0:T(8,128)(2,1)}, bf16[2,512,256]{2,1,0:T(8,128)(2,1)S(1)}, u32[]{:S(2)}, u32[]{:S(2)}) collective-permute-start(bf16[2,512,256]{2,1,0:T(8,128)(2,1)} %copy-done.22), channel_id=1, source_target_pairs={{0,1},{1,0},{2,3},{3,2},{4,5},{5,4},{6,7},{7,6},{8,9},{9,8},{10,11... | collective-permute-start | bytes 1572872 | tf_op jit(solution)/shard_map/ppermute | solution.py:33
  194.9 48.3 %collective-permute-start.28 = (bf16[2,512,256]{2,1,0:T(8,128)(2,1)}, bf16[2,512,256]{2,1,0:T(8,128)(2,1)S(1)}, u32[]{:S(2)}, u32[]{:S(2)}) collective-permute-start(bf16[2,512,256]{2,1,0:T(8,128)(2,1)} %copy-done.8), channel_id=1, source_target_pairs={{0,1},{1,0},{2,3},{3,2},{4,5},{5,4},{6,7},{7,6},{8,9},{9,8},{10,11... | collective-permute-start | bytes 1572872 | tf_op jit(solution)/shard_map/ppermute | solution.py:33
  195.2 41.1 %collective-permute-start.25 = (bf16[2,512,256]{2,1,0:T(8,128)(2,1)}, bf16[2,512,256]{2,1,0:T(8,128)(2,1)S(1)}, u32[]{:S(2)}, u32[]{:S(2)}) collective-permute-start(bf16[2,512,256]{2,1,0:T(8,128)(2,1)} %copy-done.26), channel_id=1, source_target_pairs={{0,1},{1,0},{2,3},{3,2},{4,5},{5,4},{6,7},{7,6},{8,9},{9,8},{10,11... | collective-permute-start | bytes 1572872 | tf_op jit(solution)/shard_map/ppermute | solution.py:33
  195.4 47.8 %collective-permute-start.29 = (bf16[2,512,256]{2,1,0:T(8,128)(2,1)}, bf16[2,512,256]{2,1,0:T(8,128)(2,1)S(1)}, u32[]{:S(2)}, u32[]{:S(2)}) collective-permute-start(bf16[2,512,256]{2,1,0:T(8,128)(2,1)} %copy-done.28), channel_id=1, source_target_pairs={{0,1},{1,0},{2,3},{3,2},{4,5},{5,4},{6,7},{7,6},{8,9},{9,8},{10,11... | collective-permute-start | bytes 1572872 | tf_op jit(solution)/shard_map/ppermute | solution.py:33
  222.0 28.3 %collective-permute-start.32 = (bf16[2,512,256]{2,1,0:T(8,128)(2,1)S(1)}, bf16[2,512,256]{2,1,0:T(8,128)(2,1)S(1)}, u32[]{:S(2)}, u32[]{:S(2)}) collective-permute-start(bf16[2,512,256]{2,1,0:T(8,128)(2,1)S(1)} %copy-done.7), channel_id=1, source_target_pairs={{0,1},{1,0},{2,3},{3,2},{4,5},{5,4},{6,7},{7,6},{8,9},{9,8},{10,11... | collective-permute-start | bytes 1572872 | tf_op jit(solution)/shard_map/ppermute | solution.py:33
  222.2 28.1 %collective-permute-start.33 = (bf16[2,512,256]{2,1,0:T(8,128)(2,1)}, bf16[2,512,256]{2,1,0:T(8,128)(2,1)S(1)}, u32[]{:S(2)}, u32[]{:S(2)}) collective-permute-start(bf16[2,512,256]{2,1,0:T(8,128)(2,1)} %collective-permute-done.31.d), channel_id=1, source_target_pairs={{0,1},{1,0},{2,3},{3,2},{4,5},{5,4},{6,7},{7,6},{8,9},{9,8},{10,11... | collective-permute-start | bytes 1572872 | tf_op jit(solution)/shard_map/ppermute | solution.py:33
  (48 other events, 435.1 us)

commit v2 on v1

v2 whole, which is shorter than its diff:
```python
import functools

import jax
import jax.numpy as jnp
from jax import lax
from jax.experimental import pallas as pl
from jax.experimental.pallas import tpu as pltpu
from jax.sharding import PartitionSpec as P

TOK_DEV = 512
WINDOW = 2048
AH = 16
HD = 128
SCAN_HEADS = 32
P_SIZE = 64
N = 64
GROUP = WINDOW // TOK_DEV
SUB = 128
CHUNKS = (3, 3, 3, 3, 2, 2)
NEG = -1e30
EXP_SCALE = HD ** (-0.5) * 1.4426950408889634
F32 = jnp.float32
BF16 = jnp.bfloat16


def cyclic(array, by):
    count = lax.axis_size("ctx")
    return lax.ppermute(array, "ctx", [(i, (i + by) % count) for i in range(count)])


def swapped(array, bit):
    count = lax.axis_size("ctx")
    return lax.ppermute(array, "ctx", [(i, i ^ bit) for i in range(count)])


def dot_t(a, b):
    return lax.dot_general(a, b, (((1,), (1,)), ((), ())), preferred_element_type=F32)


def dot_v(a, b):
    return lax.dot_general(a, b, (((0,), (0,)), ((), ())), preferred_element_type=F32)


def dot_f32(a, b):
    return jnp.dot(a, b, preferred_element_type=F32)


def attend_kernel(flags, q, k, v, z, d, e, g, xk, xv, *rest):
    out, near = rest[-2:]
    odd, later, full = flags[0], flags[1], flags[2]
    half = TOK_DEV // 2

    @pl.when(odd == 1)
    def _():
        near[0] = xk[...]
        near[1] = xv[...]

    @pl.when(odd == 0)
    def _():
        near[...] = e[...]

    def body(masked):
        q_all = q[...]
        q_lo, q_hi = q[:half, :], q[half:, :]
        key = lax.broadcasted_iota(jnp.int32, (half, half), 0)
        query = lax.broadcasted_iota(jnp.int32, (half, half), 1)
        causal = key <= query
        k_lo, k_hi = k[:half, :], k[half:, :]
        z_lo, z_hi = z[0, :half, :], z[0, half:, :]
        before_lo, before_hi = dot_t(z_lo, q_lo), dot_t(z_hi, q_hi)
        s10 = dot_t(z_hi, q_lo)
        s2, s3, s4 = dot_t(d[0], q_all), dot_t(near[0], q_all), dot_t(g[0], q_all)
        if masked:
            before_lo, before_hi = jnp.full_like(before_lo, NEG), jnp.full_like(before_hi, NEG)
            s10 = jnp.full_like(s10, NEG)
            bias_d = jnp.where(later == 1, 0.0, NEG)
            bias_e = jnp.where(odd == 1, 0.0, NEG)
            s2, s3, s4 = s2 + bias_d, s3 + bias_e, s4 + bias_d
        s00 = jnp.where(causal, dot_t(k_lo, q_lo), before_lo)
        s01 = dot_t(k_lo, q_hi)
        s11 = jnp.where(causal, dot_t(k_hi, q_hi), before_hi)
        most = lambda s: jnp.max(s, axis=0, keepdims=True)
        tri = jnp.concatenate(
            [jnp.maximum(most(s00), most(s10)), jnp.maximum(most(s01), most(s11))], axis=1
        )
        top = jnp.maximum(jnp.maximum(tri, most(s2)), jnp.maximum(most(s3), most(s4)))
        top = top * EXP_SCALE
        t_lo, t_hi = top[:, :half], top[:, half:]
        p00, p10 = jnp.exp2(s00 * EXP_SCALE - t_lo), jnp.exp2(s10 * EXP_SCALE - t_lo)
        p01, p11 = jnp.exp2(s01 * EXP_SCALE - t_hi), jnp.exp2(s11 * EXP_SCALE - t_hi)
        add = lambda p: jnp.sum(p, axis=0, keepdims=True)
        total = jnp.concatenate([add(p00) + add(p10), add(p01) + add(p11)], axis=1)
        mine = lambda p: jnp.where(causal, p, 0.0).astype(BF16)
        theirs = lambda p: jnp.where(causal, 0.0, p).astype(BF16)
        v_lo, v_hi = v[:half, :], v[half:, :]
        w_lo, w_hi = z[1, :half, :], z[1, half:, :]
        acc_lo = dot_v(v_lo, mine(p00)) + dot_v(w_lo, theirs(p00)) + dot_v(w_hi, p10.astype(BF16))
        acc_hi = dot_v(v_hi, mine(p11)) + dot_v(w_hi, theirs(p11)) + dot_v(v_lo, p01.astype(BF16))
        acc = jnp.concatenate([acc_lo, acc_hi], axis=1)
        for s, block in ((s2, d), (s3, near), (s4, g)):
            prob = jnp.exp2(s * EXP_SCALE - top)
            total = total + add(prob)
            acc = acc + dot_v(block[1], prob.astype(BF16))
        out[...] = jnp.transpose(acc / total).astype(BF16)

    @pl.when(full == 1)
    def _():
        body(False)

    @pl.when(full == 0)
    def _():
        body(True)


def attend(flags, low, heads, queries, keys, values, z, d, e, g, xk, xv, sofar):
    wide = pl.BlockSpec((TOK_DEV, HD), lambda j, f: (0, low + j))
    pair = pl.BlockSpec((2, TOK_DEV, HD), lambda j, f: (0, 0, j))
    left = pl.BlockSpec(memory_space=pl.ANY)
    return pl.pallas_call(
        attend_kernel,
        name="attend",
        out_shape=jax.ShapeDtypeStruct((TOK_DEV, AH * HD), BF16),
        grid_spec=pltpu.PrefetchScalarGridSpec(
            num_scalar_prefetch=1,
            grid=(heads,),
            in_specs=[wide, wide, wide, pair, pair, pair, pair, wide, wide] + [left] * len(sofar),
            out_specs=wide,
            scratch_shapes=[pltpu.VMEM((2, TOK_DEV, HD), BF16)],
        ),
        input_output_aliases={10: 0} if sofar else {},
        compiler_params=pltpu.CompilerParams(vmem_limit_bytes=32 << 20),
    )(flags, queries, keys, values, z, d, e, g, xk, xv, *sofar)


def packed(low, heads, keys, values):
    cols = slice(low * HD, (low + heads) * HD)
    return jnp.stack([keys[:, cols], values[:, cols]])


def split3(a):
    hi = a.astype(BF16)
    rest = a - hi.astype(F32)
    mid = rest.astype(BF16)
    low = (rest - mid.astype(F32)).astype(BF16)
    return hi, mid, low


def split2(a):
    hi = a.astype(BF16)
    return hi, (a - hi.astype(F32)).astype(BF16)


def pick(head, width):
    row = lax.broadcasted_iota(jnp.int32, (3 * SCAN_HEADS, width), 0) % SCAN_HEADS
    return (row == head).astype(BF16)


PAIRS = 2


def local_kernel(base, x, decay_t, b_t, c_t, skip, part, state, cum_out, cums, cum_t, cross, b, c):
    step = pl.program_id(0)
    lane = lax.broadcasted_iota(jnp.int32, (SUB, SUB), 1)
    lower = lax.broadcasted_iota(jnp.int32, (SUB, SUB), 0) >= lane
    left = lane < P_SIZE

    @pl.when(step == 0)
    def _():
        t = lax.broadcasted_iota(jnp.int32, (TOK_DEV, TOK_DEV), 0)
        u = lax.broadcasted_iota(jnp.int32, (TOK_DEV, TOK_DEV), 1)
        until = (t <= u).astype(BF16)
        hi, mid, low = split3(decay_t[...])
        total = dot_f32(hi, until) + dot_f32(mid, until) + dot_f32(low, until)
        cum_t[...] = total
        total = jnp.transpose(total)
        cum_out[...] = total
        hi, mid, low = split3(total)
        cums[:, 0:32] = hi
        cums[:, 32:64] = mid
        cums[:, 64:96] = low
        b[...] = jnp.transpose(b_t[...].astype(F32)).astype(BF16)
        c[...] = jnp.transpose(c_t[...].astype(F32)).astype(BF16)
        for s in range(TOK_DEV // SUB):
            at = pl.ds(s * SUB, SUB)
            cross[at, :] = jnp.where(lower, dot_t(c[at, :], b[at, :]), 0.0)

    for pair in range(PAIRS):
        first = 2 * (step * PAIRS + pair) + base
        cols = slice(pair * SUB, (pair + 1) * SUB)
        cum_a = dot_f32(cums[...], pick(first, SUB))
        cum_b = dot_f32(cums[...], pick(first + 1, SUB))
        row_a = cum_t[pl.ds(first, 1), :]
        row_b = cum_t[pl.ds(first + 1, 1), :]
        carry = jnp.zeros((N, SUB), F32)
        before = jnp.zeros((1, SUB), F32)
        for s in range(TOK_DEV // SUB):
            at = slice(s * SUB, (s + 1) * SUB)
            col_a, col_b = cum_a[at, :], cum_b[at, :]
            both = jnp.where(left, col_a, col_b)
            xf = x[at, cols].astype(F32)
            inner = cross[at, :]
            gap_a = jnp.minimum(col_a - row_a[:, at], 0.0)
            gap_b = jnp.minimum(col_b - row_b[:, at], 0.0)
            mix_a = (jnp.exp(gap_a) * inner).astype(BF16)
            mix_b = (jnp.exp(gap_b) * inner).astype(BF16)
            x_a = jnp.where(left, xf, 0.0).astype(BF16)
            x_b = jnp.where(left, 0.0, xf).astype(BF16)
            y = dot_f32(
                jnp.concatenate([mix_a, mix_b], axis=1), jnp.concatenate([x_a, x_b], axis=0)
            )
            if s > 0:
                hi, low = split2(carry)
                cs = c[at, :]
                reach = dot_f32(
                    jnp.concatenate([cs, cs], axis=1), jnp.concatenate([hi, low], axis=0)
                )
                y = y + jnp.exp(both - before) * reach
            part[at, cols] = y + skip[:, cols] * xf
            end = both[SUB - 1 : SUB, :]
            weighted = (xf * jnp.exp(end - both)).astype(BF16)
            added = dot_f32(b_t[:, at], weighted)
            carry = jnp.exp(end - before) * carry + added
            before = end
        state[0:N, cols] = carry
        state[N : N + 8, cols] = jnp.broadcast_to(before, (8, SUB))


def scan_local(half, x_in, decay_t, b_t, c_t, skip_wide):
    width = PAIRS * SUB
    lanes = SCAN_HEADS * P_SIZE // 2
    steps = lanes // width
    whole = lambda shape: pl.BlockSpec(shape, lambda j: (0, 0))
    return pl.pallas_call(
        functools.partial(local_kernel, half * SCAN_HEADS // 2),
        name="scan_local",
        out_shape=(
            jax.ShapeDtypeStruct((TOK_DEV, lanes), F32),
            jax.ShapeDtypeStruct((N + 8, lanes), F32),
            jax.ShapeDtypeStruct((TOK_DEV, SCAN_HEADS), F32),
        ),
        grid=(steps,),
        in_specs=[
            pl.BlockSpec((TOK_DEV, width), lambda j: (0, half * steps + j)),
            whole((SCAN_HEADS, TOK_DEV)),
            whole((N, TOK_DEV)),
            whole((N, TOK_DEV)),
            pl.BlockSpec((1, width), lambda j: (0, half * steps + j)),
        ],
        out_specs=(
            pl.BlockSpec((TOK_DEV, width), lambda j: (0, j)),
            pl.BlockSpec((N + 8, width), lambda j: (0, j)),
            whole((TOK_DEV, SCAN_HEADS)),
        ),
        scratch_shapes=[
            pltpu.VMEM((TOK_DEV, 3 * SCAN_HEADS), BF16),
            pltpu.VMEM((SCAN_HEADS, TOK_DEV), F32),
            pltpu.VMEM((TOK_DEV, SUB), F32),
            pltpu.VMEM((TOK_DEV, N), BF16),
            pltpu.VMEM((TOK_DEV, N), BF16),
        ],
        compiler_params=pltpu.CompilerParams(vmem_limit_bytes=32 << 20),
    )(x_in, decay_t, b_t, c_t, skip_wide)


def finish_kernel(part_a, part_b, cum, c_t, carried, out):
    step = pl.program_id(0)
    part = jnp.where(step < 2, part_a[...], part_b[...])
    width = out.shape[1]
    hi, mid, low = split3(cum[...])
    row = lax.broadcasted_iota(jnp.int32, (3 * SCAN_HEADS, width), 0) % SCAN_HEADS
    lane = lax.broadcasted_iota(jnp.int32, (3 * SCAN_HEADS, width), 1) // P_SIZE
    chosen = (row == lane + step * (width // P_SIZE)).astype(BF16)
    wide = dot_f32(jnp.concatenate([hi, mid, low], axis=1), chosen)
    hi, low = split2(carried[...])
    cs = c_t[...]
    reach = dot_v(jnp.concatenate([cs, cs], axis=0), jnp.concatenate([hi, low], axis=0))
    out[...] = (part + jnp.exp(wide) * reach).astype(BF16)


def scan_finish(part_a, part_b, cum, c_t, carried):
    width = 512
    whole = lambda shape: pl.BlockSpec(shape, lambda j: (0, 0))
    column = lambda rows: pl.BlockSpec((rows, width), lambda j: (0, j))
    return pl.pallas_call(
        finish_kernel,
        name="scan_finish",
        out_shape=jax.ShapeDtypeStruct((TOK_DEV, SCAN_HEADS * P_SIZE), BF16),
        grid=(SCAN_HEADS * P_SIZE // width,),
        in_specs=[
            pl.BlockSpec((TOK_DEV, width), lambda j: (0, jnp.minimum(j, 1))),
            pl.BlockSpec((TOK_DEV, width), lambda j: (0, jnp.maximum(j - 2, 0))),
            whole((TOK_DEV, SCAN_HEADS)),
            whole((N, TOK_DEV)),
            column(N),
        ],
        out_specs=column(TOK_DEV),
        compiler_params=pltpu.CompilerParams(vmem_limit_bytes=32 << 20),
    )(part_a, part_b, cum, c_t, carried)


def joined(earlier, following):
    total = earlier[N:] + following[N:]
    state = jnp.exp(following[N : N + 1]) * earlier[:N] + following[:N]
    return jnp.concatenate([state, total], axis=0)


def after(value, *others):
    return lax.optimization_barrier((value,) + others)[0]


class Carry:
    def __init__(self, state_a, state_b, core, side, plane):
        self.core, self.side, self.plane = core, side, plane
        self.mine = jnp.where(core == 0, state_a, state_b)
        self.other = swapped(jnp.where(core == 0, state_b, state_a), 1)
        self.steps = [self.chip, self.across, self.back, self.spread]

    def advance(self, *others):
        if self.steps:
            self.mine = after(self.mine, *others)
            self.other = after(self.other, *others)
            self.steps.pop(0)()

    def chip(self):
        core, side, quarter = self.core, self.side, self.mine.shape[1] // 2
        self.first = jnp.where(core == 0, self.mine, self.other)
        second = jnp.where(core == 0, self.other, self.mine)
        chip = joined(self.first, second)
        self.mine = jnp.where(side == 0, chip[:, :quarter], chip[:, quarter:])
        self.other = swapped(jnp.where(side == 0, chip[:, quarter:], chip[:, :quarter]), 2)

    def across(self):
        self.lower = jnp.where(self.side == 0, self.mine, self.other)
        upper = jnp.where(self.side == 0, self.other, self.mine)
        total = joined(self.lower, upper)
        planes = lax.axis_size("ctx") // GROUP
        self.mine = total
        if planes <= 4:
            self.other = [cyclic(total, GROUP * back) for back in range(planes - 1, 0, -1)]
        else:
            carry = jnp.where(self.plane >= 1, cyclic(total, GROUP), jnp.zeros_like(total))
            reach = 1
            while reach < planes:
                came = cyclic(carry, GROUP * reach)
                carry = jnp.where(self.plane >= reach, joined(came, carry), carry)
                reach *= 2
            self.other = carry

    def back(self):
        side = self.side
        if isinstance(self.other, list):
            carry = jnp.zeros_like(self.mine)
            for back, came in zip(range(len(self.other), 0, -1), self.other):
                carry = jnp.where(self.plane >= back, joined(carry, came), carry)
        else:
            carry = self.other
        carry = after(carry, self.mine)
        later = joined(carry, self.lower)
        self.mine = jnp.where(side == 0, carry, later)[:N]
        self.other = swapped(jnp.where(side == 0, later, carry)[:N], 2)

    def spread(self):
        core, side, mine, came = self.core, self.side, self.mine, self.other
        chip_in = jnp.concatenate(
            [jnp.where(side == 0, mine, came), jnp.where(side == 0, came, mine)], axis=1
        )
        next_in = jnp.exp(self.first[N : N + 1]) * chip_in + self.first[:N]
        self.mine = jnp.where(core == 0, chip_in, next_in)
        self.other = swapped(jnp.where(core == 0, next_in, chip_in), 1)

    def result(self):
        core, mine, came = self.core, self.mine, self.other
        return jnp.concatenate(
            [jnp.where(core == 0, mine, came), jnp.where(core == 0, came, mine)], axis=1
        )


def shards(queries, keys, values, x_in, log_decay, b_in, c_in, skip_d):
    device = lax.axis_index("ctx")
    core = device % 2
    side = (device // 2) % 2
    plane = device // GROUP
    flags = jnp.stack([core, side, jnp.where(plane > 0, 1, 0)], axis=0).astype(jnp.int32)
    groups = []
    for heads in CHUNKS:
        groups.append((sum(CHUNKS[: len(groups)]), heads))
    count = len(groups)
    own = [packed(*groups[0], keys, values)]
    for group in groups[1:]:
        own.append(packed(*group, after(keys, own[-1]), values))
    before = [cyclic(own[0], GROUP), cyclic(own[1], GROUP), cyclic(own[2], GROUP)]
    near_k, near_v = swapped(after(keys, own[1]), 1), swapped(after(values, own[1]), 1)
    skip_wide = jnp.repeat(skip_d, P_SIZE)[None, :]
    c_t = jnp.transpose(c_in)
    rest = (jnp.transpose(log_decay), jnp.transpose(b_in), c_t, skip_wide)
    part_a, state_a, cum = scan_local(0, after(x_in, own[1]), *rest)

    chosen, across, beside = {}, {}, {}

    def send(k, *others):
        came = after(before[k], *others)
        chosen[k] = jnp.where(side == 0, own[k], came)
        across[k] = swapped(chosen[k], 2)
        beside[k] = swapped(came, 1)
        if k + 3 < count:
            before.append(cyclic(after(own[k + 3], chosen[k]), GROUP))

    send(0, part_a)
    part_b, state_b, _ = scan_local(1, after(x_in, chosen[0]), *rest)
    carry = Carry(state_a, state_b, core, side, plane)
    send(1, part_b)
    out = None
    for k, (low, heads) in enumerate(groups):
        arrived = across[k]
        if k + 1 < count:
            arrived = after(arrived, chosen[k + 1])
        relayed = swapped(arrived, 1)
        if k == count - 1:
            scan_out = scan_finish(part_a, part_b, cum, c_t, after(carry.result(), out))
            relayed = after(relayed, scan_out)
        out = attend(
            flags, low, heads, queries, keys, values, before[k], arrived, beside[k],
            relayed, near_k, near_v, () if k == 0 else (out,),
        )
        if k + 2 < count:
            send(k + 2, out)
        if k in (0, 1, 3, 4):
            carry.advance(out)
    return (out, scan_out)


def solution(mesh):
    row = P(("seqs", "ctx"), None)
    in_specs = (row,) * 7 + (P(),)
    return jax.shard_map(
        shards, mesh=mesh, in_specs=in_specs, out_specs=(row, row), check_vma=False
    )
```

time: 263 us -> 167 us (0.63)
  waiting for transfers between devices: 115 us -> 29.5 us
  Pallas kernels: 72.9 us -> 61.9 us
  local copies, waits for them, and re-layouts: 16 us -> 22.3 us
  starting transfers between devices: 37.6 us -> 33.8 us
    ppermute x30 -> x24, waiting for transfers between devices: 66.3 us -> 23 us  [swapped(): return lax.ppermute(array, 'ctx', [(i, i ^ bit) for i in range(count)])]
    ppermute x11 -> x9, waiting for transfers between devices: 48.5 us -> 6.5 us  [cyclic(): lax.ppermute(array, 'ctx', [(i, (i + by) % count) for i in range(count)])]
    pallas_call x8 -> x6, Pallas kernels: 54.5 us -> 43.9 us  [attend(): pl.pallas_call(attend_kernel, name='attend', out_shape=jax.ShapeDtypeStru...]
    another operation x2 -> x7, local copies, waits for them, and re-layouts: 3.98 us -> 10.5 us  [packed(): return jnp.stack([keys[:, cols], values[:, cols]])]
    ppermute x30 -> x24, starting transfers between devices: 24.6 us -> 21.5 us  [swapped(): return lax.ppermute(array, 'ctx', [(i, i ^ bit) for i in range(count)])]
    another operation x8 -> x6, other arithmetic: 8.25 us -> 7.03 us  [packed(): return jnp.stack([keys[:, cols], values[:, cols]])]
    select_n x19 -> x17, other arithmetic: 6.86 us -> 7.67 us  [the longest x6 5.57 us: send(): chosen[k] = jnp.where(side == 0, own[k], came)]
    ppermute x11 -> x9, starting transfers between devices: 13 us -> 12.3 us  [cyclic(): lax.ppermute(array, 'ctx', [(i, (i + by) % count) for i in range(count)])]
  transfers between devices with their start and end apart: 41 -> 33, of which waited for: 16 -> 9; matrix products, arithmetic and copies ran while one was open for 6% -> 14% of each run, Pallas kernels for 26% -> 34%
where the time goes in v2:
time: 167 us; the launch traced here: 164 us
  Pallas kernels  61.9 us (37%)
  starting transfers between devices  33.8 us (20%)
  waiting for transfers between devices  29.5 us (18%)
  local copies, waits for them, and re-layouts  22.3 us (13%)
  other arithmetic  15 us (9%)
    pallas_call x6, Pallas kernels, attend(): pl.pallas_call(attend_kernel, name='attend', out_shape=jax.ShapeDtypeStru...  43.9 us
    ppermute x24, waiting for transfers between devices, swapped(): return lax.ppermute(array, 'ctx', [(i, i ^ bit) for i in range(count)])  23 us
    ppermute x24, starting transfers between devices, swapped(): return lax.ppermute(array, 'ctx', [(i, i ^ bit) for i in range(count)])  21.5 us
    pallas_call x2, Pallas kernels, scan_local(): pl.pallas_call(functools.partial(local_kernel, half * SCAN_HEADS // 2), n...  14.5 us
    ppermute x9, starting transfers between devices, cyclic(): lax.ppermute(array, 'ctx', [(i, (i + by) % count) for i in range(count)])  12.3 us
    unnamed x84, local copies, waits for them, and re-layouts  11.6 us
    another operation x7, local copies, waits for them, and re-layouts, packed(): return jnp.stack([keys[:, cols], values[:, cols]])  10.5 us
    another operation x6, other arithmetic, packed(): return jnp.stack([keys[:, cols], values[:, cols]])  7.03 us
  transfers between devices with their start and end apart: 33, of which 9 were waited for; matrix products, arithmetic and copies ran while one was open for 14% of the time, Pallas kernels for 34%

profile of v2, /device:TPU:13, one launch (start us, length us, event | category | flops | bytes accessed | tf_op | source)
XLA Modules:
  0.0 163.7 jit_solution(14876120349623137740)
XLA Ops:
  0.6 2.6 %slice_bitcast_fusion.6 = (bf16[1,512,384]{2,1,0:T(8,128)(2,1)S(1)}, bf16[1,512,384]{2,1,0:T(8,128)(2,1)}, bf16[1,512,384]{2,1,0:T(8,128)(2,1)}, bf16[1,512,384]{2,1,0:T(8,128)(2,1)S(1)}, bf16[1,512,384]{2,1,0:T(8,128)(2,1)S(1)}) fusion(bf16[512,2048]{1,0:T(8,128)(2,1)} %v.11, bf16[512,2048]{1,0:T(8,128)(2,1)} %k.11), kind=kLoop, calls=%fused_computation.19 | loop fusion | bytes 3932160 | tf_op jit(solution)/shard_map/stack | solution.py:137
  3.3 1.0 pad_maximum_fusion
  4.3 1.3 collective-permute-start.1
  5.5 1.0 slice_bitcast_fusion.5
  6.6 1.0 pad_maximum_fusion.1
  7.6 1.3 collective-permute-start.3
  8.9 1.2 collective-permute-start.6
  10.4 1.6 copy-done.4
  12.0 6.9 %scan_local.2 = (f32[512,1024]{1,0:T(8,128)S(1)}, f32[72,1024]{1,0:T(8,128)S(1)}, f32[512,32]{1,0:T(8,128)S(1)}) custom-call(bf16[512,2048]{1,0:T(8,128)(2,1)S(1)} %copy-done.4, f32[32,512]{1,0:T(8,128)S(1)} %bitcast.40, bf16[64,512]{1,0:T(8,128)(2,1)S(1)} %bitcast.42, bf16[64,512]{1,0:T(8,128)(2,1)S(1)} %bitcast.37, f32[1,2048]{1,0:T(1,128)S(1)} %broadcast_in_dim_reshape.3.skip), custom_call_target="tpu_custom_call" | custom-call | tf_op jit(solution)/shard_map/scan_local/pallas_call | solution.py:233
  18.9 1.3 copy-done.8
  20.9 2.1 %collective-permute-done.1.z = bf16[2,512,384]{2,1,0:T(8,128)(2,1)} collective-permute-done((bf16[2,512,384]{2,1,0:T(8,128)(2,1)}, bf16[2,512,384]{2,1,0:T(8,128)(2,1)}, u32[]{:S(2)}, u32[]{:S(2)}) %collective-permute-start.1) | collective-permute-done | bytes 786464 | tf_op jit(solution)/shard_map/ppermute | solution.py:28
  23.0 2.2 %broadcast_select_fusion.3 = bf16[2,512,384]{2,1,0:T(8,128)(2,1)} fusion(bf16[2,512,384]{2,1,0:T(8,128)(2,1)} %collective-permute-done.1.z, pred[]{:T(512)S(6)} %eq.7, bf16[1,512,384]{2,1,0:T(8,128)(2,1)S(1)} %copy-done.32, bf16[1,512,384]{2,1,0:T(8,128)(2,1)S(1)} %copy-done.34), kind=kLoop, calls=%fused_computation.7 | loop fusion | flops 786432 | bytes 2359297 | tf_op jit(solution)/shard_map/jit(_where)/select_n | solution.py:402
  25.1 1.8 %slice_bitcast_fusion.3 = bf16[1,512,384]{2,1,0:T(8,128)(2,1)} fusion(bf16[512,2048]{1,0:T(8,128)(2,1)} %k.11), kind=kLoop, calls=%fused_computation.16 | loop fusion | bytes 786432 | tf_op jit(solution)/shard_map/stack | solution.py:137
  26.9 2.1 %pad_maximum_fusion.2 = bf16[2,512,384]{2,1,0:T(8,128)(2,1)} fusion(bf16[1,512,384]{2,1,0:T(8,128)(2,1)} %get-tuple-element.80, bf16[1,512,384]{2,1,0:T(8,128)(2,1)} %slice_bitcast_fusion.3), kind=kLoop, calls=%fused_computation.2 | loop fusion | flops 393216 | bytes 1572864 | tf_op jit(solution)/shard_map/stack | solution.py:137
  29.1 2.7 %collective-permute-start.4 = (bf16[2,512,384]{2,1,0:T(8,128)(2,1)}, bf16[2,512,384]{2,1,0:T(8,128)(2,1)}, u32[]{:S(2)}, u32[]{:S(2)}) collective-permute-start(bf16[2,512,384]{2,1,0:T(8,128)(2,1)} %collective-permute-done.1.z), channel_id=1, source_target_pairs={{0,1},{1,0},{2,3},{3,2},{4,5},{5,4},{6,7},{7,6},{8,9},{9,8},{10,11... | collective-permute-start | bytes 2359304 | tf_op jit(solution)/shard_map/ppermute | solution.py:33
  31.8 1.0 slice_bitcast_fusion.1
  33.6 1.0 pad_maximum_fusion.3
  34.5 1.6 copy-done.5
  36.1 0.8 copy-done.16
  37.0 0.8 copy-done.18
  37.8 7.6 %scan_local.3 = (f32[512,1024]{1,0:T(8,128)S(1)}, f32[72,1024]{1,0:T(8,128)S(1)}, f32[512,32]{1,0:T(8,128)}) custom-call(bf16[512,2048]{1,0:T(8,128)(2,1)S(1)} %copy-done.5, f32[32,512]{1,0:T(8,128)S(1)} %bitcast.41, bf16[64,512]{1,0:T(8,128)(2,1)S(1)} %bitcast.43, bf16[64,512]{1,0:T(8,128)(2,1)S(1)} %bitcast.38, f32[1,2048]{1,0:T(1,128)S(1)} %broadcast_in_dim_reshape.3.skip), custom_call_target="tpu_custom_call" | custom-call | tf_op jit(solution)/shard_map/scan_local/pallas_call | solution.py:233
  45.4 1.3 copy-done.10
  46.7 1.3 collective-permute-start
  48.0 1.0 broadcast_select_fusion.2
  49.4 1.7 %slice_bitcast_fusion.11 = bf16[1,512,256]{2,1,0:T(8,128)(2,1)} fusion(bf16[512,2048]{1,0:T(8,128)(2,1)} %k.11), kind=kLoop, calls=%fused_computation.31 | loop fusion | bytes 524288 | tf_op jit(solution)/shard_map/stack | solution.py:137
  51.0 1.7 %collective-permute-start.10 = (bf16[2,512,384]{2,1,0:T(8,128)(2,1)}, bf16[2,512,384]{2,1,0:T(8,128)(2,1)}, u32[]{:S(2)}, u32[]{:S(2)}) collective-permute-start(bf16[2,512,384]{2,1,0:T(8,128)(2,1)} %broadcast_select_fusion.2), channel_id=1, source_target_pairs={{0,2},{1,3},{2,0},{3,1},{4,6},{5,7},{6,4},{7,5},{8,10},{9,11},{10,... | collective-permute-start | bytes 2359304 | tf_op jit(solution)/shard_map/ppermute | solution.py:33
  54.4 1.3 collective-permute-start.9
  55.7 7.9 %attend.6.rest_0_ = bf16[512,2048]{1,0:T(8,128)(2,1)} custom-call(s32[3]{0:T(128)S(1)} %pad_add_fusion.flags, bf16[512,2048]{1,0:T(8,128)(2,1)S(1)} %copy-done.1, bf16[512,2048]{1,0:T(8,128)(2,1)} %k.11, bf16[512,2048]{1,0:T(8,128)(2,1)S(1)} %copy-done, bf16[2,512,384]{2,1,0:T(8,128)(2,1)} %collective-permute-done.1.z, ...), custom_call_target="tpu_custom_call" | custom-call | tf_op jit(solution)/shard_map/attend/pallas_call | solution.py:119
  63.6 3.3 %collective-permute-done.z = bf16[2,512,384]{2,1,0:T(8,128)(2,1)} collective-permute-done((bf16[2,512,384]{2,1,0:T(8,128)(2,1)}, bf16[2,512,384]{2,1,0:T(8,128)(2,1)}, u32[]{:S(2)}, u32[]{:S(2)}) %collective-permute-start) | collective-permute-done | bytes 786464 | tf_op jit(solution)/shard_map/ppermute | solution.py:28
  66.9 1.2 broadcast_select_fusion.1
  68.2 2.7 %collective-permute-done.10.d = bf16[2,512,384]{2,1,0:T(8,128)(2,1)} collective-permute-done((bf16[2,512,384]{2,1,0:T(8,128)(2,1)}, bf16[2,512,384]{2,1,0:T(8,128)(2,1)}, u32[]{:S(2)}, u32[]{:S(2)}) %collective-permute-start.10) | collective-permute-done | bytes 786464 | tf_op jit(solution)/shard_map/ppermute | solution.py:33
  71.6 0.9 pad_maximum_fusion.4
  72.5 1.3 collective-permute-start.14
  73.8 1.5 collective-permute-start.15
  76.0 7.9 %attend.7.rest_0_ = bf16[512,2048]{1,0:T(8,128)(2,1)} custom-call(s32[3]{0:T(128)S(1)} %pad_add_fusion.flags, bf16[512,2048]{1,0:T(8,128)(2,1)S(1)} %copy-done.1, bf16[512,2048]{1,0:T(8,128)(2,1)} %k.11, bf16[512,2048]{1,0:T(8,128)(2,1)S(1)} %copy-done, bf16[2,512,384]{2,1,0:T(8,128)(2,1)S(1)} %collective-permute-done.3.z, ...), custom_call_target="tpu_custom_call", output_to_operand_aliasing={{}: (10, {})} | custom-call | tf_op jit(solution)/shard_map/attend/pallas_call | solution.py:119
  83.9 0.9 copy-done.6
  84.8 1.0 broadcast_select_fusion
  85.8 6.9 %collective-permute-done.15.d = bf16[2,512,384]{2,1,0:T(8,128)(2,1)} collective-permute-done((bf16[2,512,384]{2,1,0:T(8,128)(2,1)S(1)}, bf16[2,512,384]{2,1,0:T(8,128)(2,1)}, u32[]{:S(2)}, u32[]{:S(2)}) %collective-permute-start.15) | collective-permute-done | bytes 786464 | tf_op jit(solution)/shard_map/ppermute | solution.py:33
  92.7 1.1 collective-permute-start.17
  94.6 1.5 collective-permute-start.24
  96.1 1.7 %slice_bitcast_fusion.9 = bf16[1,512,256]{2,1,0:T(8,128)(2,1)} fusion(bf16[512,2048]{1,0:T(8,128)(2,1)} %k.11), kind=kLoop, calls=%fused_computation.29 | loop fusion | bytes 524288 | tf_op jit(solution)/shard_map/stack | solution.py:137
  97.7 1.1 pad_maximum_fusion.5
  98.8 1.6 collective-permute-done.24
  100.4 1.7 %collective-permute-start.8 = (bf16[2,512,256]{2,1,0:T(8,128)(2,1)S(1)}, bf16[2,512,256]{2,1,0:T(8,128)(2,1)S(1)}, u32[]{:S(2)}, u32[]{:S(2)}) collective-permute-start(bf16[2,512,256]{2,1,0:T(8,128)(2,1)S(1)} %pad_maximum_fusion.5), channel_id=1, source_target_pairs={{0,4},{1,5},{2,6},{3,7},{4,8},{5,9},{6,10},{7,11},{8,12},{9,13},{1... | collective-permute-start | bytes 1572872 | tf_op jit(solution)/shard_map/ppermute | solution.py:28
  102.1 1.1 broadcast_select_fusion.12
  103.2 1.5 collective-permute-start.18
  104.7 1.6 copy-done.2
  106.3 7.9 %attend.8.rest_0_ = bf16[512,2048]{1,0:T(8,128)(2,1)} custom-call(s32[3]{0:T(128)S(1)} %pad_add_fusion.flags, bf16[512,2048]{1,0:T(8,128)(2,1)S(1)} %copy-done.2, bf16[512,2048]{1,0:T(8,128)(2,1)} %k.11, bf16[512,2048]{1,0:T(8,128)(2,1)S(1)} %copy-done, bf16[2,512,384]{2,1,0:T(8,128)(2,1)} %collective-permute-done.z, ...), custom_call_target="tpu_custom_call", output_to_operand_aliasing={{}: (10, {})} | custom-call | tf_op jit(solution)/shard_map/attend/pallas_call | solution.py:119
  114.4 2.9 %collective-permute-done.13.d = bf16[2,512,384]{2,1,0:T(8,128)(2,1)} collective-permute-done((bf16[2,512,384]{2,1,0:T(8,128)(2,1)}, bf16[2,512,384]{2,1,0:T(8,128)(2,1)}, u32[]{:S(2)}, u32[]{:S(2)}) %collective-permute-start.13) | collective-permute-done | bytes 786464 | tf_op jit(solution)/shard_map/ppermute | solution.py:33
  117.2 0.8 collective-permute-start.19
  118.3 2.7 %collective-permute-start.26 = (f32[72,512]{1,0:T(8,128)S(1)}, f32[72,512]{1,0:T(8,128)S(1)}, u32[]{:S(2)}, u32[]{:S(2)}) collective-permute-start(f32[72,512]{1,0:T(8,128)S(1)} %pad_maximum_fusion.9), channel_id=1, source_target_pairs={{0,8},{1,9},{2,10},{3,11},{4,12},{5,13},{6,14},{7,15},{8,0},{9,1},... | collective-permute-start | bytes 442376 | tf_op jit(solution)/shard_map/ppermute | solution.py:28
  121.1 1.1 collective-permute-start.27
  122.2 1.2 collective-permute-start.28
  123.5 8.2 %attend.9.rest_0_ = bf16[512,2048]{1,0:T(8,128)(2,1)} custom-call(s32[3]{0:T(128)S(1)} %pad_add_fusion.flags, bf16[512,2048]{1,0:T(8,128)(2,1)S(1)} %copy-done.2, bf16[512,2048]{1,0:T(8,128)(2,1)} %k.11, bf16[512,2048]{1,0:T(8,128)(2,1)S(1)} %copy-done, bf16[2,512,384]{2,1,0:T(8,128)(2,1)S(1)} %copy-done.7, ...), custom_call_target="tpu_custom_call", output_to_operand_aliasing={{}: (10, {})} | custom-call | tf_op jit(solution)/shard_map/attend/pallas_call | solution.py:119
  131.6 1.1 collective-permute-start.29
  132.7 1.1 collective-permute-done.27
  134.0 0.8 collective-permute-done.28.d
  134.8 1.7 %collective-permute-start.30 = (bf16[2,512,256]{2,1,0:T(8,128)(2,1)S(1)}, bf16[2,512,256]{2,1,0:T(8,128)(2,1)S(1)}, u32[]{:S(2)}, u32[]{:S(2)}) collective-permute-start(bf16[2,512,256]{2,1,0:T(8,128)(2,1)S(1)} %collective-permute-done.28.d), channel_id=1, source_target_pairs={{0,1},{1,0},{2,3},{3,2},{4,5},{5,4},{6,7},{7,6},{8,9},{9,8},{10,11... | collective-permute-start | bytes 1572872 | tf_op jit(solution)/shard_map/ppermute | solution.py:33
  136.8 1.3 collective-permute-start.31
  138.4 6.0 %attend.10.rest_0_ = bf16[512,2048]{1,0:T(8,128)(2,1)} custom-call(s32[3]{0:T(128)S(1)} %pad_add_fusion.flags, bf16[512,2048]{1,0:T(8,128)(2,1)S(1)} %copy-done.2, bf16[512,2048]{1,0:T(8,128)(2,1)} %k.11, bf16[512,2048]{1,0:T(8,128)(2,1)S(1)} %copy-done, bf16[2,512,256]{2,1,0:T(8,128)(2,1)S(1)} %collective-permute-done.14.z, ...), custom_call_target="tpu_custom_call", output_to_operand_aliasing={{}: (10, {})} | custom-call | tf_op jit(solution)/shard_map/attend/pallas_call | solution.py:119
  145.1 8.1 %collective-permute-done.20.d = bf16[2,512,256]{2,1,0:T(8,128)(2,1)S(1)} collective-permute-done((bf16[2,512,256]{2,1,0:T(8,128)(2,1)S(1)}, bf16[2,512,256]{2,1,0:T(8,128)(2,1)S(1)}, u32[]{:S(2)}, u32[]{:S(2)}) %collective-permute-start.20) | collective-permute-done | bytes 524320 | tf_op jit(solution)/shard_map/ppermute | solution.py:33
  153.2 0.8 collective-permute-start.22
  154.2 3.6 %scan_finish.1 = bf16[512,2048]{1,0:T(8,128)(2,1)} custom-call(f32[512,1024]{1,0:T(8,128)S(1)} %copy-done.9, f32[512,1024]{1,0:T(8,128)S(1)} %copy-done.11, f32[512,32]{1,0:T(8,128)S(1)} %copy-done.14, bf16[64,512]{1,0:T(8,128)(2,1)S(1)} %bitcast.39, f32[64,2048]{1,0:T(8,128)S(1)} %pad_maximum_fusion.6.carried), custom_call_target="tpu_custom_call" | custom-call | tf_op jit(solution)/shard_map/scan_finish/pallas_call | solution.py:284
  157.8 6.0 %attend.11 = bf16[512,2048]{1,0:T(8,128)(2,1)} custom-call(s32[3]{0:T(128)S(1)} %pad_add_fusion.flags, bf16[512,2048]{1,0:T(8,128)(2,1)S(1)} %copy-done.3, bf16[512,2048]{1,0:T(8,128)(2,1)} %k.11, bf16[512,2048]{1,0:T(8,128)(2,1)S(1)} %copy-done, bf16[2,512,256]{2,1,0:T(8,128)(2,1)S(1)} %collective-permute-done.8.z, ...), custom_call_target="tpu_custom_call", output_to_operand_aliasing={{}: (10, {})} | custom-call | tf_op jit(solution)/shard_map/attend/pallas_call | solution.py:119
  (149 shorter events, 7.7 us)
Async XLA Ops:
  3.2 6.9 %copy-start.29 = (bf16[1,512,384]{2,1,0:T(8,128)(2,1)}, bf16[1,512,384]{2,1,0:T(8,128)(2,1)S(1)}, u32[]{:S(2)}) copy-start(bf16[1,512,384]{2,1,0:T(8,128)(2,1)S(1)} %get-tuple-element.81) | copy-start | bytes 1179652
  3.2 7.0 %copy-start.31 = (bf16[1,512,384]{2,1,0:T(8,128)(2,1)}, bf16[1,512,384]{2,1,0:T(8,128)(2,1)S(1)}, u32[]{:S(2)}) copy-start(bf16[1,512,384]{2,1,0:T(8,128)(2,1)S(1)} %get-tuple-element.78) | copy-start | bytes 1179652
  3.2 7.0 %copy-start.33 = (bf16[1,512,384]{2,1,0:T(8,128)(2,1)}, bf16[1,512,384]{2,1,0:T(8,128)(2,1)S(1)}, u32[]{:S(2)}) copy-start(bf16[1,512,384]{2,1,0:T(8,128)(2,1)S(1)} %get-tuple-element.98) | copy-start | bytes 1179652
  3.2 6.9 %copy-start = (bf16[512,2048]{1,0:T(8,128)(2,1)S(1)}, bf16[512,2048]{1,0:T(8,128)(2,1)}, u32[]{:S(2)}) copy-start(bf16[512,2048]{1,0:T(8,128)(2,1)} %v.11) | copy-start | bytes 6291460
  3.2 7.0 %copy-start.41 = (f32[32]{0:T(128)S(1)}, f32[32]{0:T(128)}, u32[]{:S(2)}) copy-start(f32[32]{0:T(128)} %param.15) | copy-start | bytes 388
  3.2 7.1 %copy-start.12 = (bf16[512,64]{0,1:T(8,128)(2,1)S(1)}, bf16[512,64]{0,1:T(8,128)(2,1)}, u32[]{:S(2)}) copy-start(bf16[512,64]{0,1:T(8,128)(2,1)} %param.14) | copy-start | bytes 196612
  3.2 7.1 %copy-start.15 = (f32[512,32]{0,1:T(8,128)S(1)}, f32[512,32]{0,1:T(8,128)}, u32[]{:S(2)}) copy-start(f32[512,32]{0,1:T(8,128)} %param.12) | copy-start | bytes 196612
  3.3 7.1 %copy-start.17 = (bf16[512,64]{0,1:T(8,128)(2,1)S(1)}, bf16[512,64]{0,1:T(8,128)(2,1)}, u32[]{:S(2)}) copy-start(bf16[512,64]{0,1:T(8,128)(2,1)} %param.13) | copy-start | bytes 196612
  4.3 18.7 %collective-permute-start.1 = (bf16[2,512,384]{2,1,0:T(8,128)(2,1)}, bf16[2,512,384]{2,1,0:T(8,128)(2,1)}, u32[]{:S(2)}, u32[]{:S(2)}) collective-permute-start(bf16[2,512,384]{2,1,0:T(8,128)(2,1)} %pad_maximum_fusion), channel_id=1, source_target_pairs={{0,4},{1,5},{2,6},{3,7},{4,8},{5,9},{6,10},{7,11},{8,12},{9,13},{1... | collective-permute-start | bytes 2359304 | tf_op jit(solution)/shard_map/ppermute | solution.py:28
  7.6 39.1 %collective-permute-start.3 = (bf16[2,512,384]{2,1,0:T(8,128)(2,1)}, bf16[2,512,384]{2,1,0:T(8,128)(2,1)S(1)}, u32[]{:S(2)}, u32[]{:S(2)}) collective-permute-start(bf16[2,512,384]{2,1,0:T(8,128)(2,1)} %pad_maximum_fusion.1), channel_id=1, source_target_pairs={{0,4},{1,5},{2,6},{3,7},{4,8},{5,9},{6,10},{7,11},{8,12},{9,13},{1... | collective-permute-start | bytes 2359304 | tf_op jit(solution)/shard_map/ppermute | solution.py:28
  8.9 44.8 %collective-permute-start.6 = (bf16[512,2048]{1,0:T(8,128)(2,1)}, bf16[512,2048]{1,0:T(8,128)(2,1)}, u32[]{:S(2)}, u32[]{:S(2)}) collective-permute-start(bf16[512,2048]{1,0:T(8,128)(2,1)} %k.11), channel_id=1, source_target_pairs={{0,1},{1,0},{2,3},{3,2},{4,5},{5,4},{6,7},{7,6},{8,9},{9,8},{10,11... | collective-permute-start | bytes 6291464 | tf_op jit(solution)/shard_map/ppermute | solution.py:33
  10.1 44.1 %collective-permute-start.7 = (bf16[512,2048]{1,0:T(8,128)(2,1)S(1)}, bf16[512,2048]{1,0:T(8,128)(2,1)}, u32[]{:S(2)}, u32[]{:S(2)}) collective-permute-start(bf16[512,2048]{1,0:T(8,128)(2,1)S(1)} %copy-done), channel_id=1, source_target_pairs={{0,1},{1,0},{2,3},{3,2},{4,5},{5,4},{6,7},{7,6},{8,9},{9,8},{10,11... | collective-permute-start | bytes 6291464 | tf_op jit(solution)/shard_map/ppermute | solution.py:33
  12.0 11.0 %copy-start.32 = (bf16[1,512,384]{2,1,0:T(8,128)(2,1)S(1)}, bf16[1,512,384]{2,1,0:T(8,128)(2,1)}, u32[]{:S(2)}) copy-start(bf16[1,512,384]{2,1,0:T(8,128)(2,1)} %copy-done.31) | copy-start | bytes 1179652
  12.0 11.0 %copy-start.34 = (bf16[1,512,384]{2,1,0:T(8,128)(2,1)S(1)}, bf16[1,512,384]{2,1,0:T(8,128)(2,1)}, u32[]{:S(2)}) copy-start(bf16[1,512,384]{2,1,0:T(8,128)(2,1)} %copy-done.33) | copy-start | bytes 1179652
  25.1 23.9 %collective-permute-start.2 = (bf16[2,512,384]{2,1,0:T(8,128)(2,1)}, bf16[2,512,384]{2,1,0:T(8,128)(2,1)}, u32[]{:S(2)}, u32[]{:S(2)}) collective-permute-start(bf16[2,512,384]{2,1,0:T(8,128)(2,1)} %broadcast_select_fusion.3), channel_id=1, source_target_pairs={{0,2},{1,3},{2,0},{3,1},{4,6},{5,7},{6,4},{7,5},{8,10},{9,11},{10,... | collective-permute-start | bytes 2359304 | tf_op jit(solution)/shard_map/ppermute | solution.py:33
  26.9 6.7 %copy-start.26 = (bf16[1,512,384]{2,1,0:T(8,128)(2,1)S(1)}, bf16[1,512,384]{2,1,0:T(8,128)(2,1)}, u32[]{:S(2)}) copy-start(bf16[1,512,384]{2,1,0:T(8,128)(2,1)} %get-tuple-element.79) | copy-start | bytes 1179652
  29.1 22.0 %collective-permute-start.4 = (bf16[2,512,384]{2,1,0:T(8,128)(2,1)}, bf16[2,512,384]{2,1,0:T(8,128)(2,1)}, u32[]{:S(2)}, u32[]{:S(2)}) collective-permute-start(bf16[2,512,384]{2,1,0:T(8,128)(2,1)} %collective-permute-done.1.z), channel_id=1, source_target_pairs={{0,1},{1,0},{2,3},{3,2},{4,5},{5,4},{6,7},{7,6},{8,9},{9,8},{10,11... | collective-permute-start | bytes 2359304 | tf_op jit(solution)/shard_map/ppermute | solution.py:33
  37.8 10.2 %copy-start.22 = (bf16[1,512,384]{2,1,0:T(8,128)(2,1)S(1)}, bf16[1,512,384]{2,1,0:T(8,128)(2,1)}, u32[]{:S(2)}) copy-start(bf16[1,512,384]{2,1,0:T(8,128)(2,1)} %copy-done.21) | copy-start | bytes 1179652
  37.8 10.2 %copy-start.30 = (bf16[1,512,384]{2,1,0:T(8,128)(2,1)S(1)}, bf16[1,512,384]{2,1,0:T(8,128)(2,1)}, u32[]{:S(2)}) copy-start(bf16[1,512,384]{2,1,0:T(8,128)(2,1)} %copy-done.29) | copy-start | bytes 1179652
  46.7 20.2 %collective-permute-start = (bf16[2,512,384]{2,1,0:T(8,128)(2,1)}, bf16[2,512,384]{2,1,0:T(8,128)(2,1)}, u32[]{:S(2)}, u32[]{:S(2)}) collective-permute-start(bf16[2,512,384]{2,1,0:T(8,128)(2,1)} %pad_maximum_fusion.2), channel_id=1, source_target_pairs={{0,4},{1,5},{2,6},{3,7},{4,8},{5,9},{6,10},{7,11},{8,12},{9,13},{1... | collective-permute-start | bytes 2359304 | tf_op jit(solution)/shard_map/ppermute | solution.py:28
  49.1 5.3 %collective-permute-start.5 = (bf16[2,512,384]{2,1,0:T(8,128)(2,1)}, bf16[2,512,384]{2,1,0:T(8,128)(2,1)}, u32[]{:S(2)}, u32[]{:S(2)}) collective-permute-start(bf16[2,512,384]{2,1,0:T(8,128)(2,1)} %collective-permute-done.2.d), channel_id=1, source_target_pairs={{0,1},{1,0},{2,3},{3,2},{4,5},{5,4},{6,7},{7,6},{8,9},{9,8},{10,11... | collective-permute-start | bytes 2359304 | tf_op jit(solution)/shard_map/ppermute | solution.py:33
  51.0 19.8 %collective-permute-start.10 = (bf16[2,512,384]{2,1,0:T(8,128)(2,1)}, bf16[2,512,384]{2,1,0:T(8,128)(2,1)}, u32[]{:S(2)}, u32[]{:S(2)}) collective-permute-start(bf16[2,512,384]{2,1,0:T(8,128)(2,1)} %broadcast_select_fusion.2), channel_id=1, source_target_pairs={{0,2},{1,3},{2,0},{3,1},{4,6},{5,7},{6,4},{7,5},{8,10},{9,11},{10,... | collective-permute-start | bytes 2359304 | tf_op jit(solution)/shard_map/ppermute | solution.py:33
  52.9 2.8 %copy-start.1 = (bf16[512,2048]{1,0:T(8,128)(2,1)S(1)}, bf16[512,2048]{1,0:T(8,128)(2,1)}, u32[]{:S(2)}) copy-start(bf16[512,2048]{1,0:T(8,128)(2,1)} %q.11) | copy-start | bytes 6291460
  53.6 18.0 %copy-start.39 = (bf16[1,512,256]{2,1,0:T(8,128)(2,1)}, bf16[1,512,256]{2,1,0:T(8,128)(2,1)S(1)}, u32[]{:S(2)}) copy-start(bf16[1,512,256]{2,1,0:T(8,128)(2,1)S(1)} %get-tuple-element.82) | copy-start | bytes 786436
  53.7 21.7 %collective-permute-start.11 = (bf16[2,512,384]{2,1,0:T(8,128)(2,1)S(1)}, bf16[2,512,384]{2,1,0:T(8,128)(2,1)S(1)}, u32[]{:S(2)}, u32[]{:S(2)}) collective-permute-start(bf16[2,512,384]{2,1,0:T(8,128)(2,1)S(1)} %collective-permute-done.3.z), channel_id=1, source_target_pairs={{0,1},{1,0},{2,3},{3,2},{4,5},{5,4},{6,7},{7,6},{8,9},{9,8},{10,11... | collective-permute-start | bytes 2359304 | tf_op jit(solution)/shard_map/ppermute | solution.py:33
  54.3 12.7 %copy-start.25 = (bf16[1,512,384]{2,1,0:T(8,128)(2,1)S(1)}, bf16[1,512,384]{2,1,0:T(8,128)(2,1)}, u32[]{:S(2)}) copy-start(bf16[1,512,384]{2,1,0:T(8,128)(2,1)} %slice_bitcast_fusion.3) | copy-start | bytes 1179652
  54.3 12.7 %copy-start.28 = (bf16[1,512,384]{2,1,0:T(8,128)(2,1)S(1)}, bf16[1,512,384]{2,1,0:T(8,128)(2,1)}, u32[]{:S(2)}) copy-start(bf16[1,512,384]{2,1,0:T(8,128)(2,1)} %get-tuple-element.80) | copy-start | bytes 1179652
  54.3 19.5 %collective-permute-start.23 = (f32[72,1024]{1,0:T(8,128)S(1)}, f32[72,1024]{1,0:T(8,128)S(1)}, u32[]{:S(2)}, u32[]{:S(2)}) collective-permute-start(f32[72,1024]{1,0:T(8,128)S(1)} %get-tuple-element.88), channel_id=1, source_target_pairs={{0,1},{1,0},{2,3},{3,2},{4,5},{5,4},{6,7},{7,6},{8,9},{9,8},{10,11... | collective-permute-start | bytes 884744 | tf_op jit(solution)/shard_map/ppermute | solution.py:33
  54.4 29.6 %collective-permute-start.9 = (bf16[2,512,384]{2,1,0:T(8,128)(2,1)}, bf16[2,512,384]{2,1,0:T(8,128)(2,1)S(1)}, u32[]{:S(2)}, u32[]{:S(2)}) collective-permute-start(bf16[2,512,384]{2,1,0:T(8,128)(2,1)} %pad_maximum_fusion.3), channel_id=1, source_target_pairs={{0,4},{1,5},{2,6},{3,7},{4,8},{5,9},{6,10},{7,11},{8,12},{9,13},{1... | collective-permute-start | bytes 2359304 | tf_op jit(solution)/shard_map/ppermute | solution.py:28
  63.6 8.0 %copy-start.35 = (bf16[1,512,256]{2,1,0:T(8,128)(2,1)S(1)}, bf16[1,512,256]{2,1,0:T(8,128)(2,1)}, u32[]{:S(2)}) copy-start(bf16[1,512,256]{2,1,0:T(8,128)(2,1)} %slice_bitcast_fusion.11) | copy-start | bytes 786436
  70.9 5.1 %collective-permute-start.12 = (bf16[2,512,384]{2,1,0:T(8,128)(2,1)}, bf16[2,512,384]{2,1,0:T(8,128)(2,1)S(1)}, u32[]{:S(2)}, u32[]{:S(2)}) collective-permute-start(bf16[2,512,384]{2,1,0:T(8,128)(2,1)} %collective-permute-done.10.d), channel_id=1, source_target_pairs={{0,1},{1,0},{2,3},{3,2},{4,5},{5,4},{6,7},{7,6},{8,9},{9,8},{10,11... | collective-permute-start | bytes 2359304 | tf_op jit(solution)/shard_map/ppermute | solution.py:33
  72.5 41.8 %collective-permute-start.14 = (bf16[2,512,256]{2,1,0:T(8,128)(2,1)}, bf16[2,512,256]{2,1,0:T(8,128)(2,1)S(1)}, u32[]{:S(2)}, u32[]{:S(2)}) collective-permute-start(bf16[2,512,256]{2,1,0:T(8,128)(2,1)} %pad_maximum_fusion.4), channel_id=1, source_target_pairs={{0,4},{1,5},{2,6},{3,7},{4,8},{5,9},{6,10},{7,11},{8,12},{9,13},{1... | collective-permute-start | bytes 1572872 | tf_op jit(solution)/shard_map/ppermute | solution.py:28
  73.8 19.0 %collective-permute-start.15 = (bf16[2,512,384]{2,1,0:T(8,128)(2,1)S(1)}, bf16[2,512,384]{2,1,0:T(8,128)(2,1)}, u32[]{:S(2)}, u32[]{:S(2)}) collective-permute-start(bf16[2,512,384]{2,1,0:T(8,128)(2,1)S(1)} %broadcast_select_fusion.1), channel_id=1, source_target_pairs={{0,2},{1,3},{2,0},{3,1},{4,6},{5,7},{6,4},{7,5},{8,10},{9,11},{10,... | collective-permute-start | bytes 2359304 | tf_op jit(solution)/shard_map/ppermute | solution.py:33
  75.3 18.5 %copy-start.19 = (f32[72,1024]{1,0:T(8,128)}, f32[72,1024]{1,0:T(8,128)S(1)}, u32[]{:S(2)}) copy-start(f32[72,1024]{1,0:T(8,128)S(1)} %get-tuple-element.87) | copy-start | bytes 884740
  75.3 9.5 %copy-start.24 = (bf16[1,512,384]{2,1,0:T(8,128)(2,1)S(1)}, bf16[1,512,384]{2,1,0:T(8,128)(2,1)}, u32[]{:S(2)}) copy-start(bf16[1,512,384]{2,1,0:T(8,128)(2,1)} %copy-done.23) | copy-start | bytes 1179652
  75.4 9.5 %copy-start.27 = (bf16[1,512,384]{2,1,0:T(8,128)(2,1)S(1)}, bf16[1,512,384]{2,1,0:T(8,128)(2,1)}, u32[]{:S(2)}) copy-start(bf16[1,512,384]{2,1,0:T(8,128)(2,1)} %get-tuple-element.79) | copy-start | bytes 1179652
  75.4 27.8 %collective-permute-start.16 = (bf16[2,512,384]{2,1,0:T(8,128)(2,1)}, bf16[2,512,384]{2,1,0:T(8,128)(2,1)}, u32[]{:S(2)}, u32[]{:S(2)}) collective-permute-start(bf16[2,512,384]{2,1,0:T(8,128)(2,1)} %collective-permute-done.z), channel_id=1, source_target_pairs={{0,1},{1,0},{2,3},{3,2},{4,5},{5,4},{6,7},{7,6},{8,9},{9,8},{10,11... | collective-permute-start | bytes 2359304 | tf_op jit(solution)/shard_map/ppermute | solution.py:33
  85.8 17.4 %copy-start.7 = (bf16[2,512,384]{2,1,0:T(8,128)(2,1)S(1)}, bf16[2,512,384]{2,1,0:T(8,128)(2,1)}, u32[]{:S(2)}) copy-start(bf16[2,512,384]{2,1,0:T(8,128)(2,1)} %copy-done.6) | copy-start | bytes 2359300
  92.7 12.0 %collective-permute-start.17 = (bf16[2,512,384]{2,1,0:T(8,128)(2,1)}, bf16[2,512,384]{2,1,0:T(8,128)(2,1)}, u32[]{:S(2)}, u32[]{:S(2)}) collective-permute-start(bf16[2,512,384]{2,1,0:T(8,128)(2,1)} %collective-permute-done.15.d), channel_id=1, source_target_pairs={{0,1},{1,0},{2,3},{3,2},{4,5},{5,4},{6,7},{7,6},{8,9},{9,8},{10,11... | collective-permute-start | bytes 2359304 | tf_op jit(solution)/shard_map/ppermute | solution.py:33
  94.6 5.8 %collective-permute-start.24 = (f32[72,512]{1,0:T(8,128)}, f32[72,512]{1,0:T(8,128)}, u32[]{:S(2)}, u32[]{:S(2)}) collective-permute-start(f32[72,512]{1,0:T(8,128)} %get-tuple-element.95), channel_id=1, source_target_pairs={{0,2},{1,3},{2,0},{3,1},{4,6},{5,7},{6,4},{7,5},{8,10},{9,11},{10,... | collective-permute-start | bytes 442376 | tf_op jit(solution)/shard_map/ppermute | solution.py:33
  96.0 21.2 %collective-permute-start.13 = (bf16[2,512,384]{2,1,0:T(8,128)(2,1)}, bf16[2,512,384]{2,1,0:T(8,128)(2,1)}, u32[]{:S(2)}, u32[]{:S(2)}) collective-permute-start(bf16[2,512,384]{2,1,0:T(8,128)(2,1)} %broadcast_select_fusion), channel_id=1, source_target_pairs={{0,2},{1,3},{2,0},{3,1},{4,6},{5,7},{6,4},{7,5},{8,10},{9,11},{10,... | collective-permute-start | bytes 2359304 | tf_op jit(solution)/shard_map/ppermute | solution.py:33
  100.4 31.2 %collective-permute-start.8 = (bf16[2,512,256]{2,1,0:T(8,128)(2,1)S(1)}, bf16[2,512,256]{2,1,0:T(8,128)(2,1)S(1)}, u32[]{:S(2)}, u32[]{:S(2)}) collective-permute-start(bf16[2,512,256]{2,1,0:T(8,128)(2,1)S(1)} %pad_maximum_fusion.5), channel_id=1, source_target_pairs={{0,4},{1,5},{2,6},{3,7},{4,8},{5,9},{6,10},{7,11},{8,12},{9,13},{1... | collective-permute-start | bytes 1572872 | tf_op jit(solution)/shard_map/ppermute | solution.py:28
  102.1 12.2 %copy-start.36 = (bf16[1,512,256]{2,1,0:T(8,128)(2,1)S(1)}, bf16[1,512,256]{2,1,0:T(8,128)(2,1)}, u32[]{:S(2)}) copy-start(bf16[1,512,256]{2,1,0:T(8,128)(2,1)} %slice_bitcast_fusion.11) | copy-start | bytes 786436
  102.1 12.2 %copy-start.40 = (bf16[1,512,256]{2,1,0:T(8,128)(2,1)S(1)}, bf16[1,512,256]{2,1,0:T(8,128)(2,1)}, u32[]{:S(2)}) copy-start(bf16[1,512,256]{2,1,0:T(8,128)(2,1)} %copy-done.39) | copy-start | bytes 786436
  103.2 17.9 %collective-permute-start.18 = (bf16[2,512,384]{2,1,0:T(8,128)(2,1)S(1)}, bf16[2,512,384]{2,1,0:T(8,128)(2,1)S(1)}, u32[]{:S(2)}, u32[]{:S(2)}) collective-permute-start(bf16[2,512,384]{2,1,0:T(8,128)(2,1)S(1)} %copy-done.7), channel_id=1, source_target_pairs={{0,1},{1,0},{2,3},{3,2},{4,5},{5,4},{6,7},{7,6},{8,9},{9,8},{10,11... | collective-permute-start | bytes 2359304 | tf_op jit(solution)/shard_map/ppermute | solution.py:33
  117.2 5.0 %collective-permute-start.19 = (bf16[2,512,384]{2,1,0:T(8,128)(2,1)}, bf16[2,512,384]{2,1,0:T(8,128)(2,1)S(1)}, u32[]{:S(2)}, u32[]{:S(2)}) collective-permute-start(bf16[2,512,384]{2,1,0:T(8,128)(2,1)} %collective-permute-done.13.d), channel_id=1, source_target_pairs={{0,1},{1,0},{2,3},{3,2},{4,5},{5,4},{6,7},{7,6},{8,9},{9,8},{10,11... | collective-permute-start | bytes 2359304 | tf_op jit(solution)/shard_map/ppermute | solution.py:33
  118.1 14.7 %collective-permute-start.25 = (f32[72,512]{1,0:T(8,128)S(1)}, f32[72,512]{1,0:T(8,128)S(1)}, u32[]{:S(2)}, u32[]{:S(2)}) collective-permute-start(f32[72,512]{1,0:T(8,128)S(1)} %pad_maximum_fusion.9), channel_id=1, source_target_pairs={{0,12},{1,13},{2,14},{3,15},{4,0},{5,1},{6,2},{7,3},{8,4},{9,5},{1... | collective-permute-start | bytes 442376 | tf_op jit(solution)/shard_map/ppermute | solution.py:28
  118.3 14.4 %collective-permute-start.26 = (f32[72,512]{1,0:T(8,128)S(1)}, f32[72,512]{1,0:T(8,128)S(1)}, u32[]{:S(2)}, u32[]{:S(2)}) collective-permute-start(f32[72,512]{1,0:T(8,128)S(1)} %pad_maximum_fusion.9), channel_id=1, source_target_pairs={{0,8},{1,9},{2,10},{3,11},{4,12},{5,13},{6,14},{7,15},{8,0},{9,1},... | collective-permute-start | bytes 442376 | tf_op jit(solution)/shard_map/ppermute | solution.py:28
  121.1 12.8 %collective-permute-start.27 = (f32[72,512]{1,0:T(8,128)S(1)}, f32[72,512]{1,0:T(8,128)S(1)}, u32[]{:S(2)}, u32[]{:S(2)}) collective-permute-start(f32[72,512]{1,0:T(8,128)S(1)} %pad_maximum_fusion.9), channel_id=1, source_target_pairs={{0,4},{1,5},{2,6},{3,7},{4,8},{5,9},{6,10},{7,11},{8,12},{9,13},{1... | collective-permute-start | bytes 442376 | tf_op jit(solution)/shard_map/ppermute | solution.py:28
  122.2 12.6 %collective-permute-start.28 = (bf16[2,512,256]{2,1,0:T(8,128)(2,1)S(1)}, bf16[2,512,256]{2,1,0:T(8,128)(2,1)S(1)}, u32[]{:S(2)}, u32[]{:S(2)}) collective-permute-start(bf16[2,512,256]{2,1,0:T(8,128)(2,1)S(1)} %broadcast_select_fusion.5), channel_id=1, source_target_pairs={{0,2},{1,3},{2,0},{3,1},{4,6},{5,7},{6,4},{7,5},{8,10},{9,11},{10,... | collective-permute-start | bytes 1572872 | tf_op jit(solution)/shard_map/ppermute | solution.py:33
  123.4 10.4 %copy-start.37 = (bf16[1,512,256]{2,1,0:T(8,128)(2,1)S(1)}, bf16[1,512,256]{2,1,0:T(8,128)(2,1)}, u32[]{:S(2)}) copy-start(bf16[1,512,256]{2,1,0:T(8,128)(2,1)} %slice_bitcast_fusion.9) | copy-start | bytes 786436
  123.4 10.4 %copy-start.38 = (bf16[1,512,256]{2,1,0:T(8,128)(2,1)S(1)}, bf16[1,512,256]{2,1,0:T(8,128)(2,1)}, u32[]{:S(2)}) copy-start(bf16[1,512,256]{2,1,0:T(8,128)(2,1)} %get-tuple-element.83) | copy-start | bytes 786436
  131.6 6.8 %collective-permute-start.29 = (bf16[2,512,256]{2,1,0:T(8,128)(2,1)S(1)}, bf16[2,512,256]{2,1,0:T(8,128)(2,1)S(1)}, u32[]{:S(2)}, u32[]{:S(2)}) collective-permute-start(bf16[2,512,256]{2,1,0:T(8,128)(2,1)S(1)} %collective-permute-done.14.z), channel_id=1, source_target_pairs={{0,1},{1,0},{2,3},{3,2},{4,5},{5,4},{6,7},{7,6},{8,9},{9,8},{10,11... | collective-permute-start | bytes 1572872 | tf_op jit(solution)/shard_map/ppermute | solution.py:33
  133.9 4.2 %copy-start.20 = (f32[72,1024]{1,0:T(8,128)S(1)}, f32[72,1024]{1,0:T(8,128)}, u32[]{:S(2)}) copy-start(f32[72,1024]{1,0:T(8,128)} %copy-done.19) | copy-start | bytes 884740
  134.8 3.6 %collective-permute-start.30 = (bf16[2,512,256]{2,1,0:T(8,128)(2,1)S(1)}, bf16[2,512,256]{2,1,0:T(8,128)(2,1)S(1)}, u32[]{:S(2)}, u32[]{:S(2)}) collective-permute-start(bf16[2,512,256]{2,1,0:T(8,128)(2,1)S(1)} %collective-permute-done.28.d), channel_id=1, source_target_pairs={{0,1},{1,0},{2,3},{3,2},{4,5},{5,4},{6,7},{7,6},{8,9},{9,8},{10,11... | collective-permute-start | bytes 1572872 | tf_op jit(solution)/shard_map/ppermute | solution.py:33
  136.8 7.6 %collective-permute-start.31 = (f32[64,512]{1,0:T(8,128)S(1)}, f32[64,512]{1,0:T(8,128)S(1)}, u32[]{:S(2)}, u32[]{:S(2)}) collective-permute-start(f32[64,512]{1,0:T(8,128)S(1)} %get-tuple-element.91), channel_id=1, source_target_pairs={{0,2},{1,3},{2,0},{3,1},{4,6},{5,7},{6,4},{7,5},{8,10},{9,11},{10,... | collective-permute-start | bytes 393224 | tf_op jit(solution)/shard_map/ppermute | solution.py:33
  138.1 15.1 %collective-permute-start.20 = (bf16[2,512,256]{2,1,0:T(8,128)(2,1)S(1)}, bf16[2,512,256]{2,1,0:T(8,128)(2,1)S(1)}, u32[]{:S(2)}, u32[]{:S(2)}) collective-permute-start(bf16[2,512,256]{2,1,0:T(8,128)(2,1)S(1)} %broadcast_select_fusion.4), channel_id=1, source_target_pairs={{0,2},{1,3},{2,0},{3,1},{4,6},{5,7},{6,4},{7,5},{8,10},{9,11},{10,... | collective-permute-start | bytes 1572872 | tf_op jit(solution)/shard_map/ppermute | solution.py:33
  138.4 15.7 %copy-start.11 = (f32[512,1024]{1,0:T(8,128)S(1)}, f32[512,1024]{1,0:T(8,128)}, u32[]{:S(2)}) copy-start(f32[512,1024]{1,0:T(8,128)} %copy-done.10) | copy-start | bytes 6291460
  144.4 9.7 %copy-start.9 = (f32[512,1024]{1,0:T(8,128)S(1)}, f32[512,1024]{1,0:T(8,128)}, u32[]{:S(2)}) copy-start(f32[512,1024]{1,0:T(8,128)} %copy-done.8) | copy-start | bytes 6291460
  144.4 9.8 %copy-start.14 = (f32[512,32]{1,0:T(8,128)S(1)}, f32[512,32]{1,0:T(8,128)}, u32[]{:S(2)}) copy-start(f32[512,32]{1,0:T(8,128)} %copy-done.13) | copy-start | bytes 196612
  144.5 9.5 %collective-permute-start.32 = (f32[64,1024]{1,0:T(8,128)S(1)}, f32[64,1024]{1,0:T(8,128)S(1)}, u32[]{:S(2)}, u32[]{:S(2)}) collective-permute-start(f32[64,1024]{1,0:T(8,128)S(1)} %fusion), channel_id=1, source_target_pairs={{0,1},{1,0},{2,3},{3,2},{4,5},{5,4},{6,7},{7,6},{8,9},{9,8},{10,11... | collective-permute-start | bytes 786440 | tf_op jit(solution)/shard_map/ppermute | solution.py:33
  153.2 4.5 %collective-permute-start.22 = (bf16[2,512,256]{2,1,0:T(8,128)(2,1)S(1)}, bf16[2,512,256]{2,1,0:T(8,128)(2,1)S(1)}, u32[]{:S(2)}, u32[]{:S(2)}) collective-permute-start(bf16[2,512,256]{2,1,0:T(8,128)(2,1)S(1)} %collective-permute-done.20.d), channel_id=1, source_target_pairs={{0,1},{1,0},{2,3},{3,2},{4,5},{5,4},{6,7},{7,6},{8,9},{9,8},{10,11... | collective-permute-start | bytes 1572872 | tf_op jit(solution)/shard_map/ppermute | solution.py:33
  154.0 3.7 %collective-permute-start.21 = (bf16[2,512,256]{2,1,0:T(8,128)(2,1)S(1)}, bf16[2,512,256]{2,1,0:T(8,128)(2,1)S(1)}, u32[]{:S(2)}, u32[]{:S(2)}) collective-permute-start(bf16[2,512,256]{2,1,0:T(8,128)(2,1)S(1)} %collective-permute-done.8.z), channel_id=1, source_target_pairs={{0,1},{1,0},{2,3},{3,2},{4,5},{5,4},{6,7},{7,6},{8,9},{9,8},{10,11... | collective-permute-start | bytes 1572872 | tf_op jit(solution)/shard_map/ppermute | solution.py:33
  154.2 3.6 %copy-start.3 = (bf16[512,2048]{1,0:T(8,128)(2,1)S(1)}, bf16[512,2048]{1,0:T(8,128)(2,1)}, u32[]{:S(2)}) copy-start(bf16[512,2048]{1,0:T(8,128)(2,1)} %q.11) | copy-start | bytes 6291460
  (11 other events, 13.8 us)

commit v3 on v2

--- a/solution.py
+++ b/solution.py
@@ -16,7 +16,8 @@
 N = 64
 GROUP = WINDOW // TOK_DEV
 SUB = 128
-CHUNKS = (3, 3, 3, 3, 2, 2)
+CHUNKS = (4, 4, 3, 3, 2)
+STEPS = (0, 1, 2, 3)
 NEG = -1e30
 EXP_SCALE = HD ** (-0.5) * 1.4426950408889634
 F32 = jnp.float32
@@ -424,7 +425,7 @@
         )
         if k + 2 < count:
             send(k + 2, out)
-        if k in (0, 1, 3, 4):
+        if k in STEPS:
             carry.advance(out)
     return (out, scan_out)
 

time: 167 us -> 152 us (0.910); the launches traced: 164 us -> 150 us
  local copies, waits for them, and re-layouts: 22.3 us -> 14.8 us
  other arithmetic: 15 us -> 12.4 us
  Pallas kernels: 61.9 us -> 59.6 us
    ppermute x24 -> x21, waiting for transfers between devices: 23 us -> 13.3 us  [swapped(): return lax.ppermute(array, 'ctx', [(i, i ^ bit) for i in range(count)])]
    ppermute x9 -> x8, waiting for transfers between devices: 6.5 us -> 16 us  [cyclic(): lax.ppermute(array, 'ctx', [(i, (i + by) % count) for i in range(count)])]
    another operation x7, local copies, waits for them, and re-layouts: 10.5 us -> 6.39 us  [packed(): return jnp.stack([keys[:, cols], values[:, cols]])]
    unnamed x84 -> x80, local copies, waits for them, and re-layouts: 11.6 us -> 8.16 us
    pallas_call x6 -> x5, Pallas kernels: 43.9 us -> 41.6 us  [attend(): pl.pallas_call(attend_kernel, name='attend', out_shape=jax.ShapeDtypeStru...]
    select_n x1, other arithmetic: 0.04 us -> 1.82 us  [__init__(): self.other = swapped(jnp.where(core == 0, state_b, state_a), 1)]
    select_n x6 -> x5, other arithmetic: 5.57 us -> 3.91 us  [send(): chosen[k] = jnp.where(side == 0, own[k], came)]
    another operation x6 -> x5, other arithmetic: 7.03 us -> 6.1 us  [packed(): return jnp.stack([keys[:, cols], values[:, cols]])]
  transfers between devices with their start and end apart: 33 -> 29, of which waited for: 9 -> 7; matrix products, arithmetic and copies ran while one was open for 14% -> 11% of each run, Pallas kernels for 34% -> 36%
where the time goes in v3:
time: 152 us; the launch traced here: 150 us
  Pallas kernels  59.6 us (39%)
  starting transfers between devices  33.1 us (22%)
  waiting for transfers between devices  29.3 us (19%)
  local copies, waits for them, and re-layouts  14.8 us (10%)
  other arithmetic  12.4 us (8%)
    pallas_call x5, Pallas kernels, attend(): pl.pallas_call(attend_kernel, name='attend', out_shape=jax.ShapeDtypeStru...  41.6 us
    ppermute x21, starting transfers between devices, swapped(): return lax.ppermute(array, 'ctx', [(i, i ^ bit) for i in range(count)])  20.7 us
    ppermute x8, waiting for transfers between devices, cyclic(): lax.ppermute(array, 'ctx', [(i, (i + by) % count) for i in range(count)])  16 us
    pallas_call x2, Pallas kernels, scan_local(): pl.pallas_call(functools.partial(local_kernel, half * SCAN_HEADS // 2), n...  14.5 us
    ppermute x21, waiting for transfers between devices, swapped(): return lax.ppermute(array, 'ctx', [(i, i ^ bit) for i in range(count)])  13.3 us
    ppermute x8, starting transfers between devices, cyclic(): lax.ppermute(array, 'ctx', [(i, (i + by) % count) for i in range(count)])  12.5 us
    unnamed x80, local copies, waits for them, and re-layouts  8.16 us
    another operation x7, local copies, waits for them, and re-layouts, packed(): return jnp.stack([keys[:, cols], values[:, cols]])  6.39 us
  transfers between devices with their start and end apart: 29, of which 7 were waited for; matrix products, arithmetic and copies ran while one was open for 11% of the time, Pallas kernels for 36%

profile of v3, /device:TPU:13, one launch (start us, length us, event | category | flops | bytes accessed | tf_op | source)
XLA Modules:
  0.0 150.5 jit_solution(11062229040702604855)
XLA Ops:
  0.6 1.5 slice_bitcast_fusion.2
  2.1 0.8 copy-done.22
  2.9 0.2 copy-done.24
  3.1 1.1 pad_maximum_fusion
  4.2 1.3 collective-permute-start.1
  5.5 1.1 slice_bitcast_fusion.1
  6.6 1.1 pad_maximum_fusion.1
  7.7 1.3 collective-permute-start
  9.0 1.2 collective-permute-start.7
  10.4 0.1 broadcast_in_dim_reshape.3.skip
  10.5 1.6 %copy-done.3 = bf16[512,2048]{1,0:T(8,128)(2,1)S(1)} copy-done((bf16[512,2048]{1,0:T(8,128)(2,1)S(1)}, bf16[512,2048]{1,0:T(8,128)(2,1)}, u32[]{:S(2)}) %copy-start.3) | copy-done | bytes 2097176
  12.1 0.8 copy-done.14
  12.9 0.8 copy-done.16
  13.8 6.9 %scan_local.2 = (f32[512,1024]{1,0:T(8,128)S(1)}, f32[72,1024]{1,0:T(8,128)S(1)}, f32[512,32]{1,0:T(8,128)S(1)}) custom-call(bf16[512,2048]{1,0:T(8,128)(2,1)S(1)} %copy-done.3, f32[32,512]{1,0:T(8,128)S(1)} %bitcast.36, bf16[64,512]{1,0:T(8,128)(2,1)S(1)} %bitcast.38, bf16[64,512]{1,0:T(8,128)(2,1)S(1)} %bitcast.33, f32[1,2048]{1,0:T(1,128)S(1)} %broadcast_in_dim_reshape.3.skip), custom_call_target="tpu_custom_call" | custom-call | tf_op jit(solution)/shard_map/scan_local/pallas_call | solution.py:234
  20.7 7.7 %collective-permute-done.1.z = bf16[2,512,512]{2,1,0:T(8,128)(2,1)S(1)} collective-permute-done((bf16[2,512,512]{2,1,0:T(8,128)(2,1)}, bf16[2,512,512]{2,1,0:T(8,128)(2,1)S(1)}, u32[]{:S(2)}, u32[]{:S(2)}) %collective-permute-start.1) | collective-permute-done | bytes 1048608 | tf_op jit(solution)/shard_map/ppermute | solution.py:29
  28.5 0.1 broadcast_select_fusion.1
  28.6 0.3 collective-permute-start.4
  28.9 0.1 slice_bitcast_fusion.6
  29.0 3.0 %collective-permute-start.5 = (bf16[2,512,512]{2,1,0:T(8,128)(2,1)S(1)}, bf16[2,512,512]{2,1,0:T(8,128)(2,1)S(1)}, u32[]{:S(2)}, u32[]{:S(2)}) collective-permute-start(bf16[2,512,512]{2,1,0:T(8,128)(2,1)S(1)} %collective-permute-done.1.z), channel_id=1, source_target_pairs={{0,1},{1,0},{2,3},{3,2},{4,5},{5,4},{6,7},{7,6},{8,9},{9,8},{10,11... | collective-permute-start | bytes 3145736 | tf_op jit(solution)/shard_map/ppermute | solution.py:34
  32.1 1.0 slice_bitcast_fusion.7
  33.1 1.0 pad_maximum_fusion.2
  34.1 1.0 slice_bitcast_fusion.5
  35.2 7.6 %scan_local.3 = (f32[512,1024]{1,0:T(8,128)S(1)}, f32[72,1024]{1,0:T(8,128)S(1)}, f32[512,32]{1,0:T(8,128)}) custom-call(bf16[512,2048]{1,0:T(8,128)(2,1)S(1)} %copy-done.3, f32[32,512]{1,0:T(8,128)S(1)} %bitcast.37, bf16[64,512]{1,0:T(8,128)(2,1)S(1)} %bitcast.39, bf16[64,512]{1,0:T(8,128)(2,1)S(1)} %bitcast.34, f32[1,2048]{1,0:T(1,128)S(1)} %broadcast_in_dim_reshape.3.skip), custom_call_target="tpu_custom_call" | custom-call | tf_op jit(solution)/shard_map/scan_local/pallas_call | solution.py:234
  42.8 8.2 %collective-permute-done.z = bf16[2,512,512]{2,1,0:T(8,128)(2,1)} collective-permute-done((bf16[2,512,512]{2,1,0:T(8,128)(2,1)}, bf16[2,512,512]{2,1,0:T(8,128)(2,1)}, u32[]{:S(2)}, u32[]{:S(2)}) %collective-permute-start) | collective-permute-done | bytes 1048608 | tf_op jit(solution)/shard_map/ppermute | solution.py:29
  51.0 1.3 collective-permute-start.3
  52.3 2.3 %broadcast_select_fusion = bf16[2,512,512]{2,1,0:T(8,128)(2,1)} fusion(bf16[2,512,512]{2,1,0:T(8,128)(2,1)} %collective-permute-done.z, pred[]{:T(512)S(6)} %eq.7, bf16[1,512,512]{2,1,0:T(8,128)(2,1)S(1)} %copy-done.21, bf16[1,512,512]{2,1,0:T(8,128)(2,1)S(1)} %copy-done.19), kind=kLoop, calls=%fused_computation.2 | loop fusion | flops 1048576 | bytes 3145729 | tf_op jit(solution)/shard_map/jit(_where)/select_n | solution.py:403
  54.7 1.8 %collective-permute-start.6 = (bf16[2,512,512]{2,1,0:T(8,128)(2,1)}, bf16[2,512,512]{2,1,0:T(8,128)(2,1)}, u32[]{:S(2)}, u32[]{:S(2)}) collective-permute-start(bf16[2,512,512]{2,1,0:T(8,128)(2,1)} %collective-permute-done.4.d), channel_id=1, source_target_pairs={{0,1},{1,0},{2,3},{3,2},{4,5},{5,4},{6,7},{7,6},{8,9},{9,8},{10,11... | collective-permute-start | bytes 3145736 | tf_op jit(solution)/shard_map/ppermute | solution.py:34
  56.5 0.7 slice_bitcast_fusion.8
  57.2 1.0 copy-done.8
  58.2 1.0 pad_maximum_fusion.3
  59.2 1.0 slice_bitcast_fusion.9
  60.2 1.9 %pad_maximum_fusion.4 = bf16[2,512,256]{2,1,0:T(8,128)(2,1)} fusion(bf16[1,512,256]{2,1,0:T(8,128)(2,1)} %slice_bitcast_fusion.8, bf16[1,512,256]{2,1,0:T(8,128)(2,1)S(1)} %slice_bitcast_fusion.9), kind=kLoop, calls=%fused_computation.8 | loop fusion | flops 262144 | bytes 1048576 | tf_op jit(solution)/shard_map/stack | solution.py:138
  62.1 1.8 %broadcast_select_fusion.8 = (f32[72,1024]{1,0:T(8,128)}, f32[72,1024]{1,0:T(8,128)}) fusion(f32[72,1024]{1,0:T(8,128)} %copy-done.11, f32[72,1024]{1,0:T(8,128)S(1)} %get-tuple-element.57, pred[]{:T(512)S(6)} %eq.8), kind=kLoop, calls=%fused_computation.39 | loop fusion | flops 147456 | bytes 1179649 | tf_op jit(solution)/shard_map/jit(_where)/select_n | solution.py:316
  64.0 0.5 collective-permute-start.12
  64.5 1.3 collective-permute-start.10
  65.8 1.6 %copy-done.1 = bf16[512,2048]{1,0:T(8,128)(2,1)S(1)} copy-done((bf16[512,2048]{1,0:T(8,128)(2,1)S(1)}, bf16[512,2048]{1,0:T(8,128)(2,1)}, u32[]{:S(2)}) %copy-start.1) | copy-done | bytes 2097176
  67.4 1.2 copy-done.9
  68.7 9.9 %attend.5.rest_0_ = bf16[512,2048]{1,0:T(8,128)(2,1)} custom-call(s32[3]{0:T(128)S(1)} %pad_add_fusion.flags, bf16[512,2048]{1,0:T(8,128)(2,1)S(1)} %copy-done.1, bf16[512,2048]{1,0:T(8,128)(2,1)} %k.9, bf16[512,2048]{1,0:T(8,128)(2,1)S(1)} %copy-done, bf16[2,512,512]{2,1,0:T(8,128)(2,1)S(1)} %collective-permute-done.1.z, ...), custom_call_target="tpu_custom_call" | custom-call | tf_op jit(solution)/shard_map/attend/pallas_call | solution.py:120
  78.5 2.0 %collective-permute-start.2 = (bf16[2,512,256]{2,1,0:T(8,128)(2,1)S(1)}, bf16[2,512,256]{2,1,0:T(8,128)(2,1)S(1)}, u32[]{:S(2)}, u32[]{:S(2)}) collective-permute-start(bf16[2,512,256]{2,1,0:T(8,128)(2,1)S(1)} %copy-done.38), channel_id=1, source_target_pairs={{0,4},{1,5},{2,6},{3,7},{4,8},{5,9},{6,10},{7,11},{8,12},{9,13},{1... | collective-permute-start | bytes 1572872 | tf_op jit(solution)/shard_map/ppermute | solution.py:29
  80.6 1.2 broadcast_select_fusion.3
  81.8 1.5 collective-permute-done.11.d
  83.3 0.2 collective-permute-start.9
  83.5 0.9 collective-permute-start.13
  84.6 2.2 %collective-permute-done.13.g = bf16[2,512,512]{2,1,0:T(8,128)(2,1)S(1)} collective-permute-done((bf16[2,512,512]{2,1,0:T(8,128)(2,1)}, bf16[2,512,512]{2,1,0:T(8,128)(2,1)S(1)}, u32[]{:S(2)}, u32[]{:S(2)}) %collective-permute-start.13) | collective-permute-done | bytes 1048608 | tf_op jit(solution)/shard_map/ppermute | solution.py:34
  86.9 1.5 collective-permute-start.20
  88.3 9.8 %attend.6.rest_0_ = bf16[512,2048]{1,0:T(8,128)(2,1)} custom-call(s32[3]{0:T(128)S(1)} %pad_add_fusion.flags, bf16[512,2048]{1,0:T(8,128)(2,1)S(1)} %copy-done.1, bf16[512,2048]{1,0:T(8,128)(2,1)} %k.9, bf16[512,2048]{1,0:T(8,128)(2,1)S(1)} %copy-done, bf16[2,512,512]{2,1,0:T(8,128)(2,1)} %collective-permute-done.z, ...), custom_call_target="tpu_custom_call", output_to_operand_aliasing={{}: (10, {})} | custom-call | tf_op jit(solution)/shard_map/attend/pallas_call | solution.py:120
  98.2 0.1 broadcast_select_fusion.2
  98.4 3.2 %collective-permute-done.9.d = bf16[2,512,384]{2,1,0:T(8,128)(2,1)S(1)} collective-permute-done((bf16[2,512,384]{2,1,0:T(8,128)(2,1)S(1)}, bf16[2,512,384]{2,1,0:T(8,128)(2,1)S(1)}, u32[]{:S(2)}, u32[]{:S(2)}) %collective-permute-start.9) | collective-permute-done | bytes 786464 | tf_op jit(solution)/shard_map/ppermute | solution.py:34
  101.6 2.9 %collective-permute-start.15 = (bf16[2,512,384]{2,1,0:T(8,128)(2,1)S(1)}, bf16[2,512,384]{2,1,0:T(8,128)(2,1)S(1)}, u32[]{:S(2)}, u32[]{:S(2)}) collective-permute-start(bf16[2,512,384]{2,1,0:T(8,128)(2,1)S(1)} %collective-permute-done.9.d), channel_id=1, source_target_pairs={{0,1},{1,0},{2,3},{3,2},{4,5},{5,4},{6,7},{7,6},{8,9},{9,8},{10,11... | collective-permute-start | bytes 2359304 | tf_op jit(solution)/shard_map/ppermute | solution.py:34
  104.5 0.2 collective-permute-done.20
  104.9 0.5 collective-permute-start.21
  105.4 2.4 %collective-permute-start.22 = (f32[72,512]{1,0:T(8,128)S(1)}, f32[72,512]{1,0:T(8,128)S(1)}, u32[]{:S(2)}, u32[]{:S(2)}) collective-permute-start(f32[72,512]{1,0:T(8,128)S(1)} %pad_maximum_fusion.8), channel_id=1, source_target_pairs={{0,8},{1,9},{2,10},{3,11},{4,12},{5,13},{6,14},{7,15},{8,0},{9,1},... | collective-permute-start | bytes 442376 | tf_op jit(solution)/shard_map/ppermute | solution.py:29
  107.8 2.3 %collective-permute-start.23 = (f32[72,512]{1,0:T(8,128)S(1)}, f32[72,512]{1,0:T(8,128)S(1)}, u32[]{:S(2)}, u32[]{:S(2)}) collective-permute-start(f32[72,512]{1,0:T(8,128)S(1)} %pad_maximum_fusion.8), channel_id=1, source_target_pairs={{0,4},{1,5},{2,6},{3,7},{4,8},{5,9},{6,10},{7,11},{8,12},{9,13},{1... | collective-permute-start | bytes 442376 | tf_op jit(solution)/shard_map/ppermute | solution.py:29
  110.1 7.9 %attend.7.rest_0_ = bf16[512,2048]{1,0:T(8,128)(2,1)} custom-call(s32[3]{0:T(128)S(1)} %pad_add_fusion.flags, bf16[512,2048]{1,0:T(8,128)(2,1)S(1)} %copy-done.1, bf16[512,2048]{1,0:T(8,128)(2,1)} %k.9, bf16[512,2048]{1,0:T(8,128)(2,1)S(1)} %copy-done, bf16[2,512,384]{2,1,0:T(8,128)(2,1)} %collective-permute-done.3.z, ...), custom_call_target="tpu_custom_call", output_to_operand_aliasing={{}: (10, {})} | custom-call | tf_op jit(solution)/shard_map/attend/pallas_call | solution.py:120
  118.0 3.8 %collective-permute-start.25 = (bf16[2,512,384]{2,1,0:T(8,128)(2,1)S(1)}, bf16[2,512,384]{2,1,0:T(8,128)(2,1)S(1)}, u32[]{:S(2)}, u32[]{:S(2)}) collective-permute-start(bf16[2,512,384]{2,1,0:T(8,128)(2,1)S(1)} %collective-permute-done.10.z), channel_id=1, source_target_pairs={{0,1},{1,0},{2,3},{3,2},{4,5},{5,4},{6,7},{7,6},{8,9},{9,8},{10,11... | collective-permute-start | bytes 2359304 | tf_op jit(solution)/shard_map/ppermute | solution.py:34
  122.0 1.3 collective-permute-start.26
  123.6 0.3 collective-permute-start.27
  123.8 1.3 collective-permute-start.16
  125.2 8.0 %attend.8.rest_0_ = bf16[512,2048]{1,0:T(8,128)(2,1)} custom-call(s32[3]{0:T(128)S(1)} %pad_add_fusion.flags, bf16[512,2048]{1,0:T(8,128)(2,1)S(1)} %copy-done.1, bf16[512,2048]{1,0:T(8,128)(2,1)} %k.9, bf16[512,2048]{1,0:T(8,128)(2,1)S(1)} %copy-done, bf16[2,512,384]{2,1,0:T(8,128)(2,1)S(1)} %collective-permute-done.10.z, ...), custom_call_target="tpu_custom_call", output_to_operand_aliasing={{}: (10, {})} | custom-call | tf_op jit(solution)/shard_map/attend/pallas_call | solution.py:120
  133.3 0.6 collective-permute-start.28
  133.9 6.1 %collective-permute-done.16.d = bf16[2,512,256]{2,1,0:T(8,128)(2,1)S(1)} collective-permute-done((bf16[2,512,256]{2,1,0:T(8,128)(2,1)S(1)}, bf16[2,512,256]{2,1,0:T(8,128)(2,1)S(1)}, u32[]{:S(2)}, u32[]{:S(2)}) %collective-permute-start.16) | collective-permute-done | bytes 524320 | tf_op jit(solution)/shard_map/ppermute | solution.py:34
  140.0 0.8 collective-permute-start.18
  140.9 3.6 %scan_finish.1 = bf16[512,2048]{1,0:T(8,128)(2,1)} custom-call(f32[512,1024]{1,0:T(8,128)S(1)} %copy-done.5, f32[512,1024]{1,0:T(8,128)S(1)} %copy-done.7, f32[512,32]{1,0:T(8,128)S(1)} %copy-done.13, bf16[64,512]{1,0:T(8,128)(2,1)S(1)} %bitcast.35, f32[64,2048]{1,0:T(8,128)S(1)} %pad_maximum_fusion.5.carried), custom_call_target="tpu_custom_call" | custom-call | tf_op jit(solution)/shard_map/scan_finish/pallas_call | solution.py:285
  144.5 6.0 %attend.9 = bf16[512,2048]{1,0:T(8,128)(2,1)} custom-call(s32[3]{0:T(128)S(1)} %pad_add_fusion.flags, bf16[512,2048]{1,0:T(8,128)(2,1)S(1)} %copy-done.2, bf16[512,2048]{1,0:T(8,128)(2,1)} %k.9, bf16[512,2048]{1,0:T(8,128)(2,1)S(1)} %copy-done, bf16[2,512,256]{2,1,0:T(8,128)(2,1)S(1)} %collective-permute-done.2.z, ...), custom_call_target="tpu_custom_call", output_to_operand_aliasing={{}: (10, {})} | custom-call | tf_op jit(solution)/shard_map/attend/pallas_call | solution.py:120
  (134 shorter events, 1.2 us)
Async XLA Ops:
  2.1 5.6 %copy-start.20 = (bf16[1,512,512]{2,1,0:T(8,128)(2,1)}, bf16[1,512,512]{2,1,0:T(8,128)(2,1)S(1)}, u32[]{:S(2)}) copy-start(bf16[1,512,512]{2,1,0:T(8,128)(2,1)S(1)} %get-tuple-element.71) | copy-start | bytes 1572868
  4.2 6.1 %copy-start = (bf16[512,2048]{1,0:T(8,128)(2,1)S(1)}, bf16[512,2048]{1,0:T(8,128)(2,1)}, u32[]{:S(2)}) copy-start(bf16[512,2048]{1,0:T(8,128)(2,1)} %v.9) | copy-start | bytes 6291460
  4.2 6.1 %copy-start.39 = (f32[32]{0:T(128)S(1)}, f32[32]{0:T(128)}, u32[]{:S(2)}) copy-start(f32[32]{0:T(128)} %param.15) | copy-start | bytes 388
  4.2 6.3 %copy-start.10 = (bf16[512,64]{0,1:T(8,128)(2,1)S(1)}, bf16[512,64]{0,1:T(8,128)(2,1)}, u32[]{:S(2)}) copy-start(bf16[512,64]{0,1:T(8,128)(2,1)} %param.14) | copy-start | bytes 196612
  4.2 24.2 %collective-permute-start.1 = (bf16[2,512,512]{2,1,0:T(8,128)(2,1)}, bf16[2,512,512]{2,1,0:T(8,128)(2,1)S(1)}, u32[]{:S(2)}, u32[]{:S(2)}) collective-permute-start(bf16[2,512,512]{2,1,0:T(8,128)(2,1)} %pad_maximum_fusion), channel_id=1, source_target_pairs={{0,4},{1,5},{2,6},{3,7},{4,8},{5,9},{6,10},{7,11},{8,12},{9,13},{1... | collective-permute-start | bytes 3145736 | tf_op jit(solution)/shard_map/ppermute | solution.py:29
  6.6 2.4 %copy-start.18 = (bf16[1,512,512]{2,1,0:T(8,128)(2,1)}, bf16[1,512,512]{2,1,0:T(8,128)(2,1)S(1)}, u32[]{:S(2)}) copy-start(bf16[1,512,512]{2,1,0:T(8,128)(2,1)S(1)} %slice_bitcast_fusion.1) | copy-start | bytes 1572868
  7.7 43.3 %collective-permute-start = (bf16[2,512,512]{2,1,0:T(8,128)(2,1)}, bf16[2,512,512]{2,1,0:T(8,128)(2,1)}, u32[]{:S(2)}, u32[]{:S(2)}) collective-permute-start(bf16[2,512,512]{2,1,0:T(8,128)(2,1)} %pad_maximum_fusion.1), channel_id=1, source_target_pairs={{0,4},{1,5},{2,6},{3,7},{4,8},{5,9},{6,10},{7,11},{8,12},{9,13},{1... | collective-permute-start | bytes 3145736 | tf_op jit(solution)/shard_map/ppermute | solution.py:29
  9.0 54.9 %collective-permute-start.7 = (bf16[512,2048]{1,0:T(8,128)(2,1)}, bf16[512,2048]{1,0:T(8,128)(2,1)}, u32[]{:S(2)}, u32[]{:S(2)}) collective-permute-start(bf16[512,2048]{1,0:T(8,128)(2,1)} %k.9), channel_id=1, source_target_pairs={{0,1},{1,0},{2,3},{3,2},{4,5},{5,4},{6,7},{7,6},{8,9},{9,8},{10,11... | collective-permute-start | bytes 6291464 | tf_op jit(solution)/shard_map/ppermute | solution.py:34
  10.3 53.7 %collective-permute-start.8 = (bf16[512,2048]{1,0:T(8,128)(2,1)S(1)}, bf16[512,2048]{1,0:T(8,128)(2,1)}, u32[]{:S(2)}, u32[]{:S(2)}) collective-permute-start(bf16[512,2048]{1,0:T(8,128)(2,1)S(1)} %copy-done), channel_id=1, source_target_pairs={{0,1},{1,0},{2,3},{3,2},{4,5},{5,4},{6,7},{7,6},{8,9},{9,8},{10,11... | collective-permute-start | bytes 6291464 | tf_op jit(solution)/shard_map/ppermute | solution.py:34
  10.5 1.6 %copy-start.3 = (bf16[512,2048]{1,0:T(8,128)(2,1)S(1)}, bf16[512,2048]{1,0:T(8,128)(2,1)}, u32[]{:S(2)}) copy-start(bf16[512,2048]{1,0:T(8,128)(2,1)} %x.1) | copy-start | bytes 6291460
  13.8 14.7 %copy-start.23 = (bf16[1,512,512]{2,1,0:T(8,128)(2,1)S(1)}, bf16[1,512,512]{2,1,0:T(8,128)(2,1)}, u32[]{:S(2)}) copy-start(bf16[1,512,512]{2,1,0:T(8,128)(2,1)} %copy-done.22) | copy-start | bytes 1572868
  13.8 14.7 %copy-start.25 = (bf16[1,512,512]{2,1,0:T(8,128)(2,1)S(1)}, bf16[1,512,512]{2,1,0:T(8,128)(2,1)}, u32[]{:S(2)}) copy-start(bf16[1,512,512]{2,1,0:T(8,128)(2,1)} %copy-done.24) | copy-start | bytes 1572868
  20.7 8.2 %copy-start.12 = (f32[512,32]{1,0:T(8,128)}, f32[512,32]{1,0:T(8,128)S(1)}, u32[]{:S(2)}) copy-start(f32[512,32]{1,0:T(8,128)S(1)} %get-tuple-element.55.cum) | copy-start | bytes 196612
  20.7 8.3 %copy-start.4 = (f32[512,1024]{1,0:T(8,128)}, f32[512,1024]{1,0:T(8,128)S(1)}, u32[]{:S(2)}) copy-start(f32[512,1024]{1,0:T(8,128)S(1)} %get-tuple-element.41.part_a) | copy-start | bytes 6291460
  28.6 6.6 %copy-start.15 = (f32[512,32]{0,1:T(8,128)S(1)}, f32[512,32]{0,1:T(8,128)}, u32[]{:S(2)}) copy-start(f32[512,32]{0,1:T(8,128)} %param.12) | copy-start | bytes 196612
  28.6 6.6 %copy-start.17 = (bf16[512,64]{0,1:T(8,128)(2,1)S(1)}, bf16[512,64]{0,1:T(8,128)(2,1)}, u32[]{:S(2)}) copy-start(bf16[512,64]{0,1:T(8,128)(2,1)} %param.13) | copy-start | bytes 196612
  28.6 26.1 %collective-permute-start.4 = (bf16[2,512,512]{2,1,0:T(8,128)(2,1)S(1)}, bf16[2,512,512]{2,1,0:T(8,128)(2,1)}, u32[]{:S(2)}, u32[]{:S(2)}) collective-permute-start(bf16[2,512,512]{2,1,0:T(8,128)(2,1)S(1)} %broadcast_select_fusion.1), channel_id=1, source_target_pairs={{0,2},{1,3},{2,0},{3,1},{4,6},{5,7},{6,4},{7,5},{8,10},{9,11},{10,... | collective-permute-start | bytes 3145736 | tf_op jit(solution)/shard_map/ppermute | solution.py:34
  29.0 5.1 %copy-start.30 = (bf16[1,512,384]{2,1,0:T(8,128)(2,1)}, bf16[1,512,384]{2,1,0:T(8,128)(2,1)S(1)}, u32[]{:S(2)}) copy-start(bf16[1,512,384]{2,1,0:T(8,128)(2,1)S(1)} %get-tuple-element.72) | copy-start | bytes 1179652
  29.0 29.2 %copy-start.26 = (bf16[1,512,384]{2,1,0:T(8,128)(2,1)}, bf16[1,512,384]{2,1,0:T(8,128)(2,1)S(1)}, u32[]{:S(2)}) copy-start(bf16[1,512,384]{2,1,0:T(8,128)(2,1)S(1)} %get-tuple-element.73) | copy-start | bytes 1179652
  29.0 28.2 %collective-permute-start.5 = (bf16[2,512,512]{2,1,0:T(8,128)(2,1)S(1)}, bf16[2,512,512]{2,1,0:T(8,128)(2,1)S(1)}, u32[]{:S(2)}, u32[]{:S(2)}) collective-permute-start(bf16[2,512,512]{2,1,0:T(8,128)(2,1)S(1)} %collective-permute-done.1.z), channel_id=1, source_target_pairs={{0,1},{1,0},{2,3},{3,2},{4,5},{5,4},{6,7},{7,6},{8,9},{9,8},{10,11... | collective-permute-start | bytes 3145736 | tf_op jit(solution)/shard_map/ppermute | solution.py:34
  33.1 1.0 copy-start.32
  33.1 19.2 %copy-start.19 = (bf16[1,512,512]{2,1,0:T(8,128)(2,1)S(1)}, bf16[1,512,512]{2,1,0:T(8,128)(2,1)}, u32[]{:S(2)}) copy-start(bf16[1,512,512]{2,1,0:T(8,128)(2,1)} %copy-done.18) | copy-start | bytes 1572868
  33.1 19.2 %copy-start.21 = (bf16[1,512,512]{2,1,0:T(8,128)(2,1)S(1)}, bf16[1,512,512]{2,1,0:T(8,128)(2,1)}, u32[]{:S(2)}) copy-start(bf16[1,512,512]{2,1,0:T(8,128)(2,1)} %copy-done.20) | copy-start | bytes 1572868
  35.2 23.0 %copy-start.28 = (bf16[1,512,384]{2,1,0:T(8,128)(2,1)}, bf16[1,512,384]{2,1,0:T(8,128)(2,1)S(1)}, u32[]{:S(2)}) copy-start(bf16[1,512,384]{2,1,0:T(8,128)(2,1)S(1)} %slice_bitcast_fusion.5) | copy-start | bytes 1179652
  42.8 14.4 %copy-start.6 = (f32[512,1024]{1,0:T(8,128)}, f32[512,1024]{1,0:T(8,128)S(1)}, u32[]{:S(2)}) copy-start(f32[512,1024]{1,0:T(8,128)S(1)} %get-tuple-element.44.part_b) | copy-start | bytes 6291460
  42.8 15.4 %copy-start.11 = (f32[72,1024]{1,0:T(8,128)}, f32[72,1024]{1,0:T(8,128)S(1)}, u32[]{:S(2)}) copy-start(f32[72,1024]{1,0:T(8,128)S(1)} %get-tuple-element.56) | copy-start | bytes 884740
  51.0 27.5 %collective-permute-start.3 = (bf16[2,512,384]{2,1,0:T(8,128)(2,1)}, bf16[2,512,384]{2,1,0:T(8,128)(2,1)}, u32[]{:S(2)}, u32[]{:S(2)}) collective-permute-start(bf16[2,512,384]{2,1,0:T(8,128)(2,1)} %pad_maximum_fusion.2), channel_id=1, source_target_pairs={{0,4},{1,5},{2,6},{3,7},{4,8},{5,9},{6,10},{7,11},{8,12},{9,13},{1... | collective-permute-start | bytes 2359304 | tf_op jit(solution)/shard_map/ppermute | solution.py:29
  54.7 9.9 %collective-permute-start.6 = (bf16[2,512,512]{2,1,0:T(8,128)(2,1)}, bf16[2,512,512]{2,1,0:T(8,128)(2,1)}, u32[]{:S(2)}, u32[]{:S(2)}) collective-permute-start(bf16[2,512,512]{2,1,0:T(8,128)(2,1)} %collective-permute-done.4.d), channel_id=1, source_target_pairs={{0,1},{1,0},{2,3},{3,2},{4,5},{5,4},{6,7},{7,6},{8,9},{9,8},{10,11... | collective-permute-start | bytes 3145736 | tf_op jit(solution)/shard_map/ppermute | solution.py:34
  58.2 25.1 %collective-permute-start.11 = (bf16[2,512,512]{2,1,0:T(8,128)(2,1)}, bf16[2,512,512]{2,1,0:T(8,128)(2,1)}, u32[]{:S(2)}, u32[]{:S(2)}) collective-permute-start(bf16[2,512,512]{2,1,0:T(8,128)(2,1)} %broadcast_select_fusion), channel_id=1, source_target_pairs={{0,2},{1,3},{2,0},{3,1},{4,6},{5,7},{6,4},{7,5},{8,10},{9,11},{10,... | collective-permute-start | bytes 3145736 | tf_op jit(solution)/shard_map/ppermute | solution.py:34
  60.2 3.7 %copy-start.35 = (bf16[1,512,256]{2,1,0:T(8,128)(2,1)}, bf16[1,512,256]{2,1,0:T(8,128)(2,1)S(1)}, u32[]{:S(2)}) copy-start(bf16[1,512,256]{2,1,0:T(8,128)(2,1)S(1)} %slice_bitcast_fusion.9) | copy-start | bytes 786436
  63.9 19.6 %collective-permute-start.19 = (f32[72,1024]{1,0:T(8,128)}, f32[72,1024]{1,0:T(8,128)S(1)}, u32[]{:S(2)}, u32[]{:S(2)}) collective-permute-start(f32[72,1024]{1,0:T(8,128)} %get-tuple-element.78), channel_id=1, source_target_pairs={{0,1},{1,0},{2,3},{3,2},{4,5},{5,4},{6,7},{7,6},{8,9},{9,8},{10,11... | collective-permute-start | bytes 884744 | tf_op jit(solution)/shard_map/ppermute | solution.py:34
  64.0 20.5 %collective-permute-start.12 = (bf16[2,512,512]{2,1,0:T(8,128)(2,1)}, bf16[2,512,512]{2,1,0:T(8,128)(2,1)S(1)}, u32[]{:S(2)}, u32[]{:S(2)}) collective-permute-start(bf16[2,512,512]{2,1,0:T(8,128)(2,1)} %collective-permute-done.z), channel_id=1, source_target_pairs={{0,1},{1,0},{2,3},{3,2},{4,5},{5,4},{6,7},{7,6},{8,9},{9,8},{10,11... | collective-permute-start | bytes 3145736 | tf_op jit(solution)/shard_map/ppermute | solution.py:34
  64.5 33.6 %collective-permute-start.10 = (bf16[2,512,384]{2,1,0:T(8,128)(2,1)}, bf16[2,512,384]{2,1,0:T(8,128)(2,1)S(1)}, u32[]{:S(2)}, u32[]{:S(2)}) collective-permute-start(bf16[2,512,384]{2,1,0:T(8,128)(2,1)} %pad_maximum_fusion.3), channel_id=1, source_target_pairs={{0,4},{1,5},{2,6},{3,7},{4,8},{5,9},{6,10},{7,11},{8,12},{9,13},{1... | collective-permute-start | bytes 2359304 | tf_op jit(solution)/shard_map/ppermute | solution.py:29
  65.8 1.6 %copy-start.1 = (bf16[512,2048]{1,0:T(8,128)(2,1)S(1)}, bf16[512,2048]{1,0:T(8,128)(2,1)}, u32[]{:S(2)}) copy-start(bf16[512,2048]{1,0:T(8,128)(2,1)} %q.9) | copy-start | bytes 6291460
  67.4 1.2 copy-start.9
  68.7 9.9 %copy-start.38 = (bf16[2,512,256]{2,1,0:T(8,128)(2,1)S(1)}, bf16[2,512,256]{2,1,0:T(8,128)(2,1)}, u32[]{:S(2)}) copy-start(bf16[2,512,256]{2,1,0:T(8,128)(2,1)} %pad_maximum_fusion.4) | copy-start | bytes 1572868
  68.7 11.9 %copy-start.31 = (bf16[1,512,384]{2,1,0:T(8,128)(2,1)S(1)}, bf16[1,512,384]{2,1,0:T(8,128)(2,1)}, u32[]{:S(2)}) copy-start(bf16[1,512,384]{2,1,0:T(8,128)(2,1)} %copy-done.30) | copy-start | bytes 1179652
  68.7 11.9 %copy-start.33 = (bf16[1,512,384]{2,1,0:T(8,128)(2,1)S(1)}, bf16[1,512,384]{2,1,0:T(8,128)(2,1)}, u32[]{:S(2)}) copy-start(bf16[1,512,384]{2,1,0:T(8,128)(2,1)} %copy-done.32) | copy-start | bytes 1179652
  78.5 5.9 %copy-start.37 = (f32[72,1024]{1,0:T(8,128)S(1)}, f32[72,1024]{1,0:T(8,128)}, u32[]{:S(2)}) copy-start(f32[72,1024]{1,0:T(8,128)} %get-tuple-element.59) | copy-start | bytes 884740
  78.5 39.5 %collective-permute-start.2 = (bf16[2,512,256]{2,1,0:T(8,128)(2,1)S(1)}, bf16[2,512,256]{2,1,0:T(8,128)(2,1)S(1)}, u32[]{:S(2)}, u32[]{:S(2)}) collective-permute-start(bf16[2,512,256]{2,1,0:T(8,128)(2,1)S(1)} %copy-done.38), channel_id=1, source_target_pairs={{0,4},{1,5},{2,6},{3,7},{4,8},{5,9},{6,10},{7,11},{8,12},{9,13},{1... | collective-permute-start | bytes 1572872 | tf_op jit(solution)/shard_map/ppermute | solution.py:29
  83.3 18.3 %collective-permute-start.9 = (bf16[2,512,384]{2,1,0:T(8,128)(2,1)S(1)}, bf16[2,512,384]{2,1,0:T(8,128)(2,1)S(1)}, u32[]{:S(2)}, u32[]{:S(2)}) collective-permute-start(bf16[2,512,384]{2,1,0:T(8,128)(2,1)S(1)} %broadcast_select_fusion.3), channel_id=1, source_target_pairs={{0,2},{1,3},{2,0},{3,1},{4,6},{5,7},{6,4},{7,5},{8,10},{9,11},{10,... | collective-permute-start | bytes 2359304 | tf_op jit(solution)/shard_map/ppermute | solution.py:34
  83.5 3.4 %collective-permute-start.13 = (bf16[2,512,512]{2,1,0:T(8,128)(2,1)}, bf16[2,512,512]{2,1,0:T(8,128)(2,1)S(1)}, u32[]{:S(2)}, u32[]{:S(2)}) collective-permute-start(bf16[2,512,512]{2,1,0:T(8,128)(2,1)} %collective-permute-done.11.d), channel_id=1, source_target_pairs={{0,1},{1,0},{2,3},{3,2},{4,5},{5,4},{6,7},{7,6},{8,9},{9,8},{10,11... | collective-permute-start | bytes 3145736 | tf_op jit(solution)/shard_map/ppermute | solution.py:34
  84.6 20.8 %collective-permute-start.14 = (bf16[2,512,384]{2,1,0:T(8,128)(2,1)}, bf16[2,512,384]{2,1,0:T(8,128)(2,1)S(1)}, u32[]{:S(2)}, u32[]{:S(2)}) collective-permute-start(bf16[2,512,384]{2,1,0:T(8,128)(2,1)} %collective-permute-done.3.z), channel_id=1, source_target_pairs={{0,1},{1,0},{2,3},{3,2},{4,5},{5,4},{6,7},{7,6},{8,9},{9,8},{10,11... | collective-permute-start | bytes 2359304 | tf_op jit(solution)/shard_map/ppermute | solution.py:34
  86.9 11.3 %copy-start.27 = (bf16[1,512,384]{2,1,0:T(8,128)(2,1)S(1)}, bf16[1,512,384]{2,1,0:T(8,128)(2,1)}, u32[]{:S(2)}) copy-start(bf16[1,512,384]{2,1,0:T(8,128)(2,1)} %copy-done.26) | copy-start | bytes 1179652
  86.9 11.3 %copy-start.29 = (bf16[1,512,384]{2,1,0:T(8,128)(2,1)S(1)}, bf16[1,512,384]{2,1,0:T(8,128)(2,1)}, u32[]{:S(2)}) copy-start(bf16[1,512,384]{2,1,0:T(8,128)(2,1)} %copy-done.28) | copy-start | bytes 1179652
  86.9 17.9 %collective-permute-start.20 = (f32[72,512]{1,0:T(8,128)S(1)}, f32[72,512]{1,0:T(8,128)S(1)}, u32[]{:S(2)}, u32[]{:S(2)}) collective-permute-start(f32[72,512]{1,0:T(8,128)S(1)} %get-tuple-element.85), channel_id=1, source_target_pairs={{0,2},{1,3},{2,0},{3,1},{4,6},{5,7},{6,4},{7,5},{8,10},{9,11},{10,... | collective-permute-start | bytes 442376 | tf_op jit(solution)/shard_map/ppermute | solution.py:34
  98.3 23.6 %collective-permute-start.24 = (bf16[2,512,384]{2,1,0:T(8,128)(2,1)S(1)}, bf16[2,512,384]{2,1,0:T(8,128)(2,1)S(1)}, u32[]{:S(2)}, u32[]{:S(2)}) collective-permute-start(bf16[2,512,384]{2,1,0:T(8,128)(2,1)S(1)} %broadcast_select_fusion.2), channel_id=1, source_target_pairs={{0,2},{1,3},{2,0},{3,1},{4,6},{5,7},{6,4},{7,5},{8,10},{9,11},{10,... | collective-permute-start | bytes 2359304 | tf_op jit(solution)/shard_map/ppermute | solution.py:34
  101.6 6.2 %collective-permute-start.15 = (bf16[2,512,384]{2,1,0:T(8,128)(2,1)S(1)}, bf16[2,512,384]{2,1,0:T(8,128)(2,1)S(1)}, u32[]{:S(2)}, u32[]{:S(2)}) collective-permute-start(bf16[2,512,384]{2,1,0:T(8,128)(2,1)S(1)} %collective-permute-done.9.d), channel_id=1, source_target_pairs={{0,1},{1,0},{2,3},{3,2},{4,5},{5,4},{6,7},{7,6},{8,9},{9,8},{10,11... | collective-permute-start | bytes 2359304 | tf_op jit(solution)/shard_map/ppermute | solution.py:34
  104.9 17.0 %collective-permute-start.21 = (f32[72,512]{1,0:T(8,128)S(1)}, f32[72,512]{1,0:T(8,128)S(1)}, u32[]{:S(2)}, u32[]{:S(2)}) collective-permute-start(f32[72,512]{1,0:T(8,128)S(1)} %pad_maximum_fusion.8), channel_id=1, source_target_pairs={{0,12},{1,13},{2,14},{3,15},{4,0},{5,1},{6,2},{7,3},{8,4},{9,5},{1... | collective-permute-start | bytes 442376 | tf_op jit(solution)/shard_map/ppermute | solution.py:29
  105.4 16.5 %collective-permute-start.22 = (f32[72,512]{1,0:T(8,128)S(1)}, f32[72,512]{1,0:T(8,128)S(1)}, u32[]{:S(2)}, u32[]{:S(2)}) collective-permute-start(f32[72,512]{1,0:T(8,128)S(1)} %pad_maximum_fusion.8), channel_id=1, source_target_pairs={{0,8},{1,9},{2,10},{3,11},{4,12},{5,13},{6,14},{7,15},{8,0},{9,1},... | collective-permute-start | bytes 442376 | tf_op jit(solution)/shard_map/ppermute | solution.py:29
  107.8 14.0 %collective-permute-start.23 = (f32[72,512]{1,0:T(8,128)S(1)}, f32[72,512]{1,0:T(8,128)S(1)}, u32[]{:S(2)}, u32[]{:S(2)}) collective-permute-start(f32[72,512]{1,0:T(8,128)S(1)} %pad_maximum_fusion.8), channel_id=1, source_target_pairs={{0,4},{1,5},{2,6},{3,7},{4,8},{5,9},{6,10},{7,11},{8,12},{9,13},{1... | collective-permute-start | bytes 442376 | tf_op jit(solution)/shard_map/ppermute | solution.py:29
  110.1 11.8 %copy-start.34 = (bf16[1,512,256]{2,1,0:T(8,128)(2,1)S(1)}, bf16[1,512,256]{2,1,0:T(8,128)(2,1)}, u32[]{:S(2)}) copy-start(bf16[1,512,256]{2,1,0:T(8,128)(2,1)} %slice_bitcast_fusion.8) | copy-start | bytes 786436
  110.1 11.8 %copy-start.36 = (bf16[1,512,256]{2,1,0:T(8,128)(2,1)S(1)}, bf16[1,512,256]{2,1,0:T(8,128)(2,1)}, u32[]{:S(2)}) copy-start(bf16[1,512,256]{2,1,0:T(8,128)(2,1)} %copy-done.35) | copy-start | bytes 786436
  118.0 7.1 %collective-permute-start.25 = (bf16[2,512,384]{2,1,0:T(8,128)(2,1)S(1)}, bf16[2,512,384]{2,1,0:T(8,128)(2,1)S(1)}, u32[]{:S(2)}, u32[]{:S(2)}) collective-permute-start(bf16[2,512,384]{2,1,0:T(8,128)(2,1)S(1)} %collective-permute-done.10.z), channel_id=1, source_target_pairs={{0,1},{1,0},{2,3},{3,2},{4,5},{5,4},{6,7},{7,6},{8,9},{9,8},{10,11... | collective-permute-start | bytes 2359304 | tf_op jit(solution)/shard_map/ppermute | solution.py:34
  122.0 3.2 %collective-permute-start.26 = (bf16[2,512,384]{2,1,0:T(8,128)(2,1)S(1)}, bf16[2,512,384]{2,1,0:T(8,128)(2,1)S(1)}, u32[]{:S(2)}, u32[]{:S(2)}) collective-permute-start(bf16[2,512,384]{2,1,0:T(8,128)(2,1)S(1)} %collective-permute-done.24.d), channel_id=1, source_target_pairs={{0,1},{1,0},{2,3},{3,2},{4,5},{5,4},{6,7},{7,6},{8,9},{9,8},{10,11... | collective-permute-start | bytes 2359304 | tf_op jit(solution)/shard_map/ppermute | solution.py:34
  123.6 9.6 %collective-permute-start.27 = (f32[64,512]{1,0:T(8,128)S(1)}, f32[64,512]{1,0:T(8,128)S(1)}, u32[]{:S(2)}, u32[]{:S(2)}) collective-permute-start(f32[64,512]{1,0:T(8,128)S(1)} %get-tuple-element.81), channel_id=1, source_target_pairs={{0,2},{1,3},{2,0},{3,1},{4,6},{5,7},{6,4},{7,5},{8,10},{9,11},{10,... | collective-permute-start | bytes 393224 | tf_op jit(solution)/shard_map/ppermute | solution.py:34
  123.8 16.1 %collective-permute-start.16 = (bf16[2,512,256]{2,1,0:T(8,128)(2,1)S(1)}, bf16[2,512,256]{2,1,0:T(8,128)(2,1)S(1)}, u32[]{:S(2)}, u32[]{:S(2)}) collective-permute-start(bf16[2,512,256]{2,1,0:T(8,128)(2,1)S(1)} %broadcast_select_fusion.4), channel_id=1, source_target_pairs={{0,2},{1,3},{2,0},{3,1},{4,6},{5,7},{6,4},{7,5},{8,10},{9,11},{10,... | collective-permute-start | bytes 1572872 | tf_op jit(solution)/shard_map/ppermute | solution.py:34
  125.2 15.7 %copy-start.7 = (f32[512,1024]{1,0:T(8,128)S(1)}, f32[512,1024]{1,0:T(8,128)}, u32[]{:S(2)}) copy-start(f32[512,1024]{1,0:T(8,128)} %copy-done.6) | copy-start | bytes 6291460
  133.2 7.7 %copy-start.5 = (f32[512,1024]{1,0:T(8,128)S(1)}, f32[512,1024]{1,0:T(8,128)}, u32[]{:S(2)}) copy-start(f32[512,1024]{1,0:T(8,128)} %copy-done.4) | copy-start | bytes 6291460
  133.2 7.7 %copy-start.13 = (f32[512,32]{1,0:T(8,128)S(1)}, f32[512,32]{1,0:T(8,128)}, u32[]{:S(2)}) copy-start(f32[512,32]{1,0:T(8,128)} %copy-done.12) | copy-start | bytes 196612
  133.3 7.5 %collective-permute-start.28 = (f32[64,1024]{1,0:T(8,128)S(1)}, f32[64,1024]{1,0:T(8,128)S(1)}, u32[]{:S(2)}, u32[]{:S(2)}) collective-permute-start(f32[64,1024]{1,0:T(8,128)S(1)} %fusion), channel_id=1, source_target_pairs={{0,1},{1,0},{2,3},{3,2},{4,5},{5,4},{6,7},{7,6},{8,9},{9,8},{10,11... | collective-permute-start | bytes 786440 | tf_op jit(solution)/shard_map/ppermute | solution.py:34
  140.0 4.5 %collective-permute-start.18 = (bf16[2,512,256]{2,1,0:T(8,128)(2,1)S(1)}, bf16[2,512,256]{2,1,0:T(8,128)(2,1)S(1)}, u32[]{:S(2)}, u32[]{:S(2)}) collective-permute-start(bf16[2,512,256]{2,1,0:T(8,128)(2,1)S(1)} %collective-permute-done.16.d), channel_id=1, source_target_pairs={{0,1},{1,0},{2,3},{3,2},{4,5},{5,4},{6,7},{7,6},{8,9},{9,8},{10,11... | collective-permute-start | bytes 1572872 | tf_op jit(solution)/shard_map/ppermute | solution.py:34
  140.8 3.7 %collective-permute-start.17 = (bf16[2,512,256]{2,1,0:T(8,128)(2,1)S(1)}, bf16[2,512,256]{2,1,0:T(8,128)(2,1)S(1)}, u32[]{:S(2)}, u32[]{:S(2)}) collective-permute-start(bf16[2,512,256]{2,1,0:T(8,128)(2,1)S(1)} %collective-permute-done.2.z), channel_id=1, source_target_pairs={{0,1},{1,0},{2,3},{3,2},{4,5},{5,4},{6,7},{7,6},{8,9},{9,8},{10,11... | collective-permute-start | bytes 1572872 | tf_op jit(solution)/shard_map/ppermute | solution.py:34
  140.9 3.6 %copy-start.2 = (bf16[512,2048]{1,0:T(8,128)(2,1)S(1)}, bf16[512,2048]{1,0:T(8,128)(2,1)}, u32[]{:S(2)}) copy-start(bf16[512,2048]{1,0:T(8,128)(2,1)} %q.9) | copy-start | bytes 6291460
  (5 other events, 4.4 us)

commit v4 on v3

--- a/solution.py
+++ b/solution.py
@@ -22,6 +22,10 @@
 EXP_SCALE = HD ** (-0.5) * 1.4426950408889634
 F32 = jnp.float32
 BF16 = jnp.bfloat16
+
+
+def in_hbm(*arrays):
+    return [pltpu.with_memory_space_constraint(array, pltpu.HBM) for array in arrays]
 
 
 def cyclic(array, by):
@@ -130,7 +134,7 @@
         ),
         input_output_aliases={10: 0} if sofar else {},
         compiler_params=pltpu.CompilerParams(vmem_limit_bytes=32 << 20),
-    )(flags, queries, keys, values, z, d, e, g, xk, xv, *sofar)
+    )(flags, *in_hbm(queries, keys, values), z, d, e, g, *in_hbm(xk, xv), *sofar)
 
 
 def packed(low, heads, keys, values):
@@ -235,7 +239,7 @@
         functools.partial(local_kernel, half * SCAN_HEADS // 2),
         name="scan_local",
         out_shape=(
-            jax.ShapeDtypeStruct((TOK_DEV, lanes), F32),
+            pltpu.HBM((TOK_DEV, lanes), F32),
             jax.ShapeDtypeStruct((N + 8, lanes), F32),
             jax.ShapeDtypeStruct((TOK_DEV, SCAN_HEADS), F32),
         ),
@@ -260,7 +264,7 @@
             pltpu.VMEM((TOK_DEV, N), BF16),
         ],
         compiler_params=pltpu.CompilerParams(vmem_limit_bytes=32 << 20),
-    )(x_in, decay_t, b_t, c_t, skip_wide)
+    )(*in_hbm(x_in), decay_t, b_t, c_t, skip_wide)
 
 
 def finish_kernel(part_a, part_b, cum, c_t, carried, out):
@@ -296,7 +300,7 @@
         ],
         out_specs=column(TOK_DEV),
         compiler_params=pltpu.CompilerParams(vmem_limit_bytes=32 << 20),
-    )(part_a, part_b, cum, c_t, carried)
+    )(*in_hbm(part_a, part_b), cum, c_t, carried)
 
 
 def joined(earlier, following):

time: 152 us -> 154 us (1.013)
  Pallas kernels: 59.6 us -> 63.9 us
  other arithmetic: 12.4 us -> 9.17 us
  local copies, waits for them, and re-layouts: 14.8 us -> 11.8 us
  waiting for transfers between devices: 29.3 us -> 31.6 us
    unnamed x80 -> x58, local copies, waits for them, and re-layouts: 8.16 us -> 3.08 us
    ppermute x21, waiting for transfers between devices: 13.3 us -> 16.7 us  [swapped(): return lax.ppermute(array, 'ctx', [(i, i ^ bit) for i in range(count)])]
    pallas_call x2, Pallas kernels: 14.5 us -> 17.1 us  [scan_local(): pl.pallas_call(functools.partial(local_kernel, half * SCAN_HEADS // 2), n...]
    select_n x5, other arithmetic: 3.91 us -> 1.57 us  [send(): chosen[k] = jnp.where(side == 0, own[k], came)]
    another operation x7, local copies, waits for them, and re-layouts: 6.39 us -> 8.47 us  [packed(): return jnp.stack([keys[:, cols], values[:, cols]])]
    pallas_call x1, Pallas kernels: 3.55 us -> 5.44 us  [scan_finish(): pl.pallas_call(finish_kernel, name='scan_finish', out_shape=jax.ShapeDtyp...]
  transfers between devices with their start and end apart: 29 -> 29, of which waited for: 7 -> 7; matrix products, arithmetic and copies ran while one was open for 11% -> 10% of each run, Pallas kernels for 36% -> 38%
where the time goes in v4:
time: 154 us; the launch traced here: 151 us
  Pallas kernels  63.9 us (41%)
  starting transfers between devices  33.5 us (22%)
  waiting for transfers between devices  31.6 us (21%)
  local copies, waits for them, and re-layouts  11.8 us (8%)
  other arithmetic  9.17 us (6%)
    pallas_call x5, Pallas kernels, attend(): pl.pallas_call(attend_kernel, name='attend', out_shape=jax.ShapeDtypeStru...  41.4 us
    ppermute x21, starting transfers between devices, swapped(): return lax.ppermute(array, 'ctx', [(i, i ^ bit) for i in range(count)])  21 us
    pallas_call x2, Pallas kernels, scan_local(): pl.pallas_call(functools.partial(local_kernel, half * SCAN_HEADS // 2), n...  17.1 us
    ppermute x21, waiting for transfers between devices, swapped(): return lax.ppermute(array, 'ctx', [(i, i ^ bit) for i in range(count)])  16.7 us
    ppermute x8, waiting for transfers between devices, cyclic(): lax.ppermute(array, 'ctx', [(i, (i + by) % count) for i in range(count)])  14.9 us
    ppermute x8, starting transfers between devices, cyclic(): lax.ppermute(array, 'ctx', [(i, (i + by) % count) for i in range(count)])  12.5 us
    another operation x7, local copies, waits for them, and re-layouts, packed(): return jnp.stack([keys[:, cols], values[:, cols]])  8.47 us
    another operation x5, other arithmetic, packed(): return jnp.stack([keys[:, cols], values[:, cols]])  6.11 us
  transfers between devices with their start and end apart: 29, of which 7 were waited for; matrix products, arithmetic and copies ran while one was open for 10% of the time, Pallas kernels for 38%

profile of v4, /device:TPU:13, one launch (start us, length us, event | category | flops | bytes accessed | tf_op | source)
XLA Modules:
  0.0 151.1 jit_solution(9445009390337419996)
XLA Ops:
  0.6 1.5 slice_bitcast_fusion.2
  2.1 1.2 pad_maximum_fusion
  3.3 1.3 collective-permute-start.1
  4.7 1.1 slice_bitcast_fusion.1
  5.8 0.8 copy-done.7
  6.6 1.1 pad_maximum_fusion.1
  7.6 1.3 collective-permute-start
  8.9 1.2 collective-permute-start.7
  10.2 0.1 broadcast_in_dim_reshape.3.skip
  10.4 8.4 %scan_local.2 = (f32[512,1024]{1,0:T(8,128)}, f32[72,1024]{1,0:T(8,128)S(1)}, f32[512,32]{1,0:T(8,128)S(1)}) custom-call(bf16[512,2048]{1,0:T(8,128)(2,1)} %x.1, f32[32,512]{1,0:T(8,128)S(1)} %bitcast.36, bf16[64,512]{1,0:T(8,128)(2,1)S(1)} %bitcast.38, bf16[64,512]{1,0:T(8,128)(2,1)S(1)} %bitcast.33, f32[1,2048]{1,0:T(1,128)S(1)} %broadcast_in_dim_reshape.3.skip), custom_call_target="tpu_custom_call" | custom-call | tf_op jit(solution)/shard_map/scan_local/pallas_call | solution.py:238
  18.8 8.8 %collective-permute-done.1.z = bf16[2,512,512]{2,1,0:T(8,128)(2,1)S(1)} collective-permute-done((bf16[2,512,512]{2,1,0:T(8,128)(2,1)}, bf16[2,512,512]{2,1,0:T(8,128)(2,1)S(1)}, u32[]{:S(2)}, u32[]{:S(2)}) %collective-permute-start.1) | collective-permute-done | bytes 1048608 | tf_op jit(solution)/shard_map/ppermute | solution.py:33
  27.6 0.1 broadcast_select_fusion.1
  27.8 0.3 collective-permute-start.4
  28.1 1.2 slice_bitcast_fusion.6
  29.3 3.0 %collective-permute-start.5 = (bf16[2,512,512]{2,1,0:T(8,128)(2,1)S(1)}, bf16[2,512,512]{2,1,0:T(8,128)(2,1)S(1)}, u32[]{:S(2)}, u32[]{:S(2)}) collective-permute-start(bf16[2,512,512]{2,1,0:T(8,128)(2,1)S(1)} %collective-permute-done.1.z), channel_id=1, source_target_pairs={{0,1},{1,0},{2,3},{3,2},{4,5},{5,4},{6,7},{7,6},{8,9},{9,8},{10,11... | collective-permute-start | bytes 3145736 | tf_op jit(solution)/shard_map/ppermute | solution.py:38
  32.3 1.0 slice_bitcast_fusion.7
  33.4 1.0 pad_maximum_fusion.2
  34.4 1.0 slice_bitcast_fusion.5
  35.5 8.6 %scan_local.3 = (f32[512,1024]{1,0:T(8,128)}, f32[72,1024]{1,0:T(8,128)S(1)}, f32[512,32]{1,0:T(8,128)}) custom-call(bf16[512,2048]{1,0:T(8,128)(2,1)} %x.1, f32[32,512]{1,0:T(8,128)S(1)} %bitcast.37, bf16[64,512]{1,0:T(8,128)(2,1)S(1)} %bitcast.39, bf16[64,512]{1,0:T(8,128)(2,1)S(1)} %bitcast.34, f32[1,2048]{1,0:T(1,128)S(1)} %broadcast_in_dim_reshape.3.skip), custom_call_target="tpu_custom_call" | custom-call | tf_op jit(solution)/shard_map/scan_local/pallas_call | solution.py:238
  44.1 6.1 %collective-permute-done.z = bf16[2,512,512]{2,1,0:T(8,128)(2,1)S(1)} collective-permute-done((bf16[2,512,512]{2,1,0:T(8,128)(2,1)}, bf16[2,512,512]{2,1,0:T(8,128)(2,1)S(1)}, u32[]{:S(2)}, u32[]{:S(2)}) %collective-permute-start) | collective-permute-done | bytes 1048608 | tf_op jit(solution)/shard_map/ppermute | solution.py:33
  50.2 1.3 collective-permute-start.3
  51.5 1.1 broadcast_select_fusion
  52.6 1.7 %collective-permute-start.6 = (bf16[2,512,512]{2,1,0:T(8,128)(2,1)}, bf16[2,512,512]{2,1,0:T(8,128)(2,1)}, u32[]{:S(2)}, u32[]{:S(2)}) collective-permute-start(bf16[2,512,512]{2,1,0:T(8,128)(2,1)} %collective-permute-done.4.d), channel_id=1, source_target_pairs={{0,1},{1,0},{2,3},{3,2},{4,5},{5,4},{6,7},{7,6},{8,9},{9,8},{10,11... | collective-permute-start | bytes 3145736 | tf_op jit(solution)/shard_map/ppermute | solution.py:38
  54.3 1.7 %slice_bitcast_fusion.8 = bf16[1,512,256]{2,1,0:T(8,128)(2,1)} fusion(bf16[512,2048]{1,0:T(8,128)(2,1)} %v.9), kind=kLoop, calls=%fused_computation.26 | loop fusion | bytes 524288 | tf_op jit(solution)/shard_map/stack | solution.py:142
  56.0 1.0 copy-done
  57.0 0.2 collective-permute-start.11
  57.2 1.0 pad_maximum_fusion.3
  58.2 1.0 slice_bitcast_fusion.9
  59.2 1.9 %pad_maximum_fusion.4 = bf16[2,512,256]{2,1,0:T(8,128)(2,1)} fusion(bf16[1,512,256]{2,1,0:T(8,128)(2,1)} %slice_bitcast_fusion.8, bf16[1,512,256]{2,1,0:T(8,128)(2,1)S(1)} %slice_bitcast_fusion.9), kind=kLoop, calls=%fused_computation.8 | loop fusion | flops 262144 | bytes 1048576 | tf_op jit(solution)/shard_map/stack | solution.py:142
  61.1 0.9 broadcast_select_fusion.8
  61.9 0.3 collective-permute-start.19
  62.2 0.1 pad_add_fusion.flags
  62.3 0.2 collective-permute-start.12
  62.6 1.3 collective-permute-start.10
  63.9 1.2 copy-done.1
  65.1 9.8 %attend.5.rest_0_ = bf16[512,2048]{1,0:T(8,128)(2,1)} custom-call(s32[3]{0:T(128)S(1)} %pad_add_fusion.flags, bf16[512,2048]{1,0:T(8,128)(2,1)} %q.9, bf16[512,2048]{1,0:T(8,128)(2,1)} %k.9, bf16[512,2048]{1,0:T(8,128)(2,1)} %v.9, bf16[2,512,512]{2,1,0:T(8,128)(2,1)S(1)} %collective-permute-done.1.z, bf16[2,512,512]{2,1,0:T(8,128)(2,1)} %collective-permute-done.4.d, ...), custom_call_target="tpu_custom_call" | custom-call | tf_op jit(solution)/shard_map/attend/pallas_call | solution.py:124
  74.9 2.0 %collective-permute-start.2 = (bf16[2,512,256]{2,1,0:T(8,128)(2,1)S(1)}, bf16[2,512,256]{2,1,0:T(8,128)(2,1)S(1)}, u32[]{:S(2)}, u32[]{:S(2)}) collective-permute-start(bf16[2,512,256]{2,1,0:T(8,128)(2,1)S(1)} %copy-done.27), channel_id=1, source_target_pairs={{0,4},{1,5},{2,6},{3,7},{4,8},{5,9},{6,10},{7,11},{8,12},{9,13},{1... | collective-permute-start | bytes 1572872 | tf_op jit(solution)/shard_map/ppermute | solution.py:33
  76.9 0.1 broadcast_select_fusion.3
  77.1 5.0 %collective-permute-done.11.d = bf16[2,512,512]{2,1,0:T(8,128)(2,1)} collective-permute-done((bf16[2,512,512]{2,1,0:T(8,128)(2,1)}, bf16[2,512,512]{2,1,0:T(8,128)(2,1)}, u32[]{:S(2)}, u32[]{:S(2)}) %collective-permute-start.11) | collective-permute-done | bytes 1048608 | tf_op jit(solution)/shard_map/ppermute | solution.py:38
  82.1 0.2 collective-permute-start.9
  82.3 1.1 collective-permute-start.13
  83.6 0.1 collective-permute-start.14
  83.6 2.2 %collective-permute-done.13.g = bf16[2,512,512]{2,1,0:T(8,128)(2,1)S(1)} collective-permute-done((bf16[2,512,512]{2,1,0:T(8,128)(2,1)}, bf16[2,512,512]{2,1,0:T(8,128)(2,1)S(1)}, u32[]{:S(2)}, u32[]{:S(2)}) %collective-permute-start.13) | collective-permute-done | bytes 1048608 | tf_op jit(solution)/shard_map/ppermute | solution.py:38
  85.9 1.2 collective-permute-start.20
  87.1 9.8 %attend.6.rest_0_ = bf16[512,2048]{1,0:T(8,128)(2,1)} custom-call(s32[3]{0:T(128)S(1)} %pad_add_fusion.flags, bf16[512,2048]{1,0:T(8,128)(2,1)} %q.9, bf16[512,2048]{1,0:T(8,128)(2,1)} %k.9, bf16[512,2048]{1,0:T(8,128)(2,1)} %v.9, bf16[2,512,512]{2,1,0:T(8,128)(2,1)S(1)} %collective-permute-done.z, ...), custom_call_target="tpu_custom_call", output_to_operand_aliasing={{}: (10, {})} | custom-call | tf_op jit(solution)/shard_map/attend/pallas_call | solution.py:124
  97.0 0.1 broadcast_select_fusion.2
  97.1 0.3 collective-permute-start.24
  97.4 3.0 %collective-permute-done.9.d = bf16[2,512,384]{2,1,0:T(8,128)(2,1)S(1)} collective-permute-done((bf16[2,512,384]{2,1,0:T(8,128)(2,1)S(1)}, bf16[2,512,384]{2,1,0:T(8,128)(2,1)S(1)}, u32[]{:S(2)}, u32[]{:S(2)}) %collective-permute-start.9) | collective-permute-done | bytes 786464 | tf_op jit(solution)/shard_map/ppermute | solution.py:38
  100.4 2.9 %collective-permute-start.15 = (bf16[2,512,384]{2,1,0:T(8,128)(2,1)S(1)}, bf16[2,512,384]{2,1,0:T(8,128)(2,1)S(1)}, u32[]{:S(2)}, u32[]{:S(2)}) collective-permute-start(bf16[2,512,384]{2,1,0:T(8,128)(2,1)S(1)} %collective-permute-done.9.d), channel_id=1, source_target_pairs={{0,1},{1,0},{2,3},{3,2},{4,5},{5,4},{6,7},{7,6},{8,9},{9,8},{10,11... | collective-permute-start | bytes 2359304 | tf_op jit(solution)/shard_map/ppermute | solution.py:38
  103.3 0.2 collective-permute-done.20
  103.6 1.3 collective-permute-start.21
  105.0 1.6 %collective-permute-start.22 = (f32[72,512]{1,0:T(8,128)S(1)}, f32[72,512]{1,0:T(8,128)S(1)}, u32[]{:S(2)}, u32[]{:S(2)}) collective-permute-start(f32[72,512]{1,0:T(8,128)S(1)} %pad_maximum_fusion.8), channel_id=1, source_target_pairs={{0,8},{1,9},{2,10},{3,11},{4,12},{5,13},{6,14},{7,15},{8,0},{9,1},... | collective-permute-start | bytes 442376 | tf_op jit(solution)/shard_map/ppermute | solution.py:33
  106.6 2.3 %collective-permute-start.23 = (f32[72,512]{1,0:T(8,128)S(1)}, f32[72,512]{1,0:T(8,128)S(1)}, u32[]{:S(2)}, u32[]{:S(2)}) collective-permute-start(f32[72,512]{1,0:T(8,128)S(1)} %pad_maximum_fusion.8), channel_id=1, source_target_pairs={{0,4},{1,5},{2,6},{3,7},{4,8},{5,9},{6,10},{7,11},{8,12},{9,13},{1... | collective-permute-start | bytes 442376 | tf_op jit(solution)/shard_map/ppermute | solution.py:33
  108.9 7.9 %attend.7.rest_0_ = bf16[512,2048]{1,0:T(8,128)(2,1)} custom-call(s32[3]{0:T(128)S(1)} %pad_add_fusion.flags, bf16[512,2048]{1,0:T(8,128)(2,1)} %q.9, bf16[512,2048]{1,0:T(8,128)(2,1)} %k.9, bf16[512,2048]{1,0:T(8,128)(2,1)} %v.9, bf16[2,512,384]{2,1,0:T(8,128)(2,1)S(1)} %collective-permute-done.3.z, ...), custom_call_target="tpu_custom_call", output_to_operand_aliasing={{}: (10, {})} | custom-call | tf_op jit(solution)/shard_map/attend/pallas_call | solution.py:124
  116.8 3.8 %collective-permute-start.25 = (bf16[2,512,384]{2,1,0:T(8,128)(2,1)S(1)}, bf16[2,512,384]{2,1,0:T(8,128)(2,1)S(1)}, u32[]{:S(2)}, u32[]{:S(2)}) collective-permute-start(bf16[2,512,384]{2,1,0:T(8,128)(2,1)S(1)} %collective-permute-done.10.z), channel_id=1, source_target_pairs={{0,1},{1,0},{2,3},{3,2},{4,5},{5,4},{6,7},{7,6},{8,9},{9,8},{10,11... | collective-permute-start | bytes 2359304 | tf_op jit(solution)/shard_map/ppermute | solution.py:38
  120.7 1.3 collective-permute-start.26
  122.4 0.3 collective-permute-start.27
  122.7 1.3 collective-permute-start.16
  124.0 7.9 %attend.8.rest_0_ = bf16[512,2048]{1,0:T(8,128)(2,1)} custom-call(s32[3]{0:T(128)S(1)} %pad_add_fusion.flags, bf16[512,2048]{1,0:T(8,128)(2,1)} %q.9, bf16[512,2048]{1,0:T(8,128)(2,1)} %k.9, bf16[512,2048]{1,0:T(8,128)(2,1)} %v.9, bf16[2,512,384]{2,1,0:T(8,128)(2,1)S(1)} %collective-permute-done.10.z, ...), custom_call_target="tpu_custom_call", output_to_operand_aliasing={{}: (10, {})} | custom-call | tf_op jit(solution)/shard_map/attend/pallas_call | solution.py:124
  132.0 0.6 collective-permute-start.28
  132.6 6.2 %collective-permute-done.16.d = bf16[2,512,256]{2,1,0:T(8,128)(2,1)S(1)} collective-permute-done((bf16[2,512,256]{2,1,0:T(8,128)(2,1)S(1)}, bf16[2,512,256]{2,1,0:T(8,128)(2,1)S(1)}, u32[]{:S(2)}, u32[]{:S(2)}) %collective-permute-start.16) | collective-permute-done | bytes 524320 | tf_op jit(solution)/shard_map/ppermute | solution.py:38
  138.8 0.8 collective-permute-start.18
  139.7 5.4 %scan_finish.1 = bf16[512,2048]{1,0:T(8,128)(2,1)} custom-call(f32[512,1024]{1,0:T(8,128)} %get-tuple-element.41.part_a, f32[512,1024]{1,0:T(8,128)} %get-tuple-element.44.part_b, f32[512,32]{1,0:T(8,128)S(1)} %copy-done.4, bf16[64,512]{1,0:T(8,128)(2,1)S(1)} %bitcast.35, f32[64,2048]{1,0:T(8,128)S(1)} %pad_maximum_fusion.5.carried), custom_call_target="tpu_custom_call" | custom-call | tf_op jit(solution)/shard_map/scan_finish/pallas_call | solution.py:289
  145.2 5.9 %attend.9 = bf16[512,2048]{1,0:T(8,128)(2,1)} custom-call(s32[3]{0:T(128)S(1)} %pad_add_fusion.flags, bf16[512,2048]{1,0:T(8,128)(2,1)} %q.9, bf16[512,2048]{1,0:T(8,128)(2,1)} %k.9, bf16[512,2048]{1,0:T(8,128)(2,1)} %v.9, bf16[2,512,256]{2,1,0:T(8,128)(2,1)S(1)} %collective-permute-done.2.z, ...), custom_call_target="tpu_custom_call", output_to_operand_aliasing={{}: (10, {})} | custom-call | tf_op jit(solution)/shard_map/attend/pallas_call | solution.py:124
  (112 shorter events, 0.9 us)
Async XLA Ops:
  2.1 3.7 %copy-start.9 = (bf16[1,512,512]{2,1,0:T(8,128)(2,1)}, bf16[1,512,512]{2,1,0:T(8,128)(2,1)S(1)}, u32[]{:S(2)}) copy-start(bf16[1,512,512]{2,1,0:T(8,128)(2,1)S(1)} %get-tuple-element.71) | copy-start | bytes 1572868
  2.1 5.5 %copy-start.11 = (bf16[1,512,512]{2,1,0:T(8,128)(2,1)}, bf16[1,512,512]{2,1,0:T(8,128)(2,1)S(1)}, u32[]{:S(2)}) copy-start(bf16[1,512,512]{2,1,0:T(8,128)(2,1)S(1)} %get-tuple-element.70) | copy-start | bytes 1572868
  2.1 5.5 %copy-start.13 = (bf16[1,512,512]{2,1,0:T(8,128)(2,1)}, bf16[1,512,512]{2,1,0:T(8,128)(2,1)S(1)}, u32[]{:S(2)}) copy-start(bf16[1,512,512]{2,1,0:T(8,128)(2,1)S(1)} %get-tuple-element.88) | copy-start | bytes 1572868
  3.3 6.8 %copy-start.28 = (f32[32]{0:T(128)S(1)}, f32[32]{0:T(128)}, u32[]{:S(2)}) copy-start(f32[32]{0:T(128)} %param.15) | copy-start | bytes 388
  3.3 7.0 %copy-start.2 = (bf16[512,64]{0,1:T(8,128)(2,1)S(1)}, bf16[512,64]{0,1:T(8,128)(2,1)}, u32[]{:S(2)}) copy-start(bf16[512,64]{0,1:T(8,128)(2,1)} %param.14) | copy-start | bytes 196612
  3.3 7.0 %copy-start.5 = (f32[512,32]{0,1:T(8,128)S(1)}, f32[512,32]{0,1:T(8,128)}, u32[]{:S(2)}) copy-start(f32[512,32]{0,1:T(8,128)} %param.12) | copy-start | bytes 196612
  3.3 7.0 %copy-start.6 = (bf16[512,64]{0,1:T(8,128)(2,1)S(1)}, bf16[512,64]{0,1:T(8,128)(2,1)}, u32[]{:S(2)}) copy-start(bf16[512,64]{0,1:T(8,128)(2,1)} %param.13) | copy-start | bytes 196612
  3.3 24.3 %collective-permute-start.1 = (bf16[2,512,512]{2,1,0:T(8,128)(2,1)}, bf16[2,512,512]{2,1,0:T(8,128)(2,1)S(1)}, u32[]{:S(2)}, u32[]{:S(2)}) collective-permute-start(bf16[2,512,512]{2,1,0:T(8,128)(2,1)} %pad_maximum_fusion), channel_id=1, source_target_pairs={{0,4},{1,5},{2,6},{3,7},{4,8},{5,9},{6,10},{7,11},{8,12},{9,13},{1... | collective-permute-start | bytes 3145736 | tf_op jit(solution)/shard_map/ppermute | solution.py:33
  5.8 0.8 copy-start.7
  7.6 42.6 %collective-permute-start = (bf16[2,512,512]{2,1,0:T(8,128)(2,1)}, bf16[2,512,512]{2,1,0:T(8,128)(2,1)S(1)}, u32[]{:S(2)}, u32[]{:S(2)}) collective-permute-start(bf16[2,512,512]{2,1,0:T(8,128)(2,1)} %pad_maximum_fusion.1), channel_id=1, source_target_pairs={{0,4},{1,5},{2,6},{3,7},{4,8},{5,9},{6,10},{7,11},{8,12},{9,13},{1... | collective-permute-start | bytes 3145736 | tf_op jit(solution)/shard_map/ppermute | solution.py:33
  8.9 53.0 %collective-permute-start.7 = (bf16[512,2048]{1,0:T(8,128)(2,1)}, bf16[512,2048]{1,0:T(8,128)(2,1)}, u32[]{:S(2)}, u32[]{:S(2)}) collective-permute-start(bf16[512,2048]{1,0:T(8,128)(2,1)} %k.9), channel_id=1, source_target_pairs={{0,1},{1,0},{2,3},{3,2},{4,5},{5,4},{6,7},{7,6},{8,9},{9,8},{10,11... | collective-permute-start | bytes 6291464 | tf_op jit(solution)/shard_map/ppermute | solution.py:38
  10.2 52.1 %collective-permute-start.8 = (bf16[512,2048]{1,0:T(8,128)(2,1)}, bf16[512,2048]{1,0:T(8,128)(2,1)}, u32[]{:S(2)}, u32[]{:S(2)}) collective-permute-start(bf16[512,2048]{1,0:T(8,128)(2,1)} %v.9), channel_id=1, source_target_pairs={{0,1},{1,0},{2,3},{3,2},{4,5},{5,4},{6,7},{7,6},{8,9},{9,8},{10,11... | collective-permute-start | bytes 6291464 | tf_op jit(solution)/shard_map/ppermute | solution.py:38
  10.3 17.3 %copy-start.12 = (bf16[1,512,512]{2,1,0:T(8,128)(2,1)S(1)}, bf16[1,512,512]{2,1,0:T(8,128)(2,1)}, u32[]{:S(2)}) copy-start(bf16[1,512,512]{2,1,0:T(8,128)(2,1)} %copy-done.11) | copy-start | bytes 1572868
  10.3 17.3 %copy-start.14 = (bf16[1,512,512]{2,1,0:T(8,128)(2,1)S(1)}, bf16[1,512,512]{2,1,0:T(8,128)(2,1)}, u32[]{:S(2)}) copy-start(bf16[1,512,512]{2,1,0:T(8,128)(2,1)} %copy-done.13) | copy-start | bytes 1572868
  18.8 10.5 %copy-start.3 = (f32[512,32]{1,0:T(8,128)}, f32[512,32]{1,0:T(8,128)S(1)}, u32[]{:S(2)}) copy-start(f32[512,32]{1,0:T(8,128)S(1)} %get-tuple-element.55.cum) | copy-start | bytes 196612
  27.8 24.8 %collective-permute-start.4 = (bf16[2,512,512]{2,1,0:T(8,128)(2,1)S(1)}, bf16[2,512,512]{2,1,0:T(8,128)(2,1)}, u32[]{:S(2)}, u32[]{:S(2)}) collective-permute-start(bf16[2,512,512]{2,1,0:T(8,128)(2,1)S(1)} %broadcast_select_fusion.1), channel_id=1, source_target_pairs={{0,2},{1,3},{2,0},{3,1},{4,6},{5,7},{6,4},{7,5},{8,10},{9,11},{10,... | collective-permute-start | bytes 3145736 | tf_op jit(solution)/shard_map/ppermute | solution.py:38
  29.3 5.1 %copy-start.19 = (bf16[1,512,384]{2,1,0:T(8,128)(2,1)}, bf16[1,512,384]{2,1,0:T(8,128)(2,1)S(1)}, u32[]{:S(2)}) copy-start(bf16[1,512,384]{2,1,0:T(8,128)(2,1)S(1)} %get-tuple-element.72) | copy-start | bytes 1179652
  29.3 27.9 %copy-start.15 = (bf16[1,512,384]{2,1,0:T(8,128)(2,1)}, bf16[1,512,384]{2,1,0:T(8,128)(2,1)S(1)}, u32[]{:S(2)}) copy-start(bf16[1,512,384]{2,1,0:T(8,128)(2,1)S(1)} %get-tuple-element.73) | copy-start | bytes 1179652
  29.3 26.7 %collective-permute-start.5 = (bf16[2,512,512]{2,1,0:T(8,128)(2,1)S(1)}, bf16[2,512,512]{2,1,0:T(8,128)(2,1)S(1)}, u32[]{:S(2)}, u32[]{:S(2)}) collective-permute-start(bf16[2,512,512]{2,1,0:T(8,128)(2,1)S(1)} %collective-permute-done.1.z), channel_id=1, source_target_pairs={{0,1},{1,0},{2,3},{3,2},{4,5},{5,4},{6,7},{7,6},{8,9},{9,8},{10,11... | collective-permute-start | bytes 3145736 | tf_op jit(solution)/shard_map/ppermute | solution.py:38
  33.4 1.0 copy-start.21
  33.4 18.1 %copy-start.8 = (bf16[1,512,512]{2,1,0:T(8,128)(2,1)S(1)}, bf16[1,512,512]{2,1,0:T(8,128)(2,1)}, u32[]{:S(2)}) copy-start(bf16[1,512,512]{2,1,0:T(8,128)(2,1)} %copy-done.7) | copy-start | bytes 1572868
  33.4 18.1 %copy-start.10 = (bf16[1,512,512]{2,1,0:T(8,128)(2,1)S(1)}, bf16[1,512,512]{2,1,0:T(8,128)(2,1)}, u32[]{:S(2)}) copy-start(bf16[1,512,512]{2,1,0:T(8,128)(2,1)} %copy-done.9) | copy-start | bytes 1572868
  35.5 21.8 %copy-start.17 = (bf16[1,512,384]{2,1,0:T(8,128)(2,1)}, bf16[1,512,384]{2,1,0:T(8,128)(2,1)S(1)}, u32[]{:S(2)}) copy-start(bf16[1,512,384]{2,1,0:T(8,128)(2,1)S(1)} %slice_bitcast_fusion.5) | copy-start | bytes 1179652
  50.2 24.7 %collective-permute-start.3 = (bf16[2,512,384]{2,1,0:T(8,128)(2,1)}, bf16[2,512,384]{2,1,0:T(8,128)(2,1)S(1)}, u32[]{:S(2)}, u32[]{:S(2)}) collective-permute-start(bf16[2,512,384]{2,1,0:T(8,128)(2,1)} %pad_maximum_fusion.2), channel_id=1, source_target_pairs={{0,4},{1,5},{2,6},{3,7},{4,8},{5,9},{6,10},{7,11},{8,12},{9,13},{1... | collective-permute-start | bytes 2359304 | tf_op jit(solution)/shard_map/ppermute | solution.py:33
  52.6 9.9 %collective-permute-start.6 = (bf16[2,512,512]{2,1,0:T(8,128)(2,1)}, bf16[2,512,512]{2,1,0:T(8,128)(2,1)}, u32[]{:S(2)}, u32[]{:S(2)}) collective-permute-start(bf16[2,512,512]{2,1,0:T(8,128)(2,1)} %collective-permute-done.4.d), channel_id=1, source_target_pairs={{0,1},{1,0},{2,3},{3,2},{4,5},{5,4},{6,7},{7,6},{8,9},{9,8},{10,11... | collective-permute-start | bytes 3145736 | tf_op jit(solution)/shard_map/ppermute | solution.py:38
  56.0 1.0 copy-start
  57.0 25.1 %collective-permute-start.11 = (bf16[2,512,512]{2,1,0:T(8,128)(2,1)}, bf16[2,512,512]{2,1,0:T(8,128)(2,1)}, u32[]{:S(2)}, u32[]{:S(2)}) collective-permute-start(bf16[2,512,512]{2,1,0:T(8,128)(2,1)} %broadcast_select_fusion), channel_id=1, source_target_pairs={{0,2},{1,3},{2,0},{3,1},{4,6},{5,7},{6,4},{7,5},{8,10},{9,11},{10,... | collective-permute-start | bytes 3145736 | tf_op jit(solution)/shard_map/ppermute | solution.py:38
  59.2 3.1 %copy-start.24 = (bf16[1,512,256]{2,1,0:T(8,128)(2,1)}, bf16[1,512,256]{2,1,0:T(8,128)(2,1)S(1)}, u32[]{:S(2)}) copy-start(bf16[1,512,256]{2,1,0:T(8,128)(2,1)S(1)} %slice_bitcast_fusion.9) | copy-start | bytes 786436
  61.9 20.4 %collective-permute-start.19 = (f32[72,1024]{1,0:T(8,128)}, f32[72,1024]{1,0:T(8,128)S(1)}, u32[]{:S(2)}, u32[]{:S(2)}) collective-permute-start(f32[72,1024]{1,0:T(8,128)} %get-tuple-element.78), channel_id=1, source_target_pairs={{0,1},{1,0},{2,3},{3,2},{4,5},{5,4},{6,7},{7,6},{8,9},{9,8},{10,11... | collective-permute-start | bytes 884744 | tf_op jit(solution)/shard_map/ppermute | solution.py:38
  62.3 21.3 %collective-permute-start.12 = (bf16[2,512,512]{2,1,0:T(8,128)(2,1)S(1)}, bf16[2,512,512]{2,1,0:T(8,128)(2,1)S(1)}, u32[]{:S(2)}, u32[]{:S(2)}) collective-permute-start(bf16[2,512,512]{2,1,0:T(8,128)(2,1)S(1)} %collective-permute-done.z), channel_id=1, source_target_pairs={{0,1},{1,0},{2,3},{3,2},{4,5},{5,4},{6,7},{7,6},{8,9},{9,8},{10,11... | collective-permute-start | bytes 3145736 | tf_op jit(solution)/shard_map/ppermute | solution.py:38
  62.6 34.4 %collective-permute-start.10 = (bf16[2,512,384]{2,1,0:T(8,128)(2,1)}, bf16[2,512,384]{2,1,0:T(8,128)(2,1)S(1)}, u32[]{:S(2)}, u32[]{:S(2)}) collective-permute-start(bf16[2,512,384]{2,1,0:T(8,128)(2,1)} %pad_maximum_fusion.3), channel_id=1, source_target_pairs={{0,4},{1,5},{2,6},{3,7},{4,8},{5,9},{6,10},{7,11},{8,12},{9,13},{1... | collective-permute-start | bytes 2359304 | tf_op jit(solution)/shard_map/ppermute | solution.py:33
  63.9 1.2 copy-start.1
  65.1 9.8 %copy-start.27 = (bf16[2,512,256]{2,1,0:T(8,128)(2,1)S(1)}, bf16[2,512,256]{2,1,0:T(8,128)(2,1)}, u32[]{:S(2)}) copy-start(bf16[2,512,256]{2,1,0:T(8,128)(2,1)} %pad_maximum_fusion.4) | copy-start | bytes 1572868
  65.1 11.9 %copy-start.20 = (bf16[1,512,384]{2,1,0:T(8,128)(2,1)S(1)}, bf16[1,512,384]{2,1,0:T(8,128)(2,1)}, u32[]{:S(2)}) copy-start(bf16[1,512,384]{2,1,0:T(8,128)(2,1)} %copy-done.19) | copy-start | bytes 1179652
  65.1 11.9 %copy-start.22 = (bf16[1,512,384]{2,1,0:T(8,128)(2,1)S(1)}, bf16[1,512,384]{2,1,0:T(8,128)(2,1)}, u32[]{:S(2)}) copy-start(bf16[1,512,384]{2,1,0:T(8,128)(2,1)} %copy-done.21) | copy-start | bytes 1179652
  74.9 8.5 %copy-start.26 = (f32[72,1024]{1,0:T(8,128)S(1)}, f32[72,1024]{1,0:T(8,128)}, u32[]{:S(2)}) copy-start(f32[72,1024]{1,0:T(8,128)} %get-tuple-element.59) | copy-start | bytes 884740
  74.9 41.9 %collective-permute-start.2 = (bf16[2,512,256]{2,1,0:T(8,128)(2,1)S(1)}, bf16[2,512,256]{2,1,0:T(8,128)(2,1)S(1)}, u32[]{:S(2)}, u32[]{:S(2)}) collective-permute-start(bf16[2,512,256]{2,1,0:T(8,128)(2,1)S(1)} %copy-done.27), channel_id=1, source_target_pairs={{0,4},{1,5},{2,6},{3,7},{4,8},{5,9},{6,10},{7,11},{8,12},{9,13},{1... | collective-permute-start | bytes 1572872 | tf_op jit(solution)/shard_map/ppermute | solution.py:33
  82.1 18.3 %collective-permute-start.9 = (bf16[2,512,384]{2,1,0:T(8,128)(2,1)S(1)}, bf16[2,512,384]{2,1,0:T(8,128)(2,1)S(1)}, u32[]{:S(2)}, u32[]{:S(2)}) collective-permute-start(bf16[2,512,384]{2,1,0:T(8,128)(2,1)S(1)} %broadcast_select_fusion.3), channel_id=1, source_target_pairs={{0,2},{1,3},{2,0},{3,1},{4,6},{5,7},{6,4},{7,5},{8,10},{9,11},{10,... | collective-permute-start | bytes 2359304 | tf_op jit(solution)/shard_map/ppermute | solution.py:38
  82.3 3.6 %collective-permute-start.13 = (bf16[2,512,512]{2,1,0:T(8,128)(2,1)}, bf16[2,512,512]{2,1,0:T(8,128)(2,1)S(1)}, u32[]{:S(2)}, u32[]{:S(2)}) collective-permute-start(bf16[2,512,512]{2,1,0:T(8,128)(2,1)} %collective-permute-done.11.d), channel_id=1, source_target_pairs={{0,1},{1,0},{2,3},{3,2},{4,5},{5,4},{6,7},{7,6},{8,9},{9,8},{10,11... | collective-permute-start | bytes 3145736 | tf_op jit(solution)/shard_map/ppermute | solution.py:38
  83.6 21.4 %collective-permute-start.14 = (bf16[2,512,384]{2,1,0:T(8,128)(2,1)S(1)}, bf16[2,512,384]{2,1,0:T(8,128)(2,1)S(1)}, u32[]{:S(2)}, u32[]{:S(2)}) collective-permute-start(bf16[2,512,384]{2,1,0:T(8,128)(2,1)S(1)} %collective-permute-done.3.z), channel_id=1, source_target_pairs={{0,1},{1,0},{2,3},{3,2},{4,5},{5,4},{6,7},{7,6},{8,9},{9,8},{10,11... | collective-permute-start | bytes 2359304 | tf_op jit(solution)/shard_map/ppermute | solution.py:38
  85.9 11.1 %copy-start.16 = (bf16[1,512,384]{2,1,0:T(8,128)(2,1)S(1)}, bf16[1,512,384]{2,1,0:T(8,128)(2,1)}, u32[]{:S(2)}) copy-start(bf16[1,512,384]{2,1,0:T(8,128)(2,1)} %copy-done.15) | copy-start | bytes 1179652
  85.9 11.1 %copy-start.18 = (bf16[1,512,384]{2,1,0:T(8,128)(2,1)S(1)}, bf16[1,512,384]{2,1,0:T(8,128)(2,1)}, u32[]{:S(2)}) copy-start(bf16[1,512,384]{2,1,0:T(8,128)(2,1)} %copy-done.17) | copy-start | bytes 1179652
  85.9 17.6 %collective-permute-start.20 = (f32[72,512]{1,0:T(8,128)S(1)}, f32[72,512]{1,0:T(8,128)S(1)}, u32[]{:S(2)}, u32[]{:S(2)}) collective-permute-start(f32[72,512]{1,0:T(8,128)S(1)} %get-tuple-element.85), channel_id=1, source_target_pairs={{0,2},{1,3},{2,0},{3,1},{4,6},{5,7},{6,4},{7,5},{8,10},{9,11},{10,... | collective-permute-start | bytes 442376 | tf_op jit(solution)/shard_map/ppermute | solution.py:38
  97.1 23.6 %collective-permute-start.24 = (bf16[2,512,384]{2,1,0:T(8,128)(2,1)S(1)}, bf16[2,512,384]{2,1,0:T(8,128)(2,1)S(1)}, u32[]{:S(2)}, u32[]{:S(2)}) collective-permute-start(bf16[2,512,384]{2,1,0:T(8,128)(2,1)S(1)} %broadcast_select_fusion.2), channel_id=1, source_target_pairs={{0,2},{1,3},{2,0},{3,1},{4,6},{5,7},{6,4},{7,5},{8,10},{9,11},{10,... | collective-permute-start | bytes 2359304 | tf_op jit(solution)/shard_map/ppermute | solution.py:38
  100.4 6.2 %collective-permute-start.15 = (bf16[2,512,384]{2,1,0:T(8,128)(2,1)S(1)}, bf16[2,512,384]{2,1,0:T(8,128)(2,1)S(1)}, u32[]{:S(2)}, u32[]{:S(2)}) collective-permute-start(bf16[2,512,384]{2,1,0:T(8,128)(2,1)S(1)} %collective-permute-done.9.d), channel_id=1, source_target_pairs={{0,1},{1,0},{2,3},{3,2},{4,5},{5,4},{6,7},{7,6},{8,9},{9,8},{10,11... | collective-permute-start | bytes 2359304 | tf_op jit(solution)/shard_map/ppermute | solution.py:38
  103.6 17.0 %collective-permute-start.21 = (f32[72,512]{1,0:T(8,128)S(1)}, f32[72,512]{1,0:T(8,128)S(1)}, u32[]{:S(2)}, u32[]{:S(2)}) collective-permute-start(f32[72,512]{1,0:T(8,128)S(1)} %pad_maximum_fusion.8), channel_id=1, source_target_pairs={{0,12},{1,13},{2,14},{3,15},{4,0},{5,1},{6,2},{7,3},{8,4},{9,5},{1... | collective-permute-start | bytes 442376 | tf_op jit(solution)/shard_map/ppermute | solution.py:33
  105.0 15.6 %collective-permute-start.22 = (f32[72,512]{1,0:T(8,128)S(1)}, f32[72,512]{1,0:T(8,128)S(1)}, u32[]{:S(2)}, u32[]{:S(2)}) collective-permute-start(f32[72,512]{1,0:T(8,128)S(1)} %pad_maximum_fusion.8), channel_id=1, source_target_pairs={{0,8},{1,9},{2,10},{3,11},{4,12},{5,13},{6,14},{7,15},{8,0},{9,1},... | collective-permute-start | bytes 442376 | tf_op jit(solution)/shard_map/ppermute | solution.py:33
  106.6 14.0 %collective-permute-start.23 = (f32[72,512]{1,0:T(8,128)S(1)}, f32[72,512]{1,0:T(8,128)S(1)}, u32[]{:S(2)}, u32[]{:S(2)}) collective-permute-start(f32[72,512]{1,0:T(8,128)S(1)} %pad_maximum_fusion.8), channel_id=1, source_target_pairs={{0,4},{1,5},{2,6},{3,7},{4,8},{5,9},{6,10},{7,11},{8,12},{9,13},{1... | collective-permute-start | bytes 442376 | tf_op jit(solution)/shard_map/ppermute | solution.py:33
  108.9 11.7 %copy-start.23 = (bf16[1,512,256]{2,1,0:T(8,128)(2,1)S(1)}, bf16[1,512,256]{2,1,0:T(8,128)(2,1)}, u32[]{:S(2)}) copy-start(bf16[1,512,256]{2,1,0:T(8,128)(2,1)} %slice_bitcast_fusion.8) | copy-start | bytes 786436
  108.9 11.7 %copy-start.25 = (bf16[1,512,256]{2,1,0:T(8,128)(2,1)S(1)}, bf16[1,512,256]{2,1,0:T(8,128)(2,1)}, u32[]{:S(2)}) copy-start(bf16[1,512,256]{2,1,0:T(8,128)(2,1)} %copy-done.24) | copy-start | bytes 786436
  116.8 7.2 %collective-permute-start.25 = (bf16[2,512,384]{2,1,0:T(8,128)(2,1)S(1)}, bf16[2,512,384]{2,1,0:T(8,128)(2,1)S(1)}, u32[]{:S(2)}, u32[]{:S(2)}) collective-permute-start(bf16[2,512,384]{2,1,0:T(8,128)(2,1)S(1)} %collective-permute-done.10.z), channel_id=1, source_target_pairs={{0,1},{1,0},{2,3},{3,2},{4,5},{5,4},{6,7},{7,6},{8,9},{9,8},{10,11... | collective-permute-start | bytes 2359304 | tf_op jit(solution)/shard_map/ppermute | solution.py:38
  120.7 3.2 %collective-permute-start.26 = (bf16[2,512,384]{2,1,0:T(8,128)(2,1)S(1)}, bf16[2,512,384]{2,1,0:T(8,128)(2,1)S(1)}, u32[]{:S(2)}, u32[]{:S(2)}) collective-permute-start(bf16[2,512,384]{2,1,0:T(8,128)(2,1)S(1)} %collective-permute-done.24.d), channel_id=1, source_target_pairs={{0,1},{1,0},{2,3},{3,2},{4,5},{5,4},{6,7},{7,6},{8,9},{9,8},{10,11... | collective-permute-start | bytes 2359304 | tf_op jit(solution)/shard_map/ppermute | solution.py:38
  122.4 9.5 %collective-permute-start.27 = (f32[64,512]{1,0:T(8,128)S(1)}, f32[64,512]{1,0:T(8,128)S(1)}, u32[]{:S(2)}, u32[]{:S(2)}) collective-permute-start(f32[64,512]{1,0:T(8,128)S(1)} %get-tuple-element.81), channel_id=1, source_target_pairs={{0,2},{1,3},{2,0},{3,1},{4,6},{5,7},{6,4},{7,5},{8,10},{9,11},{10,... | collective-permute-start | bytes 393224 | tf_op jit(solution)/shard_map/ppermute | solution.py:38
  122.7 16.1 %collective-permute-start.16 = (bf16[2,512,256]{2,1,0:T(8,128)(2,1)S(1)}, bf16[2,512,256]{2,1,0:T(8,128)(2,1)S(1)}, u32[]{:S(2)}, u32[]{:S(2)}) collective-permute-start(bf16[2,512,256]{2,1,0:T(8,128)(2,1)S(1)} %broadcast_select_fusion.4), channel_id=1, source_target_pairs={{0,2},{1,3},{2,0},{3,1},{4,6},{5,7},{6,4},{7,5},{8,10},{9,11},{10,... | collective-permute-start | bytes 1572872 | tf_op jit(solution)/shard_map/ppermute | solution.py:38
  131.9 7.8 %copy-start.4 = (f32[512,32]{1,0:T(8,128)S(1)}, f32[512,32]{1,0:T(8,128)}, u32[]{:S(2)}) copy-start(f32[512,32]{1,0:T(8,128)} %copy-done.3) | copy-start | bytes 196612
  132.0 7.6 %collective-permute-start.28 = (f32[64,1024]{1,0:T(8,128)S(1)}, f32[64,1024]{1,0:T(8,128)S(1)}, u32[]{:S(2)}, u32[]{:S(2)}) collective-permute-start(f32[64,1024]{1,0:T(8,128)S(1)} %fusion), channel_id=1, source_target_pairs={{0,1},{1,0},{2,3},{3,2},{4,5},{5,4},{6,7},{7,6},{8,9},{9,8},{10,11... | collective-permute-start | bytes 786440 | tf_op jit(solution)/shard_map/ppermute | solution.py:38
  138.8 6.4 %collective-permute-start.18 = (bf16[2,512,256]{2,1,0:T(8,128)(2,1)S(1)}, bf16[2,512,256]{2,1,0:T(8,128)(2,1)S(1)}, u32[]{:S(2)}, u32[]{:S(2)}) collective-permute-start(bf16[2,512,256]{2,1,0:T(8,128)(2,1)S(1)} %collective-permute-done.16.d), channel_id=1, source_target_pairs={{0,1},{1,0},{2,3},{3,2},{4,5},{5,4},{6,7},{7,6},{8,9},{9,8},{10,11... | collective-permute-start | bytes 1572872 | tf_op jit(solution)/shard_map/ppermute | solution.py:38
  139.6 5.6 %collective-permute-start.17 = (bf16[2,512,256]{2,1,0:T(8,128)(2,1)S(1)}, bf16[2,512,256]{2,1,0:T(8,128)(2,1)S(1)}, u32[]{:S(2)}, u32[]{:S(2)}) collective-permute-start(bf16[2,512,256]{2,1,0:T(8,128)(2,1)S(1)} %collective-permute-done.2.z), channel_id=1, source_target_pairs={{0,1},{1,0},{2,3},{3,2},{4,5},{5,4},{6,7},{7,6},{8,9},{9,8},{10,11... | collective-permute-start | bytes 1572872 | tf_op jit(solution)/shard_map/ppermute | solution.py:38

commit v5 on v4

--- a/solution.py
+++ b/solution.py
@@ -239,7 +239,7 @@
         functools.partial(local_kernel, half * SCAN_HEADS // 2),
         name="scan_local",
         out_shape=(
-            pltpu.HBM((TOK_DEV, lanes), F32),
+            jax.ShapeDtypeStruct((TOK_DEV, lanes), F32),
             jax.ShapeDtypeStruct((N + 8, lanes), F32),
             jax.ShapeDtypeStruct((TOK_DEV, SCAN_HEADS), F32),
         ),
@@ -300,7 +300,7 @@
         ],
         out_specs=column(TOK_DEV),
         compiler_params=pltpu.CompilerParams(vmem_limit_bytes=32 << 20),
-    )(*in_hbm(part_a, part_b), cum, c_t, carried)
+    )(part_a, part_b, cum, c_t, carried)
 
 
 def joined(earlier, following):

time: 154 us -> 152 us (0.987)
  Pallas kernels: 63.9 us -> 61.4 us
    pallas_call x1, Pallas kernels: 5.44 us -> 3.55 us  [scan_finish(): pl.pallas_call(finish_kernel, name='scan_finish', out_shape=jax.ShapeDtyp...]
    unnamed x58 -> x66, local copies, waits for them, and re-layouts: 3.08 us -> 3.14 us
  transfers between devices with their start and end apart: 29 -> 29, of which waited for: 7 -> 7; matrix products, arithmetic and copies ran while one was open for 10% -> 10% of each run, Pallas kernels for 38% -> 37%
where the time goes in v5:
time: 152 us; the launch traced here: 149 us
  Pallas kernels  61.4 us (40%)
  starting transfers between devices  33.5 us (22%)
  waiting for transfers between devices  32.1 us (21%)
  local copies, waits for them, and re-layouts  11.8 us (8%)
  other arithmetic  9.36 us (6%)
    pallas_call x5, Pallas kernels, attend(): pl.pallas_call(attend_kernel, name='attend', out_shape=jax.ShapeDtypeStru...  41.4 us
    ppermute x21, starting transfers between devices, swapped(): return lax.ppermute(array, 'ctx', [(i, i ^ bit) for i in range(count)])  21 us
    ppermute x21, waiting for transfers between devices, swapped(): return lax.ppermute(array, 'ctx', [(i, i ^ bit) for i in range(count)])  16.6 us
    pallas_call x2, Pallas kernels, scan_local(): pl.pallas_call(functools.partial(local_kernel, half * SCAN_HEADS // 2), n...  16.4 us
    ppermute x8, waiting for transfers between devices, cyclic(): lax.ppermute(array, 'ctx', [(i, (i + by) % count) for i in range(count)])  15.6 us
    ppermute x8, starting transfers between devices, cyclic(): lax.ppermute(array, 'ctx', [(i, (i + by) % count) for i in range(count)])  12.5 us
    another operation x7, local copies, waits for them, and re-layouts, packed(): return jnp.stack([keys[:, cols], values[:, cols]])  8.49 us
    another operation x5, other arithmetic, packed(): return jnp.stack([keys[:, cols], values[:, cols]])  6.19 us
  transfers between devices with their start and end apart: 29, of which 7 were waited for; matrix products, arithmetic and copies ran while one was open for 10% of the time, Pallas kernels for 37%

profile of v5, /device:TPU:13, one launch (start us, length us, event | category | flops | bytes accessed | tf_op | source)
XLA Modules:
  0.0 149.4 jit_solution(14242514104904354040)
XLA Ops:
  0.6 1.5 slice_bitcast_fusion.2
  2.1 1.2 pad_maximum_fusion
  3.4 1.3 collective-permute-start.1
  4.7 1.1 slice_bitcast_fusion.1
  5.8 0.8 copy-done.11
  6.7 1.1 pad_maximum_fusion.1
  7.7 1.3 collective-permute-start
  9.0 1.2 collective-permute-start.7
  10.3 0.1 broadcast_in_dim_reshape.3.skip
  10.5 7.8 %scan_local.2 = (f32[512,1024]{1,0:T(8,128)S(1)}, f32[72,1024]{1,0:T(8,128)S(1)}, f32[512,32]{1,0:T(8,128)S(1)}) custom-call(bf16[512,2048]{1,0:T(8,128)(2,1)} %x.1, f32[32,512]{1,0:T(8,128)S(1)} %bitcast.36, bf16[64,512]{1,0:T(8,128)(2,1)S(1)} %bitcast.38, bf16[64,512]{1,0:T(8,128)(2,1)S(1)} %bitcast.33, f32[1,2048]{1,0:T(1,128)S(1)} %broadcast_in_dim_reshape.3.skip), custom_call_target="tpu_custom_call" | custom-call | tf_op jit(solution)/shard_map/scan_local/pallas_call | solution.py:238
  18.3 9.4 %collective-permute-done.1.z = bf16[2,512,512]{2,1,0:T(8,128)(2,1)S(1)} collective-permute-done((bf16[2,512,512]{2,1,0:T(8,128)(2,1)}, bf16[2,512,512]{2,1,0:T(8,128)(2,1)S(1)}, u32[]{:S(2)}, u32[]{:S(2)}) %collective-permute-start.1) | collective-permute-done | bytes 1048608 | tf_op jit(solution)/shard_map/ppermute | solution.py:33
  27.7 0.1 broadcast_select_fusion.1
  27.8 0.3 collective-permute-start.4
  28.1 1.2 slice_bitcast_fusion.6
  29.3 3.0 %collective-permute-start.5 = (bf16[2,512,512]{2,1,0:T(8,128)(2,1)S(1)}, bf16[2,512,512]{2,1,0:T(8,128)(2,1)S(1)}, u32[]{:S(2)}, u32[]{:S(2)}) collective-permute-start(bf16[2,512,512]{2,1,0:T(8,128)(2,1)S(1)} %collective-permute-done.1.z), channel_id=1, source_target_pairs={{0,1},{1,0},{2,3},{3,2},{4,5},{5,4},{6,7},{7,6},{8,9},{9,8},{10,11... | collective-permute-start | bytes 3145736 | tf_op jit(solution)/shard_map/ppermute | solution.py:38
  32.4 1.0 slice_bitcast_fusion.7
  33.5 1.0 pad_maximum_fusion.2
  34.4 1.0 slice_bitcast_fusion.5
  35.5 8.6 %scan_local.3 = (f32[512,1024]{1,0:T(8,128)S(1)}, f32[72,1024]{1,0:T(8,128)S(1)}, f32[512,32]{1,0:T(8,128)}) custom-call(bf16[512,2048]{1,0:T(8,128)(2,1)} %x.1, f32[32,512]{1,0:T(8,128)S(1)} %bitcast.37, bf16[64,512]{1,0:T(8,128)(2,1)S(1)} %bitcast.39, bf16[64,512]{1,0:T(8,128)(2,1)S(1)} %bitcast.34, f32[1,2048]{1,0:T(1,128)S(1)} %broadcast_in_dim_reshape.3.skip), custom_call_target="tpu_custom_call" | custom-call | tf_op jit(solution)/shard_map/scan_local/pallas_call | solution.py:238
  44.1 6.2 %collective-permute-done.z = bf16[2,512,512]{2,1,0:T(8,128)(2,1)S(1)} collective-permute-done((bf16[2,512,512]{2,1,0:T(8,128)(2,1)}, bf16[2,512,512]{2,1,0:T(8,128)(2,1)S(1)}, u32[]{:S(2)}, u32[]{:S(2)}) %collective-permute-start) | collective-permute-done | bytes 1048608 | tf_op jit(solution)/shard_map/ppermute | solution.py:33
  50.2 1.3 collective-permute-start.3
  51.5 1.2 broadcast_select_fusion
  52.7 1.7 %collective-permute-start.6 = (bf16[2,512,512]{2,1,0:T(8,128)(2,1)}, bf16[2,512,512]{2,1,0:T(8,128)(2,1)}, u32[]{:S(2)}, u32[]{:S(2)}) collective-permute-start(bf16[2,512,512]{2,1,0:T(8,128)(2,1)} %collective-permute-done.4.d), channel_id=1, source_target_pairs={{0,1},{1,0},{2,3},{3,2},{4,5},{5,4},{6,7},{7,6},{8,9},{9,8},{10,11... | collective-permute-start | bytes 3145736 | tf_op jit(solution)/shard_map/ppermute | solution.py:38
  54.5 1.7 %slice_bitcast_fusion.8 = bf16[1,512,256]{2,1,0:T(8,128)(2,1)} fusion(bf16[512,2048]{1,0:T(8,128)(2,1)} %v.9), kind=kLoop, calls=%fused_computation.26 | loop fusion | bytes 524288 | tf_op jit(solution)/shard_map/stack | solution.py:142
  56.2 1.0 copy-done.4
  57.1 0.2 collective-permute-start.11
  57.4 1.0 pad_maximum_fusion.3
  58.4 1.0 slice_bitcast_fusion.9
  59.4 1.9 %pad_maximum_fusion.4 = bf16[2,512,256]{2,1,0:T(8,128)(2,1)} fusion(bf16[1,512,256]{2,1,0:T(8,128)(2,1)} %slice_bitcast_fusion.8, bf16[1,512,256]{2,1,0:T(8,128)(2,1)S(1)} %slice_bitcast_fusion.9), kind=kLoop, calls=%fused_computation.8 | loop fusion | flops 262144 | bytes 1048576 | tf_op jit(solution)/shard_map/stack | solution.py:142
  61.3 0.9 broadcast_select_fusion.8
  62.2 0.3 collective-permute-start.19
  62.5 0.1 pad_add_fusion.flags
  62.5 0.2 collective-permute-start.12
  62.8 1.3 collective-permute-start.10
  64.1 1.2 copy-done.5
  65.3 9.8 %attend.5.rest_0_ = bf16[512,2048]{1,0:T(8,128)(2,1)} custom-call(s32[3]{0:T(128)S(1)} %pad_add_fusion.flags, bf16[512,2048]{1,0:T(8,128)(2,1)} %q.9, bf16[512,2048]{1,0:T(8,128)(2,1)} %k.9, bf16[512,2048]{1,0:T(8,128)(2,1)} %v.9, bf16[2,512,512]{2,1,0:T(8,128)(2,1)S(1)} %collective-permute-done.1.z, bf16[2,512,512]{2,1,0:T(8,128)(2,1)} %collective-permute-done.4.d, ...), custom_call_target="tpu_custom_call" | custom-call | tf_op jit(solution)/shard_map/attend/pallas_call | solution.py:124
  75.1 2.0 %collective-permute-start.2 = (bf16[2,512,256]{2,1,0:T(8,128)(2,1)S(1)}, bf16[2,512,256]{2,1,0:T(8,128)(2,1)S(1)}, u32[]{:S(2)}, u32[]{:S(2)}) collective-permute-start(bf16[2,512,256]{2,1,0:T(8,128)(2,1)S(1)} %copy-done.31), channel_id=1, source_target_pairs={{0,4},{1,5},{2,6},{3,7},{4,8},{5,9},{6,10},{7,11},{8,12},{9,13},{1... | collective-permute-start | bytes 1572872 | tf_op jit(solution)/shard_map/ppermute | solution.py:33
  77.2 0.1 broadcast_select_fusion.3
  77.3 4.9 %collective-permute-done.11.d = bf16[2,512,512]{2,1,0:T(8,128)(2,1)} collective-permute-done((bf16[2,512,512]{2,1,0:T(8,128)(2,1)}, bf16[2,512,512]{2,1,0:T(8,128)(2,1)}, u32[]{:S(2)}, u32[]{:S(2)}) %collective-permute-start.11) | collective-permute-done | bytes 1048608 | tf_op jit(solution)/shard_map/ppermute | solution.py:38
  82.3 0.2 collective-permute-start.9
  82.5 1.1 collective-permute-start.13
  83.7 0.1 collective-permute-start.14
  83.8 2.2 %collective-permute-done.13.g = bf16[2,512,512]{2,1,0:T(8,128)(2,1)S(1)} collective-permute-done((bf16[2,512,512]{2,1,0:T(8,128)(2,1)}, bf16[2,512,512]{2,1,0:T(8,128)(2,1)S(1)}, u32[]{:S(2)}, u32[]{:S(2)}) %collective-permute-start.13) | collective-permute-done | bytes 1048608 | tf_op jit(solution)/shard_map/ppermute | solution.py:38
  86.1 1.2 collective-permute-start.20
  87.3 9.8 %attend.6.rest_0_ = bf16[512,2048]{1,0:T(8,128)(2,1)} custom-call(s32[3]{0:T(128)S(1)} %pad_add_fusion.flags, bf16[512,2048]{1,0:T(8,128)(2,1)} %q.9, bf16[512,2048]{1,0:T(8,128)(2,1)} %k.9, bf16[512,2048]{1,0:T(8,128)(2,1)} %v.9, bf16[2,512,512]{2,1,0:T(8,128)(2,1)S(1)} %collective-permute-done.z, ...), custom_call_target="tpu_custom_call", output_to_operand_aliasing={{}: (10, {})} | custom-call | tf_op jit(solution)/shard_map/attend/pallas_call | solution.py:124
  97.2 0.1 broadcast_select_fusion.2
  97.3 0.3 collective-permute-start.24
  97.6 3.0 %collective-permute-done.9.d = bf16[2,512,384]{2,1,0:T(8,128)(2,1)S(1)} collective-permute-done((bf16[2,512,384]{2,1,0:T(8,128)(2,1)S(1)}, bf16[2,512,384]{2,1,0:T(8,128)(2,1)S(1)}, u32[]{:S(2)}, u32[]{:S(2)}) %collective-permute-start.9) | collective-permute-done | bytes 786464 | tf_op jit(solution)/shard_map/ppermute | solution.py:38
  100.5 2.9 %collective-permute-start.15 = (bf16[2,512,384]{2,1,0:T(8,128)(2,1)S(1)}, bf16[2,512,384]{2,1,0:T(8,128)(2,1)S(1)}, u32[]{:S(2)}, u32[]{:S(2)}) collective-permute-start(bf16[2,512,384]{2,1,0:T(8,128)(2,1)S(1)} %collective-permute-done.9.d), channel_id=1, source_target_pairs={{0,1},{1,0},{2,3},{3,2},{4,5},{5,4},{6,7},{7,6},{8,9},{9,8},{10,11... | collective-permute-start | bytes 2359304 | tf_op jit(solution)/shard_map/ppermute | solution.py:38
  103.5 0.2 collective-permute-done.20
  103.8 1.2 collective-permute-start.21
  105.1 1.7 %collective-permute-start.22 = (f32[72,512]{1,0:T(8,128)S(1)}, f32[72,512]{1,0:T(8,128)S(1)}, u32[]{:S(2)}, u32[]{:S(2)}) collective-permute-start(f32[72,512]{1,0:T(8,128)S(1)} %pad_maximum_fusion.8), channel_id=1, source_target_pairs={{0,8},{1,9},{2,10},{3,11},{4,12},{5,13},{6,14},{7,15},{8,0},{9,1},... | collective-permute-start | bytes 442376 | tf_op jit(solution)/shard_map/ppermute | solution.py:33
  106.8 2.3 %collective-permute-start.23 = (f32[72,512]{1,0:T(8,128)S(1)}, f32[72,512]{1,0:T(8,128)S(1)}, u32[]{:S(2)}, u32[]{:S(2)}) collective-permute-start(f32[72,512]{1,0:T(8,128)S(1)} %pad_maximum_fusion.8), channel_id=1, source_target_pairs={{0,4},{1,5},{2,6},{3,7},{4,8},{5,9},{6,10},{7,11},{8,12},{9,13},{1... | collective-permute-start | bytes 442376 | tf_op jit(solution)/shard_map/ppermute | solution.py:33
  109.1 7.9 %attend.7.rest_0_ = bf16[512,2048]{1,0:T(8,128)(2,1)} custom-call(s32[3]{0:T(128)S(1)} %pad_add_fusion.flags, bf16[512,2048]{1,0:T(8,128)(2,1)} %q.9, bf16[512,2048]{1,0:T(8,128)(2,1)} %k.9, bf16[512,2048]{1,0:T(8,128)(2,1)} %v.9, bf16[2,512,384]{2,1,0:T(8,128)(2,1)S(1)} %collective-permute-done.3.z, ...), custom_call_target="tpu_custom_call", output_to_operand_aliasing={{}: (10, {})} | custom-call | tf_op jit(solution)/shard_map/attend/pallas_call | solution.py:124
  117.0 3.8 %collective-permute-start.25 = (bf16[2,512,384]{2,1,0:T(8,128)(2,1)S(1)}, bf16[2,512,384]{2,1,0:T(8,128)(2,1)S(1)}, u32[]{:S(2)}, u32[]{:S(2)}) collective-permute-start(bf16[2,512,384]{2,1,0:T(8,128)(2,1)S(1)} %collective-permute-done.10.z), channel_id=1, source_target_pairs={{0,1},{1,0},{2,3},{3,2},{4,5},{5,4},{6,7},{7,6},{8,9},{9,8},{10,11... | collective-permute-start | bytes 2359304 | tf_op jit(solution)/shard_map/ppermute | solution.py:38
  120.9 1.3 collective-permute-start.26
  122.5 0.3 collective-permute-start.27
  122.8 1.3 collective-permute-start.16
  124.1 8.0 %attend.8.rest_0_ = bf16[512,2048]{1,0:T(8,128)(2,1)} custom-call(s32[3]{0:T(128)S(1)} %pad_add_fusion.flags, bf16[512,2048]{1,0:T(8,128)(2,1)} %q.9, bf16[512,2048]{1,0:T(8,128)(2,1)} %k.9, bf16[512,2048]{1,0:T(8,128)(2,1)} %v.9, bf16[2,512,384]{2,1,0:T(8,128)(2,1)S(1)} %collective-permute-done.10.z, ...), custom_call_target="tpu_custom_call", output_to_operand_aliasing={{}: (10, {})} | custom-call | tf_op jit(solution)/shard_map/attend/pallas_call | solution.py:124
  132.2 0.6 collective-permute-start.28
  132.8 6.1 %collective-permute-done.16.d = bf16[2,512,256]{2,1,0:T(8,128)(2,1)S(1)} collective-permute-done((bf16[2,512,256]{2,1,0:T(8,128)(2,1)S(1)}, bf16[2,512,256]{2,1,0:T(8,128)(2,1)S(1)}, u32[]{:S(2)}, u32[]{:S(2)}) %collective-permute-start.16) | collective-permute-done | bytes 524320 | tf_op jit(solution)/shard_map/ppermute | solution.py:38
  138.9 0.8 collective-permute-start.18
  139.9 3.6 %scan_finish.1 = bf16[512,2048]{1,0:T(8,128)(2,1)} custom-call(f32[512,1024]{1,0:T(8,128)S(1)} %copy-done.1, f32[512,1024]{1,0:T(8,128)S(1)} %copy-done.3, f32[512,32]{1,0:T(8,128)S(1)} %copy-done.8, bf16[64,512]{1,0:T(8,128)(2,1)S(1)} %bitcast.35, f32[64,2048]{1,0:T(8,128)S(1)} %pad_maximum_fusion.5.carried), custom_call_target="tpu_custom_call" | custom-call | tf_op jit(solution)/shard_map/scan_finish/pallas_call | solution.py:289
  143.4 5.9 %attend.9 = bf16[512,2048]{1,0:T(8,128)(2,1)} custom-call(s32[3]{0:T(128)S(1)} %pad_add_fusion.flags, bf16[512,2048]{1,0:T(8,128)(2,1)} %q.9, bf16[512,2048]{1,0:T(8,128)(2,1)} %k.9, bf16[512,2048]{1,0:T(8,128)(2,1)} %v.9, bf16[2,512,256]{2,1,0:T(8,128)(2,1)S(1)} %collective-permute-done.2.z, ...), custom_call_target="tpu_custom_call", output_to_operand_aliasing={{}: (10, {})} | custom-call | tf_op jit(solution)/shard_map/attend/pallas_call | solution.py:124
  (120 shorter events, 0.9 us)
Async XLA Ops:
  2.1 3.7 %copy-start.13 = (bf16[1,512,512]{2,1,0:T(8,128)(2,1)}, bf16[1,512,512]{2,1,0:T(8,128)(2,1)S(1)}, u32[]{:S(2)}) copy-start(bf16[1,512,512]{2,1,0:T(8,128)(2,1)S(1)} %get-tuple-element.71) | copy-start | bytes 1572868
  2.1 5.6 %copy-start.15 = (bf16[1,512,512]{2,1,0:T(8,128)(2,1)}, bf16[1,512,512]{2,1,0:T(8,128)(2,1)S(1)}, u32[]{:S(2)}) copy-start(bf16[1,512,512]{2,1,0:T(8,128)(2,1)S(1)} %get-tuple-element.70) | copy-start | bytes 1572868
  2.1 5.6 %copy-start.17 = (bf16[1,512,512]{2,1,0:T(8,128)(2,1)}, bf16[1,512,512]{2,1,0:T(8,128)(2,1)S(1)}, u32[]{:S(2)}) copy-start(bf16[1,512,512]{2,1,0:T(8,128)(2,1)S(1)} %get-tuple-element.88) | copy-start | bytes 1572868
  3.4 6.9 %copy-start.32 = (f32[32]{0:T(128)S(1)}, f32[32]{0:T(128)}, u32[]{:S(2)}) copy-start(f32[32]{0:T(128)} %param.15) | copy-start | bytes 388
  3.4 7.1 %copy-start.6 = (bf16[512,64]{0,1:T(8,128)(2,1)S(1)}, bf16[512,64]{0,1:T(8,128)(2,1)}, u32[]{:S(2)}) copy-start(bf16[512,64]{0,1:T(8,128)(2,1)} %param.14) | copy-start | bytes 196612
  3.4 7.1 %copy-start.9 = (f32[512,32]{0,1:T(8,128)S(1)}, f32[512,32]{0,1:T(8,128)}, u32[]{:S(2)}) copy-start(f32[512,32]{0,1:T(8,128)} %param.12) | copy-start | bytes 196612
  3.4 7.1 %copy-start.10 = (bf16[512,64]{0,1:T(8,128)(2,1)S(1)}, bf16[512,64]{0,1:T(8,128)(2,1)}, u32[]{:S(2)}) copy-start(bf16[512,64]{0,1:T(8,128)(2,1)} %param.13) | copy-start | bytes 196612
  3.4 24.3 %collective-permute-start.1 = (bf16[2,512,512]{2,1,0:T(8,128)(2,1)}, bf16[2,512,512]{2,1,0:T(8,128)(2,1)S(1)}, u32[]{:S(2)}, u32[]{:S(2)}) collective-permute-start(bf16[2,512,512]{2,1,0:T(8,128)(2,1)} %pad_maximum_fusion), channel_id=1, source_target_pairs={{0,4},{1,5},{2,6},{3,7},{4,8},{5,9},{6,10},{7,11},{8,12},{9,13},{1... | collective-permute-start | bytes 3145736 | tf_op jit(solution)/shard_map/ppermute | solution.py:33
  5.8 0.8 copy-start.11
  7.7 42.5 %collective-permute-start = (bf16[2,512,512]{2,1,0:T(8,128)(2,1)}, bf16[2,512,512]{2,1,0:T(8,128)(2,1)S(1)}, u32[]{:S(2)}, u32[]{:S(2)}) collective-permute-start(bf16[2,512,512]{2,1,0:T(8,128)(2,1)} %pad_maximum_fusion.1), channel_id=1, source_target_pairs={{0,4},{1,5},{2,6},{3,7},{4,8},{5,9},{6,10},{7,11},{8,12},{9,13},{1... | collective-permute-start | bytes 3145736 | tf_op jit(solution)/shard_map/ppermute | solution.py:33
  9.0 53.2 %collective-permute-start.7 = (bf16[512,2048]{1,0:T(8,128)(2,1)}, bf16[512,2048]{1,0:T(8,128)(2,1)}, u32[]{:S(2)}, u32[]{:S(2)}) collective-permute-start(bf16[512,2048]{1,0:T(8,128)(2,1)} %k.9), channel_id=1, source_target_pairs={{0,1},{1,0},{2,3},{3,2},{4,5},{5,4},{6,7},{7,6},{8,9},{9,8},{10,11... | collective-permute-start | bytes 6291464 | tf_op jit(solution)/shard_map/ppermute | solution.py:38
  10.3 52.3 %collective-permute-start.8 = (bf16[512,2048]{1,0:T(8,128)(2,1)}, bf16[512,2048]{1,0:T(8,128)(2,1)}, u32[]{:S(2)}, u32[]{:S(2)}) collective-permute-start(bf16[512,2048]{1,0:T(8,128)(2,1)} %v.9), channel_id=1, source_target_pairs={{0,1},{1,0},{2,3},{3,2},{4,5},{5,4},{6,7},{7,6},{8,9},{9,8},{10,11... | collective-permute-start | bytes 6291464 | tf_op jit(solution)/shard_map/ppermute | solution.py:38
  10.4 17.3 %copy-start.16 = (bf16[1,512,512]{2,1,0:T(8,128)(2,1)S(1)}, bf16[1,512,512]{2,1,0:T(8,128)(2,1)}, u32[]{:S(2)}) copy-start(bf16[1,512,512]{2,1,0:T(8,128)(2,1)} %copy-done.15) | copy-start | bytes 1572868
  10.4 17.3 %copy-start.18 = (bf16[1,512,512]{2,1,0:T(8,128)(2,1)S(1)}, bf16[1,512,512]{2,1,0:T(8,128)(2,1)}, u32[]{:S(2)}) copy-start(bf16[1,512,512]{2,1,0:T(8,128)(2,1)} %copy-done.17) | copy-start | bytes 1572868
  18.3 11.0 %copy-start = (f32[512,1024]{1,0:T(8,128)}, f32[512,1024]{1,0:T(8,128)S(1)}, u32[]{:S(2)}) copy-start(f32[512,1024]{1,0:T(8,128)S(1)} %get-tuple-element.41.part_a) | copy-start | bytes 6291460
  18.3 11.0 %copy-start.7 = (f32[512,32]{1,0:T(8,128)}, f32[512,32]{1,0:T(8,128)S(1)}, u32[]{:S(2)}) copy-start(f32[512,32]{1,0:T(8,128)S(1)} %get-tuple-element.55.cum) | copy-start | bytes 196612
  27.8 24.9 %collective-permute-start.4 = (bf16[2,512,512]{2,1,0:T(8,128)(2,1)S(1)}, bf16[2,512,512]{2,1,0:T(8,128)(2,1)}, u32[]{:S(2)}, u32[]{:S(2)}) collective-permute-start(bf16[2,512,512]{2,1,0:T(8,128)(2,1)S(1)} %broadcast_select_fusion.1), channel_id=1, source_target_pairs={{0,2},{1,3},{2,0},{3,1},{4,6},{5,7},{6,4},{7,5},{8,10},{9,11},{10,... | collective-permute-start | bytes 3145736 | tf_op jit(solution)/shard_map/ppermute | solution.py:38
  29.3 5.1 %copy-start.23 = (bf16[1,512,384]{2,1,0:T(8,128)(2,1)}, bf16[1,512,384]{2,1,0:T(8,128)(2,1)S(1)}, u32[]{:S(2)}) copy-start(bf16[1,512,384]{2,1,0:T(8,128)(2,1)S(1)} %get-tuple-element.72) | copy-start | bytes 1179652
  29.3 28.0 %copy-start.19 = (bf16[1,512,384]{2,1,0:T(8,128)(2,1)}, bf16[1,512,384]{2,1,0:T(8,128)(2,1)S(1)}, u32[]{:S(2)}) copy-start(bf16[1,512,384]{2,1,0:T(8,128)(2,1)S(1)} %get-tuple-element.73) | copy-start | bytes 1179652
  29.3 26.8 %collective-permute-start.5 = (bf16[2,512,512]{2,1,0:T(8,128)(2,1)S(1)}, bf16[2,512,512]{2,1,0:T(8,128)(2,1)S(1)}, u32[]{:S(2)}, u32[]{:S(2)}) collective-permute-start(bf16[2,512,512]{2,1,0:T(8,128)(2,1)S(1)} %collective-permute-done.1.z), channel_id=1, source_target_pairs={{0,1},{1,0},{2,3},{3,2},{4,5},{5,4},{6,7},{7,6},{8,9},{9,8},{10,11... | collective-permute-start | bytes 3145736 | tf_op jit(solution)/shard_map/ppermute | solution.py:38
  33.4 1.0 copy-start.25
  33.4 18.1 %copy-start.12 = (bf16[1,512,512]{2,1,0:T(8,128)(2,1)S(1)}, bf16[1,512,512]{2,1,0:T(8,128)(2,1)}, u32[]{:S(2)}) copy-start(bf16[1,512,512]{2,1,0:T(8,128)(2,1)} %copy-done.11) | copy-start | bytes 1572868
  33.4 18.1 %copy-start.14 = (bf16[1,512,512]{2,1,0:T(8,128)(2,1)S(1)}, bf16[1,512,512]{2,1,0:T(8,128)(2,1)}, u32[]{:S(2)}) copy-start(bf16[1,512,512]{2,1,0:T(8,128)(2,1)} %copy-done.13) | copy-start | bytes 1572868
  35.5 21.9 %copy-start.21 = (bf16[1,512,384]{2,1,0:T(8,128)(2,1)}, bf16[1,512,384]{2,1,0:T(8,128)(2,1)S(1)}, u32[]{:S(2)}) copy-start(bf16[1,512,384]{2,1,0:T(8,128)(2,1)S(1)} %slice_bitcast_fusion.5) | copy-start | bytes 1179652
  44.1 12.1 %copy-start.2 = (f32[512,1024]{1,0:T(8,128)}, f32[512,1024]{1,0:T(8,128)S(1)}, u32[]{:S(2)}) copy-start(f32[512,1024]{1,0:T(8,128)S(1)} %get-tuple-element.44.part_b) | copy-start | bytes 6291460
  50.2 24.9 %collective-permute-start.3 = (bf16[2,512,384]{2,1,0:T(8,128)(2,1)}, bf16[2,512,384]{2,1,0:T(8,128)(2,1)S(1)}, u32[]{:S(2)}, u32[]{:S(2)}) collective-permute-start(bf16[2,512,384]{2,1,0:T(8,128)(2,1)} %pad_maximum_fusion.2), channel_id=1, source_target_pairs={{0,4},{1,5},{2,6},{3,7},{4,8},{5,9},{6,10},{7,11},{8,12},{9,13},{1... | collective-permute-start | bytes 2359304 | tf_op jit(solution)/shard_map/ppermute | solution.py:33
  52.7 10.0 %collective-permute-start.6 = (bf16[2,512,512]{2,1,0:T(8,128)(2,1)}, bf16[2,512,512]{2,1,0:T(8,128)(2,1)}, u32[]{:S(2)}, u32[]{:S(2)}) collective-permute-start(bf16[2,512,512]{2,1,0:T(8,128)(2,1)} %collective-permute-done.4.d), channel_id=1, source_target_pairs={{0,1},{1,0},{2,3},{3,2},{4,5},{5,4},{6,7},{7,6},{8,9},{9,8},{10,11... | collective-permute-start | bytes 3145736 | tf_op jit(solution)/shard_map/ppermute | solution.py:38
  56.2 1.0 copy-start.4
  57.1 25.1 %collective-permute-start.11 = (bf16[2,512,512]{2,1,0:T(8,128)(2,1)}, bf16[2,512,512]{2,1,0:T(8,128)(2,1)}, u32[]{:S(2)}, u32[]{:S(2)}) collective-permute-start(bf16[2,512,512]{2,1,0:T(8,128)(2,1)} %broadcast_select_fusion), channel_id=1, source_target_pairs={{0,2},{1,3},{2,0},{3,1},{4,6},{5,7},{6,4},{7,5},{8,10},{9,11},{10,... | collective-permute-start | bytes 3145736 | tf_op jit(solution)/shard_map/ppermute | solution.py:38
  59.4 3.1 %copy-start.28 = (bf16[1,512,256]{2,1,0:T(8,128)(2,1)}, bf16[1,512,256]{2,1,0:T(8,128)(2,1)S(1)}, u32[]{:S(2)}) copy-start(bf16[1,512,256]{2,1,0:T(8,128)(2,1)S(1)} %slice_bitcast_fusion.9) | copy-start | bytes 786436
  62.2 20.3 %collective-permute-start.19 = (f32[72,1024]{1,0:T(8,128)}, f32[72,1024]{1,0:T(8,128)S(1)}, u32[]{:S(2)}, u32[]{:S(2)}) collective-permute-start(f32[72,1024]{1,0:T(8,128)} %get-tuple-element.78), channel_id=1, source_target_pairs={{0,1},{1,0},{2,3},{3,2},{4,5},{5,4},{6,7},{7,6},{8,9},{9,8},{10,11... | collective-permute-start | bytes 884744 | tf_op jit(solution)/shard_map/ppermute | solution.py:38
  62.5 21.2 %collective-permute-start.12 = (bf16[2,512,512]{2,1,0:T(8,128)(2,1)S(1)}, bf16[2,512,512]{2,1,0:T(8,128)(2,1)S(1)}, u32[]{:S(2)}, u32[]{:S(2)}) collective-permute-start(bf16[2,512,512]{2,1,0:T(8,128)(2,1)S(1)} %collective-permute-done.z), channel_id=1, source_target_pairs={{0,1},{1,0},{2,3},{3,2},{4,5},{5,4},{6,7},{7,6},{8,9},{9,8},{10,11... | collective-permute-start | bytes 3145736 | tf_op jit(solution)/shard_map/ppermute | solution.py:38
  62.8 34.4 %collective-permute-start.10 = (bf16[2,512,384]{2,1,0:T(8,128)(2,1)}, bf16[2,512,384]{2,1,0:T(8,128)(2,1)S(1)}, u32[]{:S(2)}, u32[]{:S(2)}) collective-permute-start(bf16[2,512,384]{2,1,0:T(8,128)(2,1)} %pad_maximum_fusion.3), channel_id=1, source_target_pairs={{0,4},{1,5},{2,6},{3,7},{4,8},{5,9},{6,10},{7,11},{8,12},{9,13},{1... | collective-permute-start | bytes 2359304 | tf_op jit(solution)/shard_map/ppermute | solution.py:33
  64.1 1.2 copy-start.5
  65.3 9.8 %copy-start.31 = (bf16[2,512,256]{2,1,0:T(8,128)(2,1)S(1)}, bf16[2,512,256]{2,1,0:T(8,128)(2,1)}, u32[]{:S(2)}) copy-start(bf16[2,512,256]{2,1,0:T(8,128)(2,1)} %pad_maximum_fusion.4) | copy-start | bytes 1572868
  65.3 11.9 %copy-start.24 = (bf16[1,512,384]{2,1,0:T(8,128)(2,1)S(1)}, bf16[1,512,384]{2,1,0:T(8,128)(2,1)}, u32[]{:S(2)}) copy-start(bf16[1,512,384]{2,1,0:T(8,128)(2,1)} %copy-done.23) | copy-start | bytes 1179652
  65.3 11.9 %copy-start.26 = (bf16[1,512,384]{2,1,0:T(8,128)(2,1)S(1)}, bf16[1,512,384]{2,1,0:T(8,128)(2,1)}, u32[]{:S(2)}) copy-start(bf16[1,512,384]{2,1,0:T(8,128)(2,1)} %copy-done.25) | copy-start | bytes 1179652
  75.1 8.4 %copy-start.30 = (f32[72,1024]{1,0:T(8,128)S(1)}, f32[72,1024]{1,0:T(8,128)}, u32[]{:S(2)}) copy-start(f32[72,1024]{1,0:T(8,128)} %get-tuple-element.59) | copy-start | bytes 884740
  75.1 41.8 %collective-permute-start.2 = (bf16[2,512,256]{2,1,0:T(8,128)(2,1)S(1)}, bf16[2,512,256]{2,1,0:T(8,128)(2,1)S(1)}, u32[]{:S(2)}, u32[]{:S(2)}) collective-permute-start(bf16[2,512,256]{2,1,0:T(8,128)(2,1)S(1)} %copy-done.31), channel_id=1, source_target_pairs={{0,4},{1,5},{2,6},{3,7},{4,8},{5,9},{6,10},{7,11},{8,12},{9,13},{1... | collective-permute-start | bytes 1572872 | tf_op jit(solution)/shard_map/ppermute | solution.py:33
  82.3 18.3 %collective-permute-start.9 = (bf16[2,512,384]{2,1,0:T(8,128)(2,1)S(1)}, bf16[2,512,384]{2,1,0:T(8,128)(2,1)S(1)}, u32[]{:S(2)}, u32[]{:S(2)}) collective-permute-start(bf16[2,512,384]{2,1,0:T(8,128)(2,1)S(1)} %broadcast_select_fusion.3), channel_id=1, source_target_pairs={{0,2},{1,3},{2,0},{3,1},{4,6},{5,7},{6,4},{7,5},{8,10},{9,11},{10,... | collective-permute-start | bytes 2359304 | tf_op jit(solution)/shard_map/ppermute | solution.py:38
  82.5 3.6 %collective-permute-start.13 = (bf16[2,512,512]{2,1,0:T(8,128)(2,1)}, bf16[2,512,512]{2,1,0:T(8,128)(2,1)S(1)}, u32[]{:S(2)}, u32[]{:S(2)}) collective-permute-start(bf16[2,512,512]{2,1,0:T(8,128)(2,1)} %collective-permute-done.11.d), channel_id=1, source_target_pairs={{0,1},{1,0},{2,3},{3,2},{4,5},{5,4},{6,7},{7,6},{8,9},{9,8},{10,11... | collective-permute-start | bytes 3145736 | tf_op jit(solution)/shard_map/ppermute | solution.py:38
  83.7 21.3 %collective-permute-start.14 = (bf16[2,512,384]{2,1,0:T(8,128)(2,1)S(1)}, bf16[2,512,384]{2,1,0:T(8,128)(2,1)S(1)}, u32[]{:S(2)}, u32[]{:S(2)}) collective-permute-start(bf16[2,512,384]{2,1,0:T(8,128)(2,1)S(1)} %collective-permute-done.3.z), channel_id=1, source_target_pairs={{0,1},{1,0},{2,3},{3,2},{4,5},{5,4},{6,7},{7,6},{8,9},{9,8},{10,11... | collective-permute-start | bytes 2359304 | tf_op jit(solution)/shard_map/ppermute | solution.py:38
  86.0 11.1 %copy-start.20 = (bf16[1,512,384]{2,1,0:T(8,128)(2,1)S(1)}, bf16[1,512,384]{2,1,0:T(8,128)(2,1)}, u32[]{:S(2)}) copy-start(bf16[1,512,384]{2,1,0:T(8,128)(2,1)} %copy-done.19) | copy-start | bytes 1179652
  86.1 11.1 %copy-start.22 = (bf16[1,512,384]{2,1,0:T(8,128)(2,1)S(1)}, bf16[1,512,384]{2,1,0:T(8,128)(2,1)}, u32[]{:S(2)}) copy-start(bf16[1,512,384]{2,1,0:T(8,128)(2,1)} %copy-done.21) | copy-start | bytes 1179652
  86.1 17.6 %collective-permute-start.20 = (f32[72,512]{1,0:T(8,128)S(1)}, f32[72,512]{1,0:T(8,128)S(1)}, u32[]{:S(2)}, u32[]{:S(2)}) collective-permute-start(f32[72,512]{1,0:T(8,128)S(1)} %get-tuple-element.85), channel_id=1, source_target_pairs={{0,2},{1,3},{2,0},{3,1},{4,6},{5,7},{6,4},{7,5},{8,10},{9,11},{10,... | collective-permute-start | bytes 442376 | tf_op jit(solution)/shard_map/ppermute | solution.py:38
  97.3 23.6 %collective-permute-start.24 = (bf16[2,512,384]{2,1,0:T(8,128)(2,1)S(1)}, bf16[2,512,384]{2,1,0:T(8,128)(2,1)S(1)}, u32[]{:S(2)}, u32[]{:S(2)}) collective-permute-start(bf16[2,512,384]{2,1,0:T(8,128)(2,1)S(1)} %broadcast_select_fusion.2), channel_id=1, source_target_pairs={{0,2},{1,3},{2,0},{3,1},{4,6},{5,7},{6,4},{7,5},{8,10},{9,11},{10,... | collective-permute-start | bytes 2359304 | tf_op jit(solution)/shard_map/ppermute | solution.py:38
  100.5 6.2 %collective-permute-start.15 = (bf16[2,512,384]{2,1,0:T(8,128)(2,1)S(1)}, bf16[2,512,384]{2,1,0:T(8,128)(2,1)S(1)}, u32[]{:S(2)}, u32[]{:S(2)}) collective-permute-start(bf16[2,512,384]{2,1,0:T(8,128)(2,1)S(1)} %collective-permute-done.9.d), channel_id=1, source_target_pairs={{0,1},{1,0},{2,3},{3,2},{4,5},{5,4},{6,7},{7,6},{8,9},{9,8},{10,11... | collective-permute-start | bytes 2359304 | tf_op jit(solution)/shard_map/ppermute | solution.py:38
  103.8 17.0 %collective-permute-start.21 = (f32[72,512]{1,0:T(8,128)S(1)}, f32[72,512]{1,0:T(8,128)S(1)}, u32[]{:S(2)}, u32[]{:S(2)}) collective-permute-start(f32[72,512]{1,0:T(8,128)S(1)} %pad_maximum_fusion.8), channel_id=1, source_target_pairs={{0,12},{1,13},{2,14},{3,15},{4,0},{5,1},{6,2},{7,3},{8,4},{9,5},{1... | collective-permute-start | bytes 442376 | tf_op jit(solution)/shard_map/ppermute | solution.py:33
  105.1 15.7 %collective-permute-start.22 = (f32[72,512]{1,0:T(8,128)S(1)}, f32[72,512]{1,0:T(8,128)S(1)}, u32[]{:S(2)}, u32[]{:S(2)}) collective-permute-start(f32[72,512]{1,0:T(8,128)S(1)} %pad_maximum_fusion.8), channel_id=1, source_target_pairs={{0,8},{1,9},{2,10},{3,11},{4,12},{5,13},{6,14},{7,15},{8,0},{9,1},... | collective-permute-start | bytes 442376 | tf_op jit(solution)/shard_map/ppermute | solution.py:33
  106.8 14.0 %collective-permute-start.23 = (f32[72,512]{1,0:T(8,128)S(1)}, f32[72,512]{1,0:T(8,128)S(1)}, u32[]{:S(2)}, u32[]{:S(2)}) collective-permute-start(f32[72,512]{1,0:T(8,128)S(1)} %pad_maximum_fusion.8), channel_id=1, source_target_pairs={{0,4},{1,5},{2,6},{3,7},{4,8},{5,9},{6,10},{7,11},{8,12},{9,13},{1... | collective-permute-start | bytes 442376 | tf_op jit(solution)/shard_map/ppermute | solution.py:33
  109.1 11.7 %copy-start.27 = (bf16[1,512,256]{2,1,0:T(8,128)(2,1)S(1)}, bf16[1,512,256]{2,1,0:T(8,128)(2,1)}, u32[]{:S(2)}) copy-start(bf16[1,512,256]{2,1,0:T(8,128)(2,1)} %slice_bitcast_fusion.8) | copy-start | bytes 786436
  109.1 11.8 %copy-start.29 = (bf16[1,512,256]{2,1,0:T(8,128)(2,1)S(1)}, bf16[1,512,256]{2,1,0:T(8,128)(2,1)}, u32[]{:S(2)}) copy-start(bf16[1,512,256]{2,1,0:T(8,128)(2,1)} %copy-done.28) | copy-start | bytes 786436
  117.0 7.1 %collective-permute-start.25 = (bf16[2,512,384]{2,1,0:T(8,128)(2,1)S(1)}, bf16[2,512,384]{2,1,0:T(8,128)(2,1)S(1)}, u32[]{:S(2)}, u32[]{:S(2)}) collective-permute-start(bf16[2,512,384]{2,1,0:T(8,128)(2,1)S(1)} %collective-permute-done.10.z), channel_id=1, source_target_pairs={{0,1},{1,0},{2,3},{3,2},{4,5},{5,4},{6,7},{7,6},{8,9},{9,8},{10,11... | collective-permute-start | bytes 2359304 | tf_op jit(solution)/shard_map/ppermute | solution.py:38
  120.9 3.2 %collective-permute-start.26 = (bf16[2,512,384]{2,1,0:T(8,128)(2,1)S(1)}, bf16[2,512,384]{2,1,0:T(8,128)(2,1)S(1)}, u32[]{:S(2)}, u32[]{:S(2)}) collective-permute-start(bf16[2,512,384]{2,1,0:T(8,128)(2,1)S(1)} %collective-permute-done.24.d), channel_id=1, source_target_pairs={{0,1},{1,0},{2,3},{3,2},{4,5},{5,4},{6,7},{7,6},{8,9},{9,8},{10,11... | collective-permute-start | bytes 2359304 | tf_op jit(solution)/shard_map/ppermute | solution.py:38
  122.5 9.6 %collective-permute-start.27 = (f32[64,512]{1,0:T(8,128)S(1)}, f32[64,512]{1,0:T(8,128)S(1)}, u32[]{:S(2)}, u32[]{:S(2)}) collective-permute-start(f32[64,512]{1,0:T(8,128)S(1)} %get-tuple-element.81), channel_id=1, source_target_pairs={{0,2},{1,3},{2,0},{3,1},{4,6},{5,7},{6,4},{7,5},{8,10},{9,11},{10,... | collective-permute-start | bytes 393224 | tf_op jit(solution)/shard_map/ppermute | solution.py:38
  122.8 16.1 %collective-permute-start.16 = (bf16[2,512,256]{2,1,0:T(8,128)(2,1)S(1)}, bf16[2,512,256]{2,1,0:T(8,128)(2,1)S(1)}, u32[]{:S(2)}, u32[]{:S(2)}) collective-permute-start(bf16[2,512,256]{2,1,0:T(8,128)(2,1)S(1)} %broadcast_select_fusion.4), channel_id=1, source_target_pairs={{0,2},{1,3},{2,0},{3,1},{4,6},{5,7},{6,4},{7,5},{8,10},{9,11},{10,... | collective-permute-start | bytes 1572872 | tf_op jit(solution)/shard_map/ppermute | solution.py:38
  124.1 15.7 %copy-start.3 = (f32[512,1024]{1,0:T(8,128)S(1)}, f32[512,1024]{1,0:T(8,128)}, u32[]{:S(2)}) copy-start(f32[512,1024]{1,0:T(8,128)} %copy-done.2) | copy-start | bytes 6291460
  132.1 7.8 %copy-start.1 = (f32[512,1024]{1,0:T(8,128)S(1)}, f32[512,1024]{1,0:T(8,128)}, u32[]{:S(2)}) copy-start(f32[512,1024]{1,0:T(8,128)} %copy-done) | copy-start | bytes 6291460
  132.1 7.8 %copy-start.8 = (f32[512,32]{1,0:T(8,128)S(1)}, f32[512,32]{1,0:T(8,128)}, u32[]{:S(2)}) copy-start(f32[512,32]{1,0:T(8,128)} %copy-done.7) | copy-start | bytes 196612
  132.2 7.5 %collective-permute-start.28 = (f32[64,1024]{1,0:T(8,128)S(1)}, f32[64,1024]{1,0:T(8,128)S(1)}, u32[]{:S(2)}, u32[]{:S(2)}) collective-permute-start(f32[64,1024]{1,0:T(8,128)S(1)} %fusion), channel_id=1, source_target_pairs={{0,1},{1,0},{2,3},{3,2},{4,5},{5,4},{6,7},{7,6},{8,9},{9,8},{10,11... | collective-permute-start | bytes 786440 | tf_op jit(solution)/shard_map/ppermute | solution.py:38
  138.9 4.5 %collective-permute-start.18 = (bf16[2,512,256]{2,1,0:T(8,128)(2,1)S(1)}, bf16[2,512,256]{2,1,0:T(8,128)(2,1)S(1)}, u32[]{:S(2)}, u32[]{:S(2)}) collective-permute-start(bf16[2,512,256]{2,1,0:T(8,128)(2,1)S(1)} %collective-permute-done.16.d), channel_id=1, source_target_pairs={{0,1},{1,0},{2,3},{3,2},{4,5},{5,4},{6,7},{7,6},{8,9},{9,8},{10,11... | collective-permute-start | bytes 1572872 | tf_op jit(solution)/shard_map/ppermute | solution.py:38
  139.7 3.7 %collective-permute-start.17 = (bf16[2,512,256]{2,1,0:T(8,128)(2,1)S(1)}, bf16[2,512,256]{2,1,0:T(8,128)(2,1)S(1)}, u32[]{:S(2)}, u32[]{:S(2)}) collective-permute-start(bf16[2,512,256]{2,1,0:T(8,128)(2,1)S(1)} %collective-permute-done.2.z), channel_id=1, source_target_pairs={{0,1},{1,0},{2,3},{3,2},{4,5},{5,4},{6,7},{7,6},{8,9},{9,8},{10,11... | collective-permute-start | bytes 1572872 | tf_op jit(solution)/shard_map/ppermute | solution.py:38
